TPU v7x, 32 devices: a whole 2x2x4 slice. The times are simulated.
32 devices in a mesh: fsdp: 2 (over x), ctx: 16 (over z, y, core).
Axes of the slice: x: 2, y: 2, z: 4, core: 2. Of those that a mesh axis runs over, the one named last changes fastest.
Arguments:
- inputs: bfloat16 [2, 2048, 960], P('fsdp', 'ctx'), may hold values from -6 to 6
- grad_output: bfloat16 [2, 2048, 960], P('fsdp', 'ctx'), may hold values from -6 to 6
- w_query: bfloat16 [960, 960], P('fsdp', 'ctx'), may hold values from -50 to 50
- w_key: bfloat16 [960, 320], P('fsdp', 'ctx'), may hold values from -50 to 50
- w_value: bfloat16 [960, 320], P('fsdp', 'ctx'), may hold values from -0.1875 to 0.1875
- w_out: bfloat16 [960, 960], P('fsdp', 'ctx'), may hold values from -0.75 to 0.75
- w_gate: bfloat16 [960, 2560], P('fsdp', 'ctx'), may hold values from -0.1875 to 0.1875
- w_up: bfloat16 [960, 2560], P('fsdp', 'ctx'), may hold values from -0.1875 to 0.1875
- w_down: bfloat16 [2560, 960], P('fsdp', 'ctx'), may hold values from -0.125 to 0.125
- gain_attn: bfloat16 [960], P('ctx'), may hold values from 0.5 to 1.5
- gain_mlp: bfloat16 [960], P('ctx'), may hold values from 0.5 to 1.5
Outputs:
- output: bfloat16 [2, 2048, 960], P('fsdp', 'ctx')
- grad_input: bfloat16 [2, 2048, 960], P('fsdp', 'ctx')
- grad_w_query: float32 [960, 960], P('fsdp', 'ctx')
- grad_w_key: float32 [960, 320], P('fsdp', 'ctx')
- grad_w_value: float32 [960, 320], P('fsdp', 'ctx')
- grad_w_out: float32 [960, 960], P('fsdp', 'ctx')
- grad_w_gate: float32 [960, 2560], P('fsdp', 'ctx')
- grad_w_up: float32 [960, 2560], P('fsdp', 'ctx')
- grad_w_down: float32 [2560, 960], P('fsdp', 'ctx')
- grad_gain_attn: float32 [960], P('ctx')
- grad_gain_mlp: float32 [960], P('ctx')
All inputs are finite; a program needn't handle non-finite values.
Results may differ from a plain program's by a relative error of at most 0.018.
Values may be sent and summed in bfloat16 or wider, within the bound.
A program may use at most 256 MiB of HBM per device.

v0:
```python
import jax
import jax.numpy as jnp
from jax import lax
from jax.sharding import PartitionSpec as P

HEADS = 15
KV_HEADS = 5
HEAD = 64


EPSILON = 1e-05
ROPE_THETA = 100000.0


def tables(positions, head_size):
    half_size = head_size // 2
    frequency = ROPE_THETA ** (-jnp.arange(half_size, dtype=jnp.float32) * 2.0 / head_size)
    angles = positions.astype(jnp.float32)[:, None] * frequency[None, :]
    return (jnp.cos(angles), jnp.sin(angles))


def rotate(values, cosine, sine_table):
    half_size = values.shape[-1] // 2
    first_half = values[..., :half_size]
    second = values[..., half_size:]
    cosine = cosine[:, None, :]
    sine_table = sine_table[:, None, :]
    return jnp.concatenate(
        [first_half * cosine - second * sine_table, second * cosine + first_half * sine_table],
        axis=-1,
    )


def unrotate(values, cosine, sine_table):
    half_size = values.shape[-1] // 2
    first_half = values[..., :half_size]
    second = values[..., half_size:]
    cosine = cosine[:, None, :]
    sine_table = sine_table[:, None, :]
    return jnp.concatenate(
        [first_half * cosine + second * sine_table, second * cosine - first_half * sine_table],
        axis=-1,
    )


def normed(row_values, gain_vec):
    scale_rows = lax.rsqrt(jnp.mean(row_values * row_values, axis=-1, keepdims=True) + EPSILON)
    return row_values * scale_rows * gain_vec


BOTH = ("fsdp", "ctx")


def forward_dot(pieces, halves):
    total = None
    for piece, half in zip(pieces, halves):
        term = lax.dot_general(
            piece, half, (((1,), (1,)), ((), ())), preferred_element_type=jnp.float32
        )
        total = term if total is None else total + term
    return total


def backward_dot(grads, halves):
    return jnp.concatenate(
        [jnp.dot(grads, half, preferred_element_type=jnp.float32) for half in halves], axis=-1
    )


def weight_terms(grads, pieces, cycle_size):
    terms = [
        lax.dot_general(
            grads, piece, (((0,), (0,)), ((), ())), preferred_element_type=jnp.float32
        ).astype(jnp.bfloat16)
        for piece in pieces
    ]
    return jnp.stack(
        [term.reshape(cycle_size, term.shape[0] // cycle_size, term.shape[1]) for term in terms]
    )


def cut(rows, count):
    return jnp.split(rows, count, axis=-1)


def gather_rows(packed, split_count, cycle_size):
    gathered = lax.all_gather(packed, BOTH, axis=0, tiled=False)
    return gathered.reshape(split_count, cycle_size, *packed.shape)


def take(gathered, start, size):
    piece = lax.slice_in_dim(gathered, start, start + size, axis=2)
    return [part.reshape(-1, part.shape[-1]) for part in piece]


def scatter_rows(terms):
    merged = terms.reshape(-1, *terms.shape[2:])
    return lax.psum_scatter(merged, BOTH, scatter_dimension=0, tiled=True)[0].astype(jnp.float32)


def local(
    inputs, grad_output, w_query, w_key, w_value, w_out, w_gate, w_up, w_down, gain_attn, gain_mlp
):
    seq_count, block_len, model_width = inputs.shape
    row_count = seq_count * block_len
    split_count = lax.axis_size("fsdp")
    cycle_size = lax.axis_size("ctx")
    cycle_index = lax.axis_index("ctx")
    length = block_len * cycle_size
    key_block = min(512, length)
    groups = KV_HEADS
    head_size = HEAD
    repeat_count = HEADS // KV_HEADS
    kv_width = groups * head_size
    positions = cycle_index * block_len + jnp.arange(block_len, dtype=jnp.int32)
    cosine, sine_table = tables(positions, head_size)
    cosine = jnp.tile(cosine, (seq_count, 1))
    sine_table = jnp.tile(sine_table, (seq_count, 1))
    needed = (cycle_index * block_len + block_len + key_block - 1) // key_block
    wide_q, wide_k, wide_v = w_query.shape[1], w_key.shape[1], w_value.shape[1]
    wide_o, wide_g, wide_u = w_out.shape[1], w_gate.shape[1], w_up.shape[1]
    part_width = w_query.shape[0]
    gain_size = gain_attn.shape[0]
    gain_row = jnp.pad(
        jnp.concatenate([gain_attn, gain_mlp]), (0, part_width - 2 * gain_size)
    )[None, :]
    packed_first = jnp.concatenate([w_query.T, w_key.T, w_value.T, gain_row], axis=0)
    packed_rest = jnp.concatenate([w_out.T, w_gate.T, w_up.T], axis=0)
    first = gather_rows(packed_first, split_count, cycle_size)
    rest = gather_rows(packed_rest, split_count, cycle_size)
    down = gather_rows(w_down.T, split_count, cycle_size)
    full_query = take(first, 0, wide_q)
    full_key = take(first, wide_q, wide_k)
    full_value = take(first, wide_q + wide_k, wide_v)
    gain_rows = first[0, :, wide_q + wide_k + wide_v, :]
    gain_first = gain_rows[:, :gain_size].reshape(-1).astype(jnp.float32)
    gain_second = gain_rows[:, gain_size : 2 * gain_size].reshape(-1).astype(jnp.float32)
    full_out = take(rest, 0, wide_o)
    full_gate = take(rest, wide_o, wide_g)
    full_up = take(rest, wide_o + wide_g, wide_u)
    full_down = take(down, 0, w_down.shape[1])

    resid1 = inputs.reshape(row_count, model_width).astype(jnp.float32)
    normal1 = normed(resid1, gain_first).astype(jnp.bfloat16)
    normal1_parts = cut(normal1, split_count)
    query_raw = forward_dot(normal1_parts, full_query).reshape(row_count, HEADS, head_size)
    query_rot = rotate(query_raw, cosine, sine_table).astype(jnp.bfloat16)
    key_raw = forward_dot(normal1_parts, full_key).reshape(row_count, groups, head_size)
    key_rows = (
        rotate(key_raw, cosine, sine_table)
        .astype(jnp.bfloat16)
        .reshape(seq_count, block_len, kv_width)
    )
    value_rows = (
        forward_dot(normal1_parts, full_value)
        .astype(jnp.bfloat16)
        .reshape(seq_count, block_len, kv_width)
    )
    query_grouped = query_rot.reshape(seq_count, block_len, groups, repeat_count, head_size)
    pair_all = lax.all_gather(
        jnp.concatenate([key_rows, value_rows], axis=-1), "ctx", axis=1, tiled=True
    )
    keys_all = pair_all[..., :kv_width]
    values_all = pair_all[..., kv_width:]
    key_heads = keys_all.reshape(seq_count, length, groups, head_size)
    value_heads = values_all.reshape(seq_count, length, groups, head_size)
    scores = (
        jnp.einsum(
            "sqgrd,skgd->sgrqk", query_grouped, key_heads, preferred_element_type=jnp.float32
        )
        * 0.125
    )
    allowed = jnp.arange(length, dtype=jnp.int32)[None, :] <= positions[:, None]
    scores = jnp.where(allowed, scores, -jnp.inf)
    new_peak = jnp.max(scores, axis=-1)
    exp_terms = jnp.exp(scores - new_peak[..., None])
    denom_run = jnp.sum(exp_terms, axis=-1)
    running = jnp.einsum(
        "sgrqk,skgd->sgrqd",
        exp_terms.astype(jnp.bfloat16),
        value_heads,
        preferred_element_type=jnp.float32,
    )
    attended_wide = running / denom_run[..., None]
    attended = jnp.transpose(attended_wide, (0, 3, 1, 2, 4)).astype(jnp.bfloat16)
    logsum = new_peak + jnp.log(denom_run)
    attended_rows = attended.reshape(row_count, HEADS * head_size)
    attended_parts = cut(attended_rows, split_count)
    resid2 = resid1 + forward_dot(attended_parts, full_out)
    normal2 = normed(resid2, gain_second).astype(jnp.bfloat16)
    normal2_parts = cut(normal2, split_count)
    gate_act = forward_dot(normal2_parts, full_gate)
    up_act = forward_dot(normal2_parts, full_up)
    gate_sigma = jax.nn.sigmoid(gate_act)
    hidden = (gate_act * gate_sigma * up_act).astype(jnp.bfloat16)
    hidden_parts = cut(hidden, split_count)
    output = (resid2 + forward_dot(hidden_parts, full_down)).astype(jnp.bfloat16)

    grad_rows = grad_output.reshape(row_count, model_width)
    sum_down = scatter_rows(weight_terms(grad_rows, hidden_parts, cycle_size))
    grad_hidden = backward_dot(grad_rows, full_down)
    grad_up = (grad_hidden * gate_act * gate_sigma).astype(jnp.bfloat16)
    grad_gate = (grad_hidden * up_act * gate_sigma * (1.0 + gate_act * (1.0 - gate_sigma))).astype(
        jnp.bfloat16
    )
    grad_norm2 = backward_dot(grad_gate, full_gate) + backward_dot(grad_up, full_up)
    normed_out, pull_second = jax.vjp(normed, resid2, gain_second)
    grad_part2, term_gain2 = pull_second(grad_norm2)
    grad_resid2 = grad_rows.astype(jnp.float32) + grad_part2
    grad_branch = grad_resid2.astype(jnp.bfloat16)
    sum_rest = scatter_rows(
        jnp.concatenate(
            [
                weight_terms(grad_branch, attended_parts, cycle_size),
                weight_terms(grad_gate, normal2_parts, cycle_size),
                weight_terms(grad_up, normal2_parts, cycle_size),
            ],
            axis=2,
        )
    )
    grad_attended = backward_dot(grad_branch, full_out).astype(jnp.bfloat16)
    grad_grouped = grad_attended.reshape(seq_count, block_len, groups, repeat_count, head_size)
    row_delta = jnp.sum(
        jnp.transpose(grad_grouped, (0, 2, 3, 1, 4)).astype(jnp.float32) * attended_wide, axis=-1
    )

    def retrace(step_index, loop_state):
        grad_query_acc, grad_pair_all = loop_state
        key_start = step_index * key_block
        pair = lax.dynamic_slice_in_dim(pair_all, key_start, key_block, 1)
        key_heads = pair[..., :kv_width].reshape(seq_count, key_block, groups, head_size)
        value_heads = pair[..., kv_width:].reshape(seq_count, key_block, groups, head_size)
        scores = (
            jnp.einsum(
                "sqgrd,skgd->sgrqk", query_grouped, key_heads, preferred_element_type=jnp.float32
            )
            * 0.125
        )
        allowed = (key_start + jnp.arange(key_block, dtype=jnp.int32))[None, :] <= positions[
            :, None
        ]
        prob_full = jnp.where(allowed, jnp.exp(jnp.where(allowed, scores, -jnp.inf) - logsum[..., None]), 0.0)
        grad_probs = jnp.einsum(
            "sqgrd,skgd->sgrqk", grad_grouped, value_heads, preferred_element_type=jnp.float32
        )
        grad_scores = (prob_full * (grad_probs - row_delta[..., None]) * 0.125).astype(jnp.bfloat16)
        prob_low = prob_full.astype(jnp.bfloat16)
        value_term = jnp.einsum(
            "sgrqk,sqgrd->skgd", prob_low, grad_grouped, preferred_element_type=jnp.float32
        ).reshape(seq_count, key_block, kv_width)
        key_term = jnp.einsum(
            "sgrqk,sqgrd->skgd", grad_scores, query_grouped, preferred_element_type=jnp.float32
        ).reshape(seq_count, key_block, kv_width)
        grad_query_acc = grad_query_acc + jnp.einsum(
            "sgrqk,skgd->sgrqd", grad_scores, key_heads, preferred_element_type=jnp.float32
        )
        pair_term = jnp.concatenate([key_term, value_term], axis=-1).astype(jnp.bfloat16)
        grad_pair_all = lax.dynamic_update_slice_in_dim(grad_pair_all, pair_term, key_start, 1)
        return (grad_query_acc, grad_pair_all)

    back_state = (
        jnp.zeros((seq_count, groups, repeat_count, block_len, head_size), jnp.float32),
        jnp.zeros((seq_count, length, 2 * kv_width), jnp.bfloat16),
    )
    grad_query_acc, grad_pair_all = lax.fori_loop(0, needed, retrace, back_state)
    grad_pair_own = lax.psum_scatter(
        grad_pair_all, "ctx", scatter_dimension=1, tiled=True
    ).astype(jnp.float32)
    grad_query_rows = jnp.transpose(grad_query_acc, (0, 3, 1, 2, 4)).reshape(
        row_count, HEADS, head_size
    )
    grad_query = (
        unrotate(grad_query_rows, cosine, sine_table)
        .reshape(row_count, HEADS * head_size)
        .astype(jnp.bfloat16)
    )
    grad_keys = (
        unrotate(
            grad_pair_own[..., :kv_width].reshape(row_count, groups, head_size), cosine, sine_table
        )
        .reshape(row_count, kv_width)
        .astype(jnp.bfloat16)
    )
    grad_values = grad_pair_own[..., kv_width:].reshape(row_count, kv_width).astype(jnp.bfloat16)
    grad_norm1 = backward_dot(grad_query, full_query)
    grad_norm1 = grad_norm1 + backward_dot(grad_keys, full_key)
    grad_norm1 = grad_norm1 + backward_dot(grad_values, full_value)
    normed_first, pull_first = jax.vjp(normed, resid1, gain_first)
    grad_part1, term_gain1 = pull_first(grad_norm1)
    grad_input = (
        (grad_resid2 + grad_part1).astype(jnp.bfloat16).reshape(seq_count, block_len, model_width)
    )
    gain_terms = jnp.concatenate(
        [term_gain1.reshape(cycle_size, -1), term_gain2.reshape(cycle_size, -1)], axis=-1
    ).astype(jnp.bfloat16)
    gain_terms = jnp.pad(gain_terms, ((0, 0), (0, part_width - 2 * gain_size)))
    gain_terms = jnp.broadcast_to(
        gain_terms[None, :, None, :], (split_count, cycle_size, 1, part_width)
    )
    sum_first = scatter_rows(
        jnp.concatenate(
            [
                weight_terms(grad_query, normal1_parts, cycle_size),
                weight_terms(grad_keys, normal1_parts, cycle_size),
                weight_terms(grad_values, normal1_parts, cycle_size),
                gain_terms,
            ],
            axis=2,
        )
    )
    gain_sums = sum_first[wide_q + wide_k + wide_v]
    return (
        output.reshape(seq_count, block_len, model_width),
        grad_input,
        sum_first[:wide_q].T,
        sum_first[wide_q : wide_q + wide_k].T,
        sum_first[wide_q + wide_k : wide_q + wide_k + wide_v].T,
        sum_rest[:wide_o].T,
        sum_rest[wide_o : wide_o + wide_g].T,
        sum_rest[wide_o + wide_g : wide_o + wide_g + wide_u].T,
        sum_down.T,
        gain_sums[:gain_size],
        gain_sums[gain_size : 2 * gain_size],
    )


def solution(mesh):
    return jax.shard_map(
        local,
        mesh=mesh,
        in_specs=(
            P("fsdp", "ctx", None),
            P("fsdp", "ctx", None),
            P("fsdp", "ctx"),
            P("fsdp", "ctx"),
            P("fsdp", "ctx"),
            P("fsdp", "ctx"),
            P("fsdp", "ctx"),
            P("fsdp", "ctx"),
            P("fsdp", "ctx"),
            P("ctx"),
            P("ctx"),
        ),
        out_specs=(
            P("fsdp", "ctx", None),
            P("fsdp", "ctx", None),
            P("fsdp", "ctx"),
            P("fsdp", "ctx"),
            P("fsdp", "ctx"),
            P("fsdp", "ctx"),
            P("fsdp", "ctx"),
            P("fsdp", "ctx"),
            P("fsdp", "ctx"),
            P("ctx"),
            P("ctx"),
        ),
        check_vma=False,
    )
```

profile of v0, /device:TPU:0, one launch (start us, length us, event | category | flops | bytes accessed | tf_op | source)
XLA Modules:
  0.0 909.7 jit_solution(12347333619238508726)
XLA Ops:
  13.3 60.9 %all-gather.13.cloned.1.call-done = bf16[32,101,480]{2,1,0:T(8,128)(2,1)} async-done(((bf16[1,101,480]{2,1,0:T(8,128)(2,1)}), bf16[32,101,480]{2,1,0:T(8,128)(2,1)}) %all-gather.13.cloned.1.call-update) | async-done | bytes 3102736 | tf_op jit(solution)/shard_map/all_gather | solution.py:87
  74.2 3.1 copy.94
  80.6 1.8 reshape_unstack.42
  82.4 1.9 copy.96
  84.4 1.9 reshape_unstack.43
  86.2 1.9 copy.97
  88.1 1.8 reshape_unstack.44
  90.0 1.9 copy.98
  91.9 1.8 reshape_unstack.45
  100.4 1.8 copy.103
  105.6 2.1 maximum_bitcast_fusion
  111.4 2.1 copy.100
  115.7 25.2 %all-gather.17.cloned.1.call-done = bf16[32,60,1280]{2,1,0:T(8,128)(2,1)} async-done(((bf16[1,60,1280]{2,1,0:T(8,128)(2,1)}), bf16[32,60,1280]{2,1,0:T(8,128)(2,1)}) %all-gather.17.cloned.1.call-update) | async-done | bytes 4915216 | tf_op jit(solution)/shard_map/all_gather | solution.py:87
  140.9 5.5 fusion.138
  146.4 2.7 reshape.479
  149.1 4.8 reshape.478
  157.3 27.7 %all-gather.11.cloned.1.call-done = bf16[1,2048,640]{1,2,0:T(8,128)(2,1)} async-done(((bf16[1,128,640]{1,2,0:T(8,128)(2,1)}), bf16[1,2048,640]{1,2,0:T(8,128)(2,1)}) %all-gather.11.cloned.1.call-update) | async-done | bytes 2621456 | tf_op jit(solution)/shard_map/all_gather | solution.py:160
  185.0 1.9 fusion.141
  186.9 6.8 fusion.45
  193.7 8.9 fusion.43
  202.6 8.3 fusion.142
  210.9 67.0 %all-gather.15.cloned.1.call-done = bf16[32,380,480]{1,2,0:T(8,128)(2,1)} async-done(((bf16[1,380,480]{1,2,0:T(8,128)(2,1)}), bf16[32,380,480]{1,2,0:T(8,128)(2,1)}) %all-gather.15.cloned.1.call-update) | async-done | bytes 11673616 | tf_op jit(solution)/shard_map/all_gather | solution.py:87
  277.9 3.7 fusion.137
  281.6 16.0 %fusion.136 = (bf16[1,16,160,480]{2,3,1,0:T(8,128)(2,1)}, bf16[1,16,160,480]{2,3,1,0:T(8,128)(2,1)}, bf16[1,16,160,480]{2,3,1,0:T(8,128)(2,1)}, bf16[1,16,160,480]{2,3,1,0:T(8,128)(2,1)}) fusion(bf16[2,16,380,480]{2,3,1,0:T(8,128)(2,1)} %bitcast.375), kind=kLoop, calls=%fused_computation.214 | loop fusion | bytes 19660800 | tf_op jit(solution)/shard_map/unstack | solution.py:93
  297.6 1.8 copy.128
  301.0 3.2 copy.129
  306.7 5.8 copy.130
  312.5 5.1 copy.132
  317.8 4.6 fusion.105
  322.4 2.1 fusion.103
  324.6 5.0 copy.133
  329.6 6.0 copy.131
  335.7 2.5 convolution_add_fusion
  338.4 3.3 multiply_convert_fusion.1
  348.8 1.9 broadcast_in_dim.64
  350.7 7.0 while.13
  357.8 11.7 %copy.125 = bf16[1,2048,640]{2,0,1:T(2,128)(2,1)} copy(bf16[1,2048,640]{1,2,0:T(8,128)(2,1)} %get-tuple-element.66) | data formatting | bytes 5242880
  369.5 4.5 copy.135
  375.1 2.2 fusion.50
  377.4 4.2 stack_reshape.54
  381.6 2.2 fusion.51
  383.8 4.1 stack_reshape.55
  387.9 5.3 pad_maximum_fusion
  397.3 2.4 stack_reshape.43
  402.2 55.8 %reduce-scatter.13.cloned.1.call-done = bf16[128,640]{1,0:T(8,128)(2,1)} async-done(((bf16[2048,640]{1,0:T(8,128)(2,1)}), bf16[128,640]{1,0:T(8,128)(2,1)}) %reduce-scatter.13.cloned.1.call-update) | async-done | bytes 163856
  469.4 2.1 fusion.67
  471.7 3.7 pad_maximum_fusion.1
  476.5 2.2 convolution_convert_fusion.3
  478.8 3.1 copy.111
  481.9 2.4 convolution_convert_fusion.7
  484.3 2.3 stack_reshape.48
  486.6 2.4 convolution_convert_fusion.6
  489.0 2.4 stack_reshape.49
  491.4 3.5 convolution_convert_fusion.2
  494.9 4.4 copy.112
  499.2 3.4 convolution_convert_fusion.1
  502.7 4.4 copy.113
  507.1 3.4 convolution_convert_fusion
  510.5 4.4 copy.114
  514.9 11.6 %maximum_maximum_fusion = bf16[2,16,380,480]{3,2,1,0:T(8,128)(2,1)} fusion(bf16[1,16,160,480]{3,2,1,0:T(8,128)(2,1)} %bitcast.394, bf16[1,16,160,480]{3,2,1,0:T(8,128)(2,1)} %bitcast.393, bf16[1,16,160,480]{3,2,1,0:T(8,128)(2,1)} %bitcast.392, bf16[1,16,160,480]{3,2,1,0:T(8,128)(2,1)S(1)} %bitcast.389, bf16[1,16,60,480]{3,2,1,0:T(8,128)(2,1)} %stack_reshape.49, ...), kind=kLoop, calls=%fused_computation.41 | loop fusion | flops 70041600 | bytes 23347200 | tf_op jit(solution)/shard_map/concatenate | solution.py:212
  528.2 1.9 fusion.78
  532.8 71.2 %reduce-scatter.11.cloned.1.call-done = bf16[1,60,1280]{2,1,0:T(8,128)(2,1)} async-done(((bf16[32,60,1280]{2,1,0:T(8,128)(2,1)}), bf16[1,60,1280]{2,1,0:T(8,128)(2,1)}) %reduce-scatter.11.cloned.1.call-update) | async-done | bytes 153616 | tf_op jit(solution)/shard_map/reduce_scatter | solution.py:98
  605.6 137.3 %reduce-scatter.7.cloned.1.call-done = bf16[1,101,480]{2,1,0:T(8,128)(2,1)} async-done(((bf16[32,101,480]{2,1,0:T(8,128)(2,1)}), bf16[1,101,480]{2,1,0:T(8,128)(2,1)}) %reduce-scatter.7.cloned.1.call-update) | async-done | bytes 96976 | tf_op jit(solution)/shard_map/reduce_scatter | solution.py:98
  745.8 154.2 %reduce-scatter.9.cloned.1.call-done = bf16[1,380,480]{2,1,0:T(8,128)(2,1)} async-done(((bf16[32,380,480]{2,1,0:T(8,128)(2,1)}), bf16[1,380,480]{2,1,0:T(8,128)(2,1)}) %reduce-scatter.9.cloned.1.call-update) | async-done | bytes 364816 | tf_op jit(solution)/shard_map/reduce_scatter | solution.py:98
  (230 shorter events, 78.5 us)
Async XLA Ops:
  7.2 67.1 %all-gather.13.cloned.1.call-start = ((), (), s32[]{:S(2)}) async-start(), calls=%async_computation.8 | async-start | bytes 3514368 | tf_op jit(solution)/shard_map/all_gather | solution.py:87
  9.5 131.4 %all-gather.17.cloned.1.call-start = ((), (), s32[]{:S(2)}) async-start(), calls=%async_computation.10 | async-start | bytes 5406720 | tf_op jit(solution)/shard_map/all_gather | solution.py:87
  10.3 174.7 %all-gather.11.cloned.1.call-start = ((), (), s32[]{:S(2)}) async-start(), calls=%async_computation.4 | async-start | bytes 2785280 | tf_op jit(solution)/shard_map/all_gather | solution.py:160
  11.5 0.6 copy-start.53
  93.7 5.7 copy-start.36
  94.9 20.3 %copy-start.7 = (bf16[128,960]{0,1:T(8,128)(2,1)}, bf16[128,960]{0,1:T(8,128)(2,1)S(1)}, u32[]{:S(2)}) copy-start(bf16[128,960]{0,1:T(8,128)(2,1)S(1)} %fusion.66) | copy-start | bytes 737284
  100.4 177.5 %all-gather.15.cloned.1.call-start = ((), (), s32[]{:S(2)}) async-start(), calls=%async_computation.9 | async-start | bytes 12165120 | tf_op jit(solution)/shard_map/all_gather | solution.py:87
  107.8 350.2 %reduce-scatter.13.cloned.1.call-start = ((), (), s32[]{:S(2)}) async-start(), calls=%async_computation.11 | async-start | bytes 2785280
  110.9 3.1 copy-start.51
  111.4 3.8 copy-start.16
  113.5 2.1 copy-start.45
  113.5 2.1 copy-start.47
  114.0 32.4 %copy-start.18 = (bf16[960,480]{1,0:T(8,128)(2,1)}, bf16[960,480]{1,0:T(8,128)(2,1)S(1)}, u32[]{:S(2)}) copy-start(bf16[960,480]{1,0:T(8,128)(2,1)S(1)} %reshape_unstack.47) | copy-start | bytes 2764804
  149.1 6.2 copy-start.3
  149.1 4.8 copy-start.13
  153.9 1.9 copy-start.5
  157.3 29.6 %copy-start.35 = (pred[128,2048]{0,1:T(8,128)(4,1)S(1)}, pred[128,2048]{0,1:T(8,128)(4,1)}, u32[]{:S(2)}) copy-start(pred[128,2048]{0,1:T(8,128)(4,1)} %iota_compare_fusion) | copy-start | bytes 786436
  210.9 95.3 %copy-start.42 = (bf16[1,5,3,128,64]{3,4,2,1,0:T(8,128)(2,1)}, bf16[1,5,3,128,64]{3,4,2,1,0:T(8,128)(2,1)S(1)}, u32[]{:S(2)}) copy-start(bf16[1,5,3,128,64]{3,4,2,1,0:T(8,128)(2,1)S(1)} %get-tuple-element.160) | copy-start | bytes 737284
  300.9 5.3 copy-start.20
  301.0 5.3 copy-start.25
  305.8 6.7 copy-start.22
  312.5 5.1 copy-start.49
  317.6 7.0 copy-start
  317.8 6.8 copy-start.28
  335.6 2.6 copy-start.9
  335.6 2.6 copy-start.29
  335.7 2.6 copy-start.41
  335.7 2.8 copy-start.43
  338.4 3.3 copy-start.2
  341.8 2.3 copy-start.11
  341.8 4.0 copy-start.10
  342.9 1.7 copy-start.1
  345.8 1.6 copy-start.14
  345.8 1.8 copy-start.21
  346.9 1.2 copy-start.23
  347.3 1.5 copy-start.31
  347.3 1.4 copy-start.44
  347.6 1.1 copy-start.24
  373.9 0.9 copy-start.15
  373.9 1.2 copy-start.37
  373.9 230.0 %reduce-scatter.11.cloned.1.call-start = ((), (), s32[]{:S(2)}) async-start(), calls=%async_computation.7 | async-start | bytes 5406720 | tf_op jit(solution)/shard_map/reduce_scatter | solution.py:98
  393.2 0.7 copy-start.46
  393.2 0.7 copy-start.48
  393.2 1.0 copy-start.8
  393.2 349.7 %reduce-scatter.7.cloned.1.call-start = ((), (), s32[]{:S(2)}) async-start(), calls=%async_computation.5 | async-start | bytes 3514368 | tf_op jit(solution)/shard_map/reduce_scatter | solution.py:98
  394.6 5.1 copy-start.17
  395.9 5.1 copy-start.19
  459.4 1.4 copy-start.39
  461.6 7.7 copy-start.26
  461.6 7.7 copy-start.50
  461.6 7.7 copy-start.52
  463.8 7.9 copy-start.33
  463.8 7.9 copy-start.34
  475.4 1.1 copy-start.12
  475.4 1.1 copy-start.30
  475.4 424.5 %reduce-scatter.9.cloned.1.call-start = ((), (), s32[]{:S(2)}) async-start(), calls=%async_computation.6 | async-start | bytes 12976128 | tf_op jit(solution)/shard_map/reduce_scatter | solution.py:98
  526.5 1.7 copy-start.6
  528.2 1.9 copy-start.4
  528.2 1.9 copy-start.38
  530.2 1.5 copy-start.54
  530.2 1.5 copy-start.27
  530.2 1.5 copy-start.32
  530.2 1.5 copy-start.40
Sparse Core Ops, SparseCore 0:
  11.4 62.7 all-gather.12
  77.1 63.8 all-gather.16
  143.1 41.8 all-gather.10
  187.7 90.0 all-gather.14
  374.1 83.9 reduce-scatter.12
  460.2 143.7 reduce-scatter.10
  606.3 136.6 reduce-scatter.6
  748.9 150.9 reduce-scatter.8
where the time goes:
time: 917 us; the launch traced here: 910 us
  waiting for transfers between devices  600 us (65%)
  local copies, waits for them, and re-layouts  161 us (18%)
  matrix products  82.2 us (9%)
  other arithmetic  49.6 us (5%)
  between operations  15.3 us (2%)
    reduce_scatter x3, waiting for transfers between devices, scatter_rows(): lax.psum_scatter(merged, BOTH, scatter_dimension=0, tiled=True)[0]  363 us
    all_gather x3, waiting for transfers between devices, gather_rows(): gathered = lax.all_gather(packed, BOTH, axis=0, tiled=False)  153 us
    unnamed x9, waiting for transfers between devices  56.6 us
    unnamed x123, local copies, waits for them, and re-layouts  56.4 us
    another operation x21, local copies, waits for them, and re-layouts, take(): return [part.reshape(-1, part.shape[-1]) for part in piece]  55.5 us
    all_gather x1, waiting for transfers between devices, local(): lax.all_gather(jnp.concatenate([key_rows, value_rows], axis=-1), 'ctx', a...  27.7 us
    dot_general x14, matrix products, weight_terms(): lax.dot_general(grads, piece, (((0,), (0,)), ((), ())), preferred_element...  24.6 us
    dot_general x14, matrix products, forward_dot(): lax.dot_general(piece, half, (((1,), (1,)), ((), ())), preferred_element_...  21.6 us
  transfers between devices with their start and end apart: 8, of which 8 were waited for; matrix products, arithmetic and copies ran while one was open for 21% of the time, Pallas kernels for 0%

commit v1 on v0

v1 whole, which is shorter than its diff:
```python
import functools

import jax
import jax.numpy as jnp
from jax import lax
from jax.experimental import pallas as pl
from jax.experimental.pallas import tpu as pltpu
from jax.sharding import PartitionSpec as P

HEADS = 15
KV_HEADS = 5
HEAD = 64

EPSILON = 1e-05
ROPE_THETA = 100000.0
MESH = pl.DeviceIdType.MESH
VMEM_LIMIT = 60 * 1024 * 1024


def tables(positions, head_size):
    half_size = head_size // 2
    frequency = ROPE_THETA ** (-jnp.arange(half_size, dtype=jnp.float32) * 2.0 / head_size)
    angles = positions.astype(jnp.float32)[:, None] * frequency[None, :]
    return (jnp.cos(angles), jnp.sin(angles))


def rotate(values, cosine, sine_table):
    half_size = values.shape[-1] // 2
    first_half = values[..., :half_size]
    second = values[..., half_size:]
    cosine = cosine[:, None, :]
    sine_table = sine_table[:, None, :]
    return jnp.concatenate(
        [first_half * cosine - second * sine_table, second * cosine + first_half * sine_table],
        axis=-1,
    )


def unrotate(values, cosine, sine_table):
    return rotate(values, cosine, -sine_table)


def normed(row_values, gain_vec):
    scale_rows = lax.rsqrt(jnp.mean(row_values * row_values, axis=-1, keepdims=True) + EPSILON)
    return row_values * scale_rows * gain_vec


class Place:
    def __init__(self, depth, use_x):
        self.depth = depth
        self.use_x = use_x
        self.f = lax.axis_index("fsdp")
        self.ctx = lax.axis_index("ctx")
        self.c = self.ctx % 2
        self.y = (self.ctx // 2) % 2
        self.z = self.ctx // 4
        self.has_up = self.z < depth - 1
        self.has_down = self.z > 0

    def device(self, way):
        if way == "c":
            return (self.f, self.ctx + 1 - 2 * self.c)
        if way == "y":
            return (self.f, self.ctx + 2 - 4 * self.y)
        if way == "x":
            return (1 - self.f, self.ctx)
        return (self.f, self.ctx + (4 if way == "up" else -4))

    def piece(self, route, rel_p, rel_q, z):
        rel = {route[1]: rel_q}
        if route[0] is not None:
            rel[route[0]] = rel_p
        y0 = 1 - self.y if rel.get("y", 0) else self.y
        pid = z * 2 + y0
        if self.use_x:
            x0 = 1 - self.f if rel.get("x", 0) else self.f
            pid = pid + x0 * 2 * self.depth
        return pid

    def barrier(self):
        sem = pltpu.get_barrier_semaphore()
        ways = ["c", "y"] + (["x"] if self.use_x else [])
        for way in ways:
            pl.semaphore_signal(sem, inc=1, device_id=self.device(way), device_id_type=MESH)

        @pl.when(self.has_up)
        def _():
            pl.semaphore_signal(sem, inc=1, device_id=self.device("up"), device_id_type=MESH)

        @pl.when(self.has_down)
        def _():
            pl.semaphore_signal(sem, inc=1, device_id=self.device("down"), device_id_type=MESH)

        peers = len(ways) + self.has_up.astype(jnp.int32) + self.has_down.astype(jnp.int32)
        pl.semaphore_wait(sem, peers)


def both_sides(place, distance, body):
    high = place.z + distance
    low = place.z - distance

    @pl.when((distance >= 0) & (high < place.depth))
    def _():
        body(high, True)

    @pl.when((distance >= 1) & (low >= 0))
    def _():
        body(low, False)


def gather_kernel(depth, use_x, routes, *refs):
    count = len(routes)
    ins, outs = refs[:count], refs[count : 2 * count]
    recv, send_z, send_p, send_q, send_c, local_sem = refs[2 * count :]
    place = Place(depth, use_x)
    place.barrier()

    def copy(k, pid, send_sem, way, src=None):
        slot = pid * 2 + place.c
        return pltpu.make_async_remote_copy(
            src_ref=outs[k].at[slot] if src is None else src,
            dst_ref=outs[k].at[slot],
            send_sem=send_sem,
            recv_sem=recv.at[k, slot],
            device_id=place.device(way),
            device_id_type=MESH,
        )

    def forward_z(k, z0, up, src=None):
        pid = place.piece(routes[k], 0, 0, z0)
        return copy(k, pid, send_z.at[k, 0 if up else 1, z0], "up" if up else "down", src)

    def forward_p(k, z0, src=None):
        return copy(k, place.piece(routes[k], 0, 0, z0), send_p.at[k, z0], routes[k][0], src)

    def forward_q(k, rel_p, z0, src=None):
        pid = place.piece(routes[k], rel_p, 0, z0)
        return copy(k, pid, send_q.at[k, rel_p, z0], routes[k][1], src)

    def forward_c(k, pid, src=None):
        return copy(k, pid, send_c.at[k, pid], "c", src)

    def arrived(k, pid):
        copy(k, pid, send_c.at[k, pid], "c").wait_recv()

    own = []
    for k in range(count):
        pid = place.piece(routes[k], 0, 0, place.z)
        src = ins[k]

        @pl.when(place.has_up)
        def _():
            forward_z(k, place.z, True, src).start()

        @pl.when(place.has_down)
        def _():
            forward_z(k, place.z, False, src).start()

        if routes[k][0] is not None:
            forward_p(k, place.z, src).start()
        forward_q(k, 0, place.z, src).start()
        forward_c(k, pid, src).start()
        mine = pltpu.make_async_copy(src, outs[k].at[pid * 2 + place.c], local_sem.at[k])
        mine.start()
        own.append(mine)

    def step(d, carry):
        def from_z(z0, above):
            for k in range(count):
                pid = place.piece(routes[k], 0, 0, z0)
                arrived(k, pid)
                if above:

                    @pl.when(place.has_down)
                    def _():
                        forward_z(k, z0, False).start()

                else:

                    @pl.when(place.has_up)
                    def _():
                        forward_z(k, z0, True).start()

                if routes[k][0] is not None:
                    forward_p(k, z0).start()
                forward_q(k, 0, z0).start()
                forward_c(k, pid).start()

        def from_p(z0, above):
            for k in range(count):
                if routes[k][0] is not None:
                    pid = place.piece(routes[k], 1, 0, z0)
                    arrived(k, pid)
                    forward_q(k, 1, z0).start()
                    forward_c(k, pid).start()

        def from_q(rel_p, z0, above):
            for k in range(count):
                if routes[k][0] is not None or not rel_p:
                    pid = place.piece(routes[k], rel_p, 1, z0)
                    arrived(k, pid)
                    forward_c(k, pid).start()

        @pl.when((d >= 1) & (d < depth))
        def _():
            both_sides(place, d, from_z)

        both_sides(place, d - 1, from_p)
        both_sides(place, d - 1, functools.partial(from_q, 0))
        both_sides(place, d - 2, functools.partial(from_q, 1))
        return carry

    lax.fori_loop(1, depth + 2, step, 0)

    def finish(z0, carry):
        for k in range(count):

            @pl.when(place.has_up & (z0 <= place.z))
            def _():
                forward_z(k, z0, True).wait_send()

            @pl.when(place.has_down & (z0 >= place.z))
            def _():
                forward_z(k, z0, False).wait_send()

            if routes[k][0] is not None:
                forward_p(k, z0).wait_send()
                forward_q(k, 1, z0).wait_send()
            forward_q(k, 0, z0).wait_send()
        return carry

    lax.fori_loop(0, depth, finish, 0)

    def finish_partner(pid, carry):
        for k in range(count):
            forward_c(k, pid).wait_send()
            slot = pid * 2 + 1 - place.c
            pltpu.make_async_remote_copy(
                src_ref=outs[k].at[slot],
                dst_ref=outs[k].at[slot],
                send_sem=send_c.at[k, pid],
                recv_sem=recv.at[k, slot],
                device_id=place.device("c"),
                device_id_type=MESH,
            ).wait_recv()
        return carry

    lax.fori_loop(0, (4 if use_x else 2) * depth, finish_partner, 0)
    for mine in own:
        mine.wait()


def gather(arrays, routes, use_x, collective_id, name):
    depth = lax.axis_size("ctx") // 4
    pieces = (4 if use_x else 2) * depth
    count = len(arrays)
    dma = pltpu.SemaphoreType.DMA
    return pl.pallas_call(
        functools.partial(gather_kernel, depth, use_x, routes),
        out_shape=[jax.ShapeDtypeStruct((2 * pieces, *a.shape), a.dtype) for a in arrays],
        in_specs=[pl.BlockSpec(memory_space=pltpu.VMEM)] * count,
        out_specs=[pl.BlockSpec(memory_space=pl.ANY)] * count,
        scratch_shapes=[
            dma((count, 2 * pieces)),
            dma((count, 2, depth)),
            dma((count, depth)),
            dma((count, 2, depth)),
            dma((count, pieces)),
            dma((count,)),
        ],
        compiler_params=pltpu.CompilerParams(
            collective_id=collective_id, has_side_effects=True, vmem_limit_bytes=VMEM_LIMIT
        ),
        name=name,
    )(*arrays)


def add_up(dst, sources, rows):
    block = 32 if rows % 32 == 0 else 16

    def body(i, carry):
        span = pl.ds(pl.multiple_of(i * block, block), block)
        total = sources[0][span, :].astype(jnp.float32)
        for source in sources[1:]:
            total = total + source[span, :].astype(jnp.float32)
        dst[span, :] = total.astype(dst.dtype)
        return carry

    lax.fori_loop(0, rows // block, body, 0)


def scatter_kernel(depth, use_x, routes, *refs):
    count = len(routes)
    ins, outs = refs[:count], refs[count : 2 * count]
    own, part, land_q, land_p, land_z = (
        refs[(2 + i) * count : (3 + i) * count] for i in range(5)
    )
    load_sem, c_send, c_recv, q_send, q_recv, p_send, p_recv, z_send, z_recv = refs[7 * count :]
    place = Place(depth, use_x)
    pieces = (4 if use_x else 2) * depth
    rows = [out.shape[0] for out in outs]

    def load(k):
        return pltpu.make_async_copy(ins[k].at[:, place.c], own[k], load_sem.at[k])

    for k in range(count):
        load(k).start()
    place.barrier()

    def remote(src, dst, send_sem, recv_sem, way):
        return pltpu.make_async_remote_copy(
            src_ref=src,
            dst_ref=dst,
            send_sem=send_sem,
            recv_sem=recv_sem,
            device_id=place.device(way),
            device_id_type=MESH,
        )

    def send_c(k, pid):
        return remote(
            ins[k].at[pid, 1 - place.c], part[k].at[pid], c_send.at[k, pid], c_recv.at[k, pid], "c"
        )

    def send_q(k, rel_p, z0):
        pid = place.piece(routes[k], rel_p, 1, z0)
        return remote(
            own[k].at[pid],
            land_q[k].at[rel_p, z0],
            q_send.at[k, rel_p, z0],
            q_recv.at[k, rel_p, z0],
            routes[k][1],
        )

    def send_p(k, z0):
        pid = place.piece(routes[k], 1, 0, z0)
        return remote(
            own[k].at[pid], land_p[k].at[z0], p_send.at[k, z0], p_recv.at[k, z0], routes[k][0]
        )

    def send_z(k, z0, up):
        pid = place.piece(routes[k], 0, 0, z0)
        if up:
            target = z0
        else:
            target = jnp.where(z0 == place.z - 1, depth, z0)
        return remote(
            own[k].at[pid],
            land_z[k].at[target],
            z_send.at[k, z0],
            z_recv.at[k, target],
            "up" if up else "down",
        )

    def wait_z(k, index):
        pltpu.make_async_copy(land_z[k].at[index], land_z[k].at[index], z_recv.at[k, index]).wait()

    def first(s, carry):
        def body(z0, above):
            for k in range(count):
                for rel_q in (1, 0):
                    for rel_p in (1, 0) if routes[k][0] is not None else (0,):
                        send_c(k, place.piece(routes[k], rel_p, rel_q, z0)).start()

        both_sides(place, depth - 1 - s, body)
        return carry

    lax.fori_loop(0, depth, first, 0)
    for k in range(count):
        load(k).wait()

    def step(s, carry):
        def leaf(z0, above):
            for k in range(count):
                for rel_p in (1, 0) if routes[k][0] is not None else (0,):
                    pid = place.piece(routes[k], rel_p, 1, z0)
                    send_c(k, pid).wait_recv()
                    add_up(own[k].at[pid], [own[k].at[pid], part[k].at[pid]], rows[k])
                    send_q(k, rel_p, z0).start()

        def middle(z0, above):
            for k in range(count):
                if routes[k][0] is not None:
                    pid = place.piece(routes[k], 1, 0, z0)
                    send_c(k, pid).wait_recv()
                    send_q(k, 1, z0).wait_recv()
                    add_up(
                        own[k].at[pid],
                        [own[k].at[pid], part[k].at[pid], land_q[k].at[1, z0]],
                        rows[k],
                    )
                    send_p(k, z0).start()

        def sources_of(k, z0):
            pid = place.piece(routes[k], 0, 0, z0)
            send_c(k, pid).wait_recv()
            send_q(k, 0, z0).wait_recv()
            sources = [own[k].at[pid], part[k].at[pid], land_q[k].at[0, z0]]
            if routes[k][0] is not None:
                send_p(k, z0).wait_recv()
                sources.append(land_p[k].at[z0])
            return pid, sources

        def along(z0, above):
            for k in range(count):
                pid, sources = sources_of(k, z0)
                child = place.has_down if above else place.has_up

                @pl.when(child)
                def _():
                    wait_z(k, z0)
                    add_up(own[k].at[pid], sources + [land_z[k].at[z0]], rows[k])

                @pl.when(jnp.logical_not(child))
                def _():
                    add_up(own[k].at[pid], sources, rows[k])

                send_z(k, z0, above).start()

        both_sides(place, depth - 1 - s, leaf)

        @pl.when(s < depth + 1)
        def _():
            both_sides(place, depth - s, middle)

        @pl.when(depth + 1 - s >= 1)
        def _():
            both_sides(place, depth + 1 - s, along)

        @pl.when(s == depth + 1)
        def _():
            for k in range(count):
                _, sources = sources_of(k, place.z)
                add_up(outs[k], sources, rows[k])

                @pl.when(place.has_down)
                def _():
                    wait_z(k, place.z)
                    add_up(outs[k], [outs[k], land_z[k].at[place.z]], rows[k])

                @pl.when(place.has_up)
                def _():
                    wait_z(k, depth)
                    add_up(outs[k], [outs[k], land_z[k].at[depth]], rows[k])

        return carry

    lax.fori_loop(0, depth + 2, step, 0)

    def finish(z0, carry):
        for k in range(count):
            send_q(k, 0, z0).wait_send()
            if routes[k][0] is not None:
                send_q(k, 1, z0).wait_send()
                send_p(k, z0).wait_send()

            @pl.when(z0 > place.z)
            def _():
                send_z(k, z0, True).wait_send()

            @pl.when(z0 < place.z)
            def _():
                send_z(k, z0, False).wait_send()

        return carry

    lax.fori_loop(0, depth, finish, 0)

    def finish_partner(pid, carry):
        for k in range(count):
            send_c(k, pid).wait_send()
        return carry

    lax.fori_loop(0, pieces, finish_partner, 0)


def scatter(arrays, routes, use_x, collective_id, name):
    depth = lax.axis_size("ctx") // 4
    pieces = (4 if use_x else 2) * depth
    count = len(arrays)
    dma = pltpu.SemaphoreType.DMA
    shapes = [a.shape[1:] for a in arrays]
    pairs = [a.reshape(pieces, 2, *s) for a, s in zip(arrays, shapes)]
    bf16 = jnp.bfloat16
    return pl.pallas_call(
        functools.partial(scatter_kernel, depth, use_x, routes),
        out_shape=[jax.ShapeDtypeStruct(s, jnp.float32) for s in shapes],
        in_specs=[pl.BlockSpec(memory_space=pl.ANY)] * count,
        out_specs=[pl.BlockSpec(memory_space=pltpu.VMEM)] * count,
        scratch_shapes=[pltpu.VMEM((pieces, *s), bf16) for s in shapes]
        + [pltpu.VMEM((pieces, *s), bf16) for s in shapes]
        + [pltpu.VMEM((2, depth, *s), bf16) for s in shapes]
        + [pltpu.VMEM((depth, *s), bf16) for s in shapes]
        + [pltpu.VMEM((depth + 1, *s), bf16) for s in shapes]
        + [
            dma((count,)),
            dma((count, pieces)),
            dma((count, pieces)),
            dma((count, 2, depth)),
            dma((count, 2, depth)),
            dma((count, depth)),
            dma((count, depth)),
            dma((count, depth)),
            dma((count, depth + 1)),
        ],
        compiler_params=pltpu.CompilerParams(
            collective_id=collective_id, has_side_effects=True, vmem_limit_bytes=VMEM_LIMIT
        ),
        name=name,
    )(*pairs)


def padded(rows, multiple=16):
    return -(-rows // multiple) * multiple


def pad_rows(rows, total):
    return jnp.pad(rows, ((0, total - rows.shape[0]), (0, 0)))


XY, YX, ONLY_Y = ("x", "y"), ("y", "x"), (None, "y")
WEIGHT_ROUTES = (YX, YX, XY, XY, YX)


def halves(values, split_count):
    return values.reshape(values.shape[0], split_count, values.shape[1] // split_count)


def forward_dot(values, weights):
    split_count = weights.shape[0]
    part = values.shape[1] // split_count
    total = None
    for i in range(split_count):
        term = lax.dot_general(
            values[:, i * part : (i + 1) * part],
            weights[i],
            (((1,), (1,)), ((), ())),
            preferred_element_type=jnp.float32,
        )
        total = term if total is None else total + term
    return total


def backward_dot(grads, weights):
    return jnp.concatenate(
        [
            jnp.dot(grads, weights[i], preferred_element_type=jnp.float32)
            for i in range(weights.shape[0])
        ],
        axis=-1,
    )


def weight_terms(grads, values, split_count):
    part = values.shape[1] // split_count
    return jnp.stack(
        [
            lax.dot_general(
                grads,
                values[:, i * part : (i + 1) * part],
                (((0,), (0,)), ((), ())),
                preferred_element_type=jnp.float32,
            ).astype(jnp.bfloat16)
            for i in range(split_count)
        ]
    )


def local(
    inputs, grad_output, w_query, w_key, w_value, w_out, w_gate, w_up, w_down, gain_attn, gain_mlp
):
    seq_count, block_len, model_width = inputs.shape
    row_count = seq_count * block_len
    split_count = lax.axis_size("fsdp")
    cycle_size = lax.axis_size("ctx")
    cycle_index = lax.axis_index("ctx")
    length = block_len * cycle_size
    key_block = min(512, length)
    groups = KV_HEADS
    head_size = HEAD
    repeat_count = HEADS // KV_HEADS
    kv_width = groups * head_size
    positions = cycle_index * block_len + jnp.arange(block_len, dtype=jnp.int32)
    cosine, sine_table = tables(positions, head_size)
    cosine = jnp.tile(cosine, (seq_count, 1))
    sine_table = jnp.tile(sine_table, (seq_count, 1))
    needed = (cycle_index * block_len + block_len + key_block - 1) // key_block
    wide_q, wide_k, wide_v = w_query.shape[1], w_key.shape[1], w_value.shape[1]
    wide_o, wide_g, wide_u = w_out.shape[1], w_gate.shape[1], w_up.shape[1]
    wide_d = w_down.shape[1]
    pad_q, pad_k, pad_v = padded(wide_q), padded(wide_k + 1), padded(wide_v)
    pad_o, pad_g, pad_u, pad_d = padded(wide_o), padded(wide_g), padded(wide_u), padded(wide_d)
    part_width = w_query.shape[0]
    gain_size = gain_attn.shape[0]

    def open_up(values, wide, start, pad):
        pieces = values.reshape(values.shape[0], cycle_size, -1)
        return pieces[:, :, start : start + wide].reshape(values.shape[0], cycle_size * wide)

    def close_up(values, wide, pad):
        pieces = values.reshape(values.shape[0], cycle_size, wide)
        return jnp.pad(pieces, ((0, 0), (0, 0), (0, pad - wide))).reshape(values.shape[0], -1)

    gain_row = jnp.pad(
        jnp.concatenate([gain_attn, gain_mlp]), (0, part_width - 2 * gain_size)
    )[None, :]
    first_piece = jnp.concatenate(
        [
            pad_rows(w_query.T, pad_q),
            pad_rows(jnp.concatenate([w_key.T, gain_row], axis=0), pad_k),
            pad_rows(w_value.T, pad_v),
        ],
        axis=0,
    )
    first, out_w, gate_w, up_w, down_w = gather(
        [
            first_piece,
            pad_rows(w_out.T, pad_o),
            pad_rows(w_gate.T, pad_g),
            pad_rows(w_up.T, pad_u),
            pad_rows(w_down.T, pad_d),
        ],
        WEIGHT_ROUTES,
        True,
        0,
        "gather_weights",
    )
    gain_rows = first[:cycle_size, pad_q + wide_k, : 2 * gain_size]
    gain_first = gain_rows[:, :gain_size].reshape(-1).astype(jnp.float32)
    gain_second = gain_rows[:, gain_size:].reshape(-1).astype(jnp.float32)
    first, out_w, gate_w, up_w, down_w = (
        w.reshape(split_count, -1, w.shape[-1]) for w in (first, out_w, gate_w, up_w, down_w)
    )

    resid1 = inputs.reshape(row_count, model_width).astype(jnp.float32)
    normal1 = normed(resid1, gain_first).astype(jnp.bfloat16)
    raw = forward_dot(normal1, first)
    query_raw = open_up(raw, wide_q, 0, pad_q).reshape(row_count, HEADS, head_size)
    query_rot = rotate(query_raw, cosine, sine_table).astype(jnp.bfloat16)
    key_raw = open_up(raw, wide_k, pad_q, pad_k).reshape(row_count, groups, head_size)
    key_rows = (
        rotate(key_raw, cosine, sine_table)
        .astype(jnp.bfloat16)
        .reshape(seq_count, block_len, kv_width)
    )
    value_rows = (
        open_up(raw, wide_v, pad_q + pad_k, pad_v)
        .astype(jnp.bfloat16)
        .reshape(seq_count, block_len, kv_width)
    )
    query_grouped = query_rot.reshape(seq_count, block_len, groups, repeat_count, head_size)
    (pair_all,) = gather(
        [jnp.concatenate([key_rows, value_rows], axis=-1).reshape(row_count, 2 * kv_width)],
        (ONLY_Y,),
        False,
        1,
        "gather_pairs",
    )
    pair_all = pair_all.reshape(cycle_size, seq_count, block_len, 2 * kv_width)
    pair_all = jnp.transpose(pair_all, (1, 0, 2, 3)).reshape(seq_count, length, 2 * kv_width)
    keys_all = pair_all[..., :kv_width]
    values_all = pair_all[..., kv_width:]
    key_heads = keys_all.reshape(seq_count, length, groups, head_size)
    value_heads = values_all.reshape(seq_count, length, groups, head_size)
    scores = (
        jnp.einsum(
            "sqgrd,skgd->sgrqk", query_grouped, key_heads, preferred_element_type=jnp.float32
        )
        * 0.125
    )
    allowed = jnp.arange(length, dtype=jnp.int32)[None, :] <= positions[:, None]
    scores = jnp.where(allowed, scores, -jnp.inf)
    new_peak = jnp.max(scores, axis=-1)
    exp_terms = jnp.exp(scores - new_peak[..., None])
    denom_run = jnp.sum(exp_terms, axis=-1)
    running = jnp.einsum(
        "sgrqk,skgd->sgrqd",
        exp_terms.astype(jnp.bfloat16),
        value_heads,
        preferred_element_type=jnp.float32,
    )
    attended_wide = running / denom_run[..., None]
    attended = jnp.transpose(attended_wide, (0, 3, 1, 2, 4)).astype(jnp.bfloat16)
    logsum = new_peak + jnp.log(denom_run)
    attended_rows = attended.reshape(row_count, HEADS * head_size)
    resid2 = resid1 + open_up(forward_dot(attended_rows, out_w), wide_o, 0, pad_o)
    normal2 = normed(resid2, gain_second).astype(jnp.bfloat16)
    gate_act = forward_dot(normal2, gate_w)
    up_act = forward_dot(normal2, up_w)
    gate_sigma = jax.nn.sigmoid(gate_act)
    hidden = (gate_act * gate_sigma * up_act).astype(jnp.bfloat16)
    hidden_flat = open_up(hidden, wide_g, 0, pad_g)
    output = (
        resid2 + open_up(forward_dot(hidden_flat, down_w), wide_d, 0, pad_d)
    ).astype(jnp.bfloat16)

    grad_rows = grad_output.reshape(row_count, model_width)
    grad_rows_padded = close_up(grad_rows, wide_d, pad_d)
    terms_down = weight_terms(grad_rows_padded, hidden_flat, split_count)
    grad_hidden = close_up(backward_dot(grad_rows_padded, down_w), wide_g, pad_g)
    grad_up = (grad_hidden * gate_act * gate_sigma).astype(jnp.bfloat16)
    grad_gate = (grad_hidden * up_act * gate_sigma * (1.0 + gate_act * (1.0 - gate_sigma))).astype(
        jnp.bfloat16
    )
    grad_norm2 = backward_dot(grad_gate, gate_w) + backward_dot(grad_up, up_w)
    normed_out, pull_second = jax.vjp(normed, resid2, gain_second)
    grad_part2, term_gain2 = pull_second(grad_norm2)
    grad_resid2 = grad_rows.astype(jnp.float32) + grad_part2
    grad_branch = close_up(grad_resid2.astype(jnp.bfloat16), wide_o, pad_o)
    terms_out = weight_terms(grad_branch, attended_rows, split_count)
    terms_gate = weight_terms(grad_gate, normal2, split_count)
    terms_up = weight_terms(grad_up, normal2, split_count)
    grad_attended = backward_dot(grad_branch, out_w).astype(jnp.bfloat16)
    grad_grouped = grad_attended.reshape(seq_count, block_len, groups, repeat_count, head_size)
    row_delta = jnp.sum(
        jnp.transpose(grad_grouped, (0, 2, 3, 1, 4)).astype(jnp.float32) * attended_wide, axis=-1
    )

    def retrace(step_index, loop_state):
        grad_query_acc, grad_pair_all = loop_state
        key_start = step_index * key_block
        pair = lax.dynamic_slice_in_dim(pair_all, key_start, key_block, 1)
        key_heads = pair[..., :kv_width].reshape(seq_count, key_block, groups, head_size)
        value_heads = pair[..., kv_width:].reshape(seq_count, key_block, groups, head_size)
        scores = (
            jnp.einsum(
                "sqgrd,skgd->sgrqk", query_grouped, key_heads, preferred_element_type=jnp.float32
            )
            * 0.125
        )
        allowed = (key_start + jnp.arange(key_block, dtype=jnp.int32))[None, :] <= positions[
            :, None
        ]
        prob_full = jnp.where(
            allowed, jnp.exp(jnp.where(allowed, scores, -jnp.inf) - logsum[..., None]), 0.0
        )
        grad_probs = jnp.einsum(
            "sqgrd,skgd->sgrqk", grad_grouped, value_heads, preferred_element_type=jnp.float32
        )
        grad_scores = (prob_full * (grad_probs - row_delta[..., None]) * 0.125).astype(jnp.bfloat16)
        prob_low = prob_full.astype(jnp.bfloat16)
        value_term = jnp.einsum(
            "sgrqk,sqgrd->skgd", prob_low, grad_grouped, preferred_element_type=jnp.float32
        ).reshape(seq_count, key_block, kv_width)
        key_term = jnp.einsum(
            "sgrqk,sqgrd->skgd", grad_scores, query_grouped, preferred_element_type=jnp.float32
        ).reshape(seq_count, key_block, kv_width)
        grad_query_acc = grad_query_acc + jnp.einsum(
            "sgrqk,skgd->sgrqd", grad_scores, key_heads, preferred_element_type=jnp.float32
        )
        pair_term = jnp.concatenate([key_term, value_term], axis=-1).astype(jnp.bfloat16)
        grad_pair_all = lax.dynamic_update_slice_in_dim(grad_pair_all, pair_term, key_start, 1)
        return (grad_query_acc, grad_pair_all)

    back_state = (
        jnp.zeros((seq_count, groups, repeat_count, block_len, head_size), jnp.float32),
        jnp.zeros((seq_count, length, 2 * kv_width), jnp.bfloat16),
    )
    grad_query_acc, grad_pair_all = lax.fori_loop(0, needed, retrace, back_state)
    grad_pair_all = grad_pair_all.reshape(seq_count, cycle_size, block_len, 2 * kv_width)
    grad_pair_all = jnp.transpose(grad_pair_all, (1, 0, 2, 3)).reshape(
        cycle_size, row_count, 2 * kv_width
    )
    (grad_pair_own,) = scatter([grad_pair_all], (ONLY_Y,), False, 2, "scatter_pairs")
    grad_query_rows = jnp.transpose(grad_query_acc, (0, 3, 1, 2, 4)).reshape(
        row_count, HEADS, head_size
    )
    grad_query = (
        unrotate(grad_query_rows, cosine, sine_table)
        .reshape(row_count, HEADS * head_size)
        .astype(jnp.bfloat16)
    )
    grad_keys = (
        unrotate(grad_pair_own[..., :kv_width].reshape(row_count, groups, head_size), cosine, sine_table)
        .reshape(row_count, kv_width)
        .astype(jnp.bfloat16)
    )
    grad_values = grad_pair_own[..., kv_width:].astype(jnp.bfloat16)

    def shaped(values, wide, pad):
        pieces = values.reshape(row_count, cycle_size, wide)
        return jnp.pad(pieces, ((0, 0), (0, 0), (0, pad - wide)))

    grad_raw = jnp.concatenate(
        [
            shaped(grad_query, wide_q, pad_q),
            shaped(grad_keys, wide_k, pad_k),
            shaped(grad_values, wide_v, pad_v),
        ],
        axis=-1,
    ).reshape(row_count, -1)
    grad_norm1 = backward_dot(grad_raw, first)
    normed_first, pull_first = jax.vjp(normed, resid1, gain_first)
    grad_part1, term_gain1 = pull_first(grad_norm1)
    grad_input = (
        (grad_resid2 + grad_part1).astype(jnp.bfloat16).reshape(seq_count, block_len, model_width)
    )
    gain_terms = jnp.concatenate(
        [term_gain1.reshape(cycle_size, -1), term_gain2.reshape(cycle_size, -1)], axis=-1
    ).astype(jnp.bfloat16)
    terms_first = weight_terms(grad_raw, normal1, split_count)
    terms_first = terms_first.reshape(split_count, cycle_size, -1, part_width)
    terms_first = terms_first.at[:, :, pad_q + wide_k, : 2 * gain_size].set(gain_terms[None])

    def pieces_of(terms):
        return terms.reshape(split_count * cycle_size, -1, terms.shape[-1])

    sum_first, sum_out, sum_gate, sum_up, sum_down = scatter(
        [pieces_of(t) for t in (terms_first, terms_out, terms_gate, terms_up, terms_down)],
        WEIGHT_ROUTES,
        True,
        3,
        "scatter_weights",
    )
    start_k, start_v = pad_q, pad_q + pad_k
    gain_sums = sum_first[pad_q + wide_k]
    return (
        output.reshape(seq_count, block_len, model_width),
        grad_input,
        sum_first[:wide_q].T,
        sum_first[start_k : start_k + wide_k].T,
        sum_first[start_v : start_v + wide_v].T,
        sum_out[:wide_o].T,
        sum_gate[:wide_g].T,
        sum_up[:wide_u].T,
        sum_down[:wide_d].T,
        gain_sums[:gain_size],
        gain_sums[gain_size : 2 * gain_size],
    )


def solution(mesh):
    rows, weight, gain = P("fsdp", "ctx", None), P("fsdp", "ctx"), P("ctx")
    return jax.shard_map(
        local,
        mesh=mesh,
        in_specs=(rows, rows) + (weight,) * 7 + (gain, gain),
        out_specs=(rows, rows) + (weight,) * 7 + (gain, gain),
        check_vma=False,
    )
```

time: 917 us -> 485 us (0.53)
  waiting for transfers between devices: 600 us -> 0 us
  Pallas kernels: 0 us -> 289 us
  local copies, waits for them, and re-layouts: 161 us -> 83.2 us
  matrix products: 82.2 us -> 67.1 us
  between operations: 15.3 us -> 2.25 us
  other arithmetic: 49.6 us -> 36.8 us
    reduce_scatter x3 -> x0, waiting for transfers between devices: 363 us -> none  [scatter_rows(): lax.psum_scatter(merged, BOTH, scatter_dimension=0, tiled=True)[0]]
    pallas_call x0 -> x4, Pallas kernels: none -> 289 us  [the longest x2 164 us: scatter(): pl.pallas_call(functools.partial(scatter_kernel, depth, use_x, routes), o...]
    all_gather x4 -> x0, waiting for transfers between devices: 181 us -> none  [the longest x3 153 us: gather_rows(): gathered = lax.all_gather(packed, BOTH, axis=0, tiled=False)]
    unnamed x9 -> x0, waiting for transfers between devices: 56.6 us -> none
    unnamed x123 -> x157, local copies, waits for them, and re-layouts: 56.4 us -> 7.96 us
    another operation x31 -> x9, local copies, waits for them, and re-layouts: 75.5 us -> 27.4 us  [the longest x5 25.3 us: weight_terms(): jnp.stack([lax.dot_general(grads, values[:, i * part:(i + 1) * part], (((...]
    dot_general x42 -> x30, matrix products: 62.4 us -> 41.8 us  [the longest x10 18 us: backward_dot(): jnp.dot(grads, weights[i], preferred_element_type=jnp.float32)]
    slice x0 -> x11, local copies, waits for them, and re-layouts: none -> 17.9 us  [the longest x4 14.3 us: forward_dot(): weights[i]]
  transfers between devices with their start and end apart: 8 -> 0, of which waited for: 8 -> 0; matrix products, arithmetic and copies ran while one was open for 21% -> 0% of each run, Pallas kernels for 0% -> 0%
where the time goes in v1:
time: 485 us; the launch traced here: 479 us
  Pallas kernels  289 us (60%)
  local copies, waits for them, and re-layouts  83.2 us (17%)
  matrix products  67.1 us (14%)
  other arithmetic  36.8 us (8%)
    pallas_call x2, Pallas kernels, scatter(): pl.pallas_call(functools.partial(scatter_kernel, depth, use_x, routes), o...  164 us
    pallas_call x2, Pallas kernels, gather(): pl.pallas_call(functools.partial(gather_kernel, depth, use_x, routes), ou...  125 us
    another operation x5, local copies, waits for them, and re-layouts, weight_terms(): jnp.stack([lax.dot_general(grads, values[:, i * part:(i + 1) * part], (((...  25.3 us
    dot_general x10, matrix products, backward_dot(): jnp.dot(grads, weights[i], preferred_element_type=jnp.float32)  18 us
    slice x4, local copies, waits for them, and re-layouts, forward_dot(): weights[i]  14.3 us
    dot_general x10, matrix products, forward_dot(): lax.dot_general(values[:, i * part:(i + 1) * part], weights[i], (((1,), (...  14.3 us
    another operation x5, other arithmetic, weight_terms(): jnp.stack([lax.dot_general(grads, values[:, i * part:(i + 1) * part], (((...  12.3 us

profile of v1, /device:TPU:0, one launch (start us, length us, event | category | flops | bytes accessed | tf_op | source)
XLA Modules:
  0.0 478.6 jit_solution(6363528827310368215)
XLA Ops:
  0.6 1.0 reshape_reshape.26
  3.2 1.5 fusion.101.refs_0_
  4.8 1.5 pad.48.refs_1_
  6.2 1.6 pad.49.refs_4_
  7.8 100.6 %gather_weights.1 = (bf16[32,128,480]{2,1,0:T(8,128)(2,1)}, bf16[32,64,480]{2,1,0:T(8,128)(2,1)}, bf16[32,160,480]{2,1,0:T(8,128)(2,1)}, bf16[32,160,480]{2,1,0:T(8,128)(2,1)}, bf16[32,64,1280]{2,1,0:T(8,128)(2,1)}) custom-call(bf16[128,480]{1,0:T(8,128)(2,1)} %fusion.101.refs_0_, bf16[64,480]{1,0:T(8,128)(2,1)} %pad.48.refs_1_, bf16[160,480]{1,0:T(8,128)(2,1)} %bitcast.447, ...), custom_call_target="tpu_custom_call" | custom-call | tf_op jit(solution)/shard_map/gather_weights/pallas_call | solution.py:258
  108.4 3.3 convolution_bitcast_fusion
  111.7 3.1 convolution_bitcast_fusion.1
  114.8 6.0 %fusion.149 = (bf16[16,160,480]{2,1,0:T(8,128)(2,1)}, bf16[16,160,480]{2,1,0:T(8,128)(2,1)}, bf16[16,160,480]{2,1,0:T(8,128)(2,1)}, bf16[16,160,480]{2,1,0:T(8,128)(2,1)}) fusion(bf16[32,160,480]{2,1,0:T(8,128)(2,1)S(1)} %copy-done.13, bf16[32,160,480]{2,1,0:T(8,128)(2,1)} %get-tuple-element.90), kind=kLoop, calls=%fused_computation.234 | loop fusion | bytes 19660800 | tf_op jit(solution)/shard_map/slice | solution.py:536
  121.7 1.5 fusion.153
  124.5 3.9 fusion.151
  131.5 2.5 fusion.111
  134.1 1.8 convolution_add_fusion.2
  135.9 1.6 copy.87
  139.4 24.0 %gather_pairs.1 = bf16[16,128,640]{2,1,0:T(8,128)(2,1)S(1)} custom-call(bf16[128,640]{1,0:T(8,128)(2,1)} %maximum_bitcast_fusion.refs_0_), custom_call_target="tpu_custom_call" | custom-call | tf_op jit(solution)/shard_map/gather_pairs/pallas_call | solution.py:258
  163.4 2.5 fusion.152
  165.9 1.7 copy.52
  168.5 1.1 reshape_reshape.25
  169.7 6.8 %fusion.45 = (f32[5,3,128]{2,1,0:T(4,128)S(1)}, f32[5,2048,128,3]{2,1,3,0:T(8,128)}) fusion(pred[128,2048]{0,1:T(8,128)(4,1)S(1)} %copy-done.22, bf16[2048,5,64,1]{0,2,3,1:T(8,128)(2,1)S(1)} %bitcast.411, bf16[128,5,3,32]{0,3,2,1:T(8,128)(2,1)S(1)} %bitcast.432, bf16[128,5,3,32]{0,3,2,1:T(8,128)(2,1)S(1)} %bitcast.430), kind=kOutput, calls=%fused_computation.42 | convolution fusion | flops 515602560 | bytes 17554944 | tf_op jit(solution)/shard_map/sqgrd,skgd->sgrqk/dot_general | solution.py:666
  176.5 8.7 %fusion.43 = f32[5,3,128]{2,1,0:T(4,128)S(1)} fusion(f32[5,2048,128,3]{2,1,3,0:T(8,128)} %get-tuple-element.207, f32[5,3,128]{2,1,0:T(4,128)S(1)} %get-tuple-element.206, pred[128,2048]{0,1:T(8,128)(4,1)S(1)} %copy-done.22), kind=kLoop, calls=%fused_computation.40 | loop fusion | flops 15726720 | bytes 16006144 | tf_op jit(solution)/shard_map/reduce_sum | solution.py:675
  186.0 8.7 %fusion.154 = (bf16[1,5,3,128,64]{3,4,2,1,0:T(8,128)(2,1)S(1)}, f32[1,5,3,128,64]{3,4,2,1,0:T(8,128)}) fusion(f32[5,3,128]{2,1,0:T(4,128)S(1)} %fusion.43, bf16[2048,5,64,1]{0,2,3,1:T(8,128)(2,1)S(1)} %bitcast.429, f32[5,2048,128,3]{2,1,3,0:T(8,128)} %get-tuple-element.207, f32[5,3,128]{2,1,0:T(4,128)S(1)} %get-tuple-element.206, ...), kind=kOutput, calls=%fused_computation.239 | convolution fusion | flops 519290880 | bytes 18054144 | tf_op jit(solution)/shard_map/sgrqk,skgd->sgrqd/dot_general | solution.py:676
  198.3 3.0 fusion.119
  201.4 1.0 convolution_add_fusion
  203.1 1.0 fusion.121
  204.6 2.1 multiply_convert_fusion
  206.7 1.8 fusion.160
  208.5 1.8 fusion.159
  210.3 1.8 fusion.162
  212.2 1.1 fusion.161
  214.2 1.0 concatenate.164
  215.2 1.0 multiply_reduce_fusion
  218.5 1.6 fusion.80
  220.2 1.7 broadcast_in_dim.66.clone
  221.9 13.1 %while.14 = (s32[]{:T(128)}, f32[1,5,3,128,64]{3,4,2,1,0:T(8,128)S(1)}, bf16[1,2048,640]{2,1,0:T(8,128)(2,1)}, s32[]{:T(128)}, bf16[1,2048,640]{2,1,0:T(8,128)(2...) while((s32[]{:T(128)}, ...), condition=%wide.region_7.8_spmd.clone, body=%wide.region_6.7_spmd.clone.sunk | while | flops 643752576 | bytes 43806460 | solution.py:759
  221.9 1.3 constant_dynamic-slice_fusion.3
  223.4 2.6 fusion.223
  226.4 3.8 fusion.224
  230.8 2.1 fusion.226
  235.0 62.6 %scatter_pairs.1 = f32[128,640]{1,0:T(8,128)} custom-call(bf16[8,2,128,640]{3,2,1,0:T(8,128)(2,1)} %bitcast.402), custom_call_target="tpu_custom_call" | custom-call | tf_op jit(solution)/shard_map/scatter_pairs/pallas_call | solution.py:485
  297.6 1.0 slice.370
  301.7 3.0 fusion.142
  307.0 2.9 fusion.148
  310.0 1.0 fusion.93
  311.1 1.0 convolution_add_fusion.4
  313.1 2.6 fusion.76
  316.0 2.0 convolution_convert_fusion.6
  317.9 2.9 copy.86
  320.8 2.0 convolution_convert_fusion.7
  322.8 3.9 copy.85
  326.7 4.1 pad_maximum_fusion.4
  331.0 1.9 scatter.4
  334.0 2.8 copy.70
  338.4 2.7 pad_maximum_fusion.2
  341.1 7.9 %copy.71 = bf16[2,2560,480]{2,1,0:T(8,128)(2,1)} copy(bf16[2,2560,480]{1,2,0:T(8,128)(2,1)} %pad_maximum_fusion.2) | data formatting | bytes 9830400 | tf_op jit(solution)/shard_map/stack | solution.py:556
  350.5 2.6 pad_maximum_fusion.3
  353.1 8.0 %copy.72 = bf16[2,2560,480]{2,1,0:T(8,128)(2,1)} copy(bf16[2,2560,480]{1,2,0:T(8,128)(2,1)} %pad_maximum_fusion.3) | data formatting | bytes 9830400 | tf_op jit(solution)/shard_map/stack | solution.py:556
  362.8 2.8 pad_maximum_fusion.1
  365.5 101.8 %scatter_weights.1 = (f32[128,480]{1,0:T(8,128)}, f32[64,480]{1,0:T(8,128)}, f32[160,480]{1,0:T(8,128)}, f32[160,480]{1,0:T(8,128)}, f32[64,1280]{1,0:T(8,128)}) custom-call(bf16[16,2,128,480]{3,2,1,0:T(8,128)(2,1)} %bitcast.398, bf16[16,2,64,480]{3,2,1,0:T(8,128)(2,1)} %bitcast.408, bf16[16,2,160,480]{3,2,1,0:T(8,128)(2,1)} %bitcast.395, ...), custom_call_target="tpu_custom_call" | custom-call | tf_op jit(solution)/shard_map/scatter_weights/pallas_call | solution.py:485
  467.3 1.6 slice_bitcast_fusion.2
  468.9 1.5 slice_bitcast_fusion.3
  470.4 1.6 slice_bitcast_fusion.1
  471.9 1.7 slice_bitcast_fusion
  473.6 1.3 slice_bitcast_fusion.5
  475.0 1.7 copy.126
  476.7 1.7 copy.127
  (247 shorter events, 33.6 us)
Async XLA Ops:
  1.6 113.2 %copy-start.9 = (bf16[128,16,60]{0,2,1:T(8,128)(2,1)}, bf16[128,16,60]{0,2,1:T(8,128)(2,1)S(1)}, u32[]{:S(2)}) copy-start(bf16[128,16,60]{0,2,1:T(8,128)(2,1)S(1)} %reshape_reshape.26) | copy-start | bytes 737284
  108.4 6.4 %copy-start.13 = (bf16[32,160,480]{2,1,0:T(8,128)(2,1)S(1)}, bf16[32,160,480]{2,1,0:T(8,128)(2,1)}, u32[]{:S(2)}) copy-start(bf16[32,160,480]{2,1,0:T(8,128)(2,1)} %get-tuple-element.89) | copy-start | bytes 14745604
  114.8 6.0 %copy-start.8 = (bf16[1,128,960]{1,2,0:T(8,128)(2,1)S(1)}, bf16[1,128,960]{1,2,0:T(8,128)(2,1)}, u32[]{:S(2)}) copy-start(bf16[1,128,960]{1,2,0:T(8,128)(2,1)} %param.15) | copy-start | bytes 737284
  114.8 6.8 %copy-start.35 = (bf16[32,64,480]{2,1,0:T(8,128)(2,1)S(1)}, bf16[32,64,480]{2,1,0:T(8,128)(2,1)}, u32[]{:S(2)}) copy-start(bf16[32,64,480]{2,1,0:T(8,128)(2,1)} %get-tuple-element.88) | copy-start | bytes 5898244
  131.5 2.5 copy-start.25
  135.9 1.8 copy-start.77
  163.4 2.5 copy-start.1
  165.9 3.7 copy-start.54
  165.9 3.8 copy-start.22
  169.7 6.8 %copy-start.39 = (bf16[128,15,32]{0,2,1:T(8,128)(2,1)}, bf16[128,15,32]{0,2,1:T(8,128)(2,1)S(1)}, u32[]{:S(2)}) copy-start(bf16[128,15,32]{0,2,1:T(8,128)(2,1)S(1)} %get-tuple-element.191) | copy-start | bytes 368644
  169.7 6.8 %copy-start.41 = (bf16[128,15,32]{0,2,1:T(8,128)(2,1)}, bf16[128,15,32]{0,2,1:T(8,128)(2,1)S(1)}, u32[]{:S(2)}) copy-start(bf16[128,15,32]{0,2,1:T(8,128)(2,1)S(1)} %get-tuple-element.192) | copy-start | bytes 368644
  176.5 9.5 %copy-start.57 = (f32[5,3,128]{2,1,0:T(4,128)}, f32[5,3,128]{2,1,0:T(4,128)S(1)}, u32[]{:S(2)}) copy-start(f32[5,3,128]{2,1,0:T(4,128)S(1)} %get-tuple-element.206) | copy-start | bytes 23044
  176.5 8.7 %copy-start.12 = (bf16[1,2048,320]{2,1,0:T(8,128)(2,1)S(1)}, bf16[1,2048,320]{2,1,0:T(8,128)(2,1)}, u32[]{:S(2)}) copy-start(bf16[1,2048,320]{2,1,0:T(8,128)(2,1)} %get-tuple-element.183) | copy-start | bytes 3932164
  185.2 9.5 %copy-start.61 = (f32[5,3,128]{2,1,0:T(4,128)}, f32[5,3,128]{2,1,0:T(4,128)S(1)}, u32[]{:S(2)}) copy-start(f32[5,3,128]{2,1,0:T(4,128)S(1)} %fusion.43) | copy-start | bytes 23044
  186.0 8.8 %copy-start.21 = (bf16[16,64,480]{2,1,0:T(8,128)(2,1)S(1)}, bf16[16,64,480]{2,1,0:T(8,128)(2,1)}, u32[]{:S(2)}) copy-start(bf16[16,64,480]{2,1,0:T(8,128)(2,1)} %get-tuple-element.185) | copy-start | bytes 2949124
  186.0 9.5 %copy-start.20 = (bf16[16,64,480]{2,1,0:T(8,128)(2,1)S(1)}, bf16[16,64,480]{2,1,0:T(8,128)(2,1)}, u32[]{:S(2)}) copy-start(bf16[16,64,480]{2,1,0:T(8,128)(2,1)} %get-tuple-element.184) | copy-start | bytes 2949124
  196.0 2.0 copy-start.55
  197.1 4.2 copy-start.75
  198.0 3.4 copy-start.2
  198.1 4.3 copy-start.63
  198.1 4.3 copy-start.66
  198.3 5.8 %copy-start.14 = (bf16[128,960]{0,1:T(8,128)(2,1)}, bf16[128,960]{0,1:T(8,128)(2,1)S(1)}, u32[]{:S(2)}) copy-start(bf16[128,960]{0,1:T(8,128)(2,1)S(1)} %fusion.88) | copy-start | bytes 737284
  201.4 1.7 copy-start.4
  202.4 1.9 copy-start.5
  202.4 2.0 copy-start.50
  202.4 2.2 copy-start.51
  206.7 3.6 copy-start.6
  210.3 1.9 copy-start.3
  212.1 1.9 copy-start.30
  212.2 2.0 copy-start.28
  212.2 3.0 copy-start.18
  212.2 3.0 copy-start.56
  212.2 3.0 copy-start.67
  213.4 2.8 copy-start.76
  213.4 2.8 copy-start.10
  216.2 2.3 copy-start.52
  216.8 3.4 copy-start.43
  226.4 4.4 copy-start
  301.0 3.7 copy-start.19
  301.7 4.0 copy-start.37
  301.7 4.1 copy-start.17
  304.7 5.3 %copy-start.46 = (f32[128,480,1]{0,1,2:T(8,128)}, f32[128,480,1]{0,1,2:T(8,128)S(1)}, u32[]{:S(2)}) copy-start(f32[128,480,1]{0,1,2:T(8,128)S(1)} %fusion.142) | copy-start | bytes 737284
  304.7 1.9 copy-start.60
  304.7 1.9 copy-start.70
  304.8 2.3 copy-start.74
  305.7 4.3 copy-start.47
  307.0 3.0 copy-start.23
  311.0 2.1 copy-start.29
  311.0 2.1 copy-start.31
  311.0 2.1 copy-start.33
  311.0 2.1 copy-start.45
  311.0 2.1 copy-start.64
  311.0 2.1 copy-start.68
  311.0 2.1 copy-start.72
  312.2 3.4 copy-start.38
  312.3 3.7 copy-start.26
  317.9 2.9 copy-start.27
  326.7 4.2 copy-start.65
  326.7 6.2 %copy-start.44 = (bf16[128,16,60]{0,2,1:T(8,128)(2,1)S(1)}, bf16[128,16,60]{0,2,1:T(8,128)(2,1)}, u32[]{:S(2)}) copy-start(bf16[128,16,60]{0,2,1:T(8,128)(2,1)} %copy-done.43) | copy-start | bytes 737284
  326.7 6.2 %copy-start.49 = (bf16[1,5,3,128,64]{3,4,2,1,0:T(8,128)(2,1)S(1)}, bf16[1,5,3,128,64]{3,4,2,1,0:T(8,128)(2,1)}, u32[]{:S(2)}) copy-start(bf16[1,5,3,128,64]{3,4,2,1,0:T(8,128)(2,1)} %copy-done.48) | copy-start | bytes 737284
  334.0 2.8 copy-start.7
  334.0 2.8 copy-start.15
  353.1 8.0 %copy-start.11 = (bf16[128,16,60]{0,2,1:T(8,128)(2,1)S(1)}, bf16[128,16,60]{0,2,1:T(8,128)(2,1)}, u32[]{:S(2)}) copy-start(bf16[128,16,60]{0,2,1:T(8,128)(2,1)} %copy-done.9) | copy-start | bytes 737284
  353.1 8.0 %copy-start.24 = (bf16[128,2560]{1,0:T(8,128)(2,1)S(1)}, bf16[128,2560]{1,0:T(8,128)(2,1)}, u32[]{:S(2)}) copy-start(bf16[128,2560]{1,0:T(8,128)(2,1)} %get-tuple-element.181) | copy-start | bytes 1966084
  (14 other events, 14.4 us)

commit v2 on v1

--- a/solution.py
+++ b/solution.py
@@ -14,7 +14,7 @@
 EPSILON = 1e-05
 ROPE_THETA = 100000.0
 MESH = pl.DeviceIdType.MESH
-VMEM_LIMIT = 60 * 1024 * 1024
+VMEM_LIMIT = 67_000_000
 
 
 def tables(positions, head_size):
@@ -108,10 +108,11 @@
         body(low, False)
 
 
-def gather_kernel(depth, use_x, routes, *refs):
+def gather_kernel(depth, use_x, routes, work, *refs):
     count = len(routes)
-    ins, outs = refs[:count], refs[count : 2 * count]
-    recv, send_z, send_p, send_q, send_c, local_sem = refs[2 * count :]
+    ins, work_ins, refs = refs[:count], refs[count : count + work.ins], refs[count + work.ins :]
+    outs, work_outs, refs = refs[:count], refs[count : count + work.outs], refs[count + work.outs :]
+    recv, send_z, send_p, send_q, send_c, local_sem = refs
     place = Place(depth, use_x)
     place.barrier()
 
@@ -208,9 +209,18 @@
         both_sides(place, d - 1, from_p)
         both_sides(place, d - 1, functools.partial(from_q, 0))
         both_sides(place, d - 2, functools.partial(from_q, 1))
+
+        if work.count:
+
+            @pl.when(d - 1 < work.count)
+            def _():
+                work.body(d - 1, place.ctx, *work_ins, *work_outs)
+
         return carry
 
     lax.fori_loop(1, depth + 2, step, 0)
+    for item in range(depth + 1, work.count):
+        work.body(item, place.ctx, *work_ins, *work_outs)
 
     def finish(z0, carry):
         for k in range(count):
@@ -250,16 +260,24 @@
         mine.wait()
 
 
-def gather(arrays, routes, use_x, collective_id, name):
+class Work:
+    def __init__(self, count=0, body=None, arrays=(), shapes=()):
+        self.count, self.body, self.arrays, self.shapes = count, body, arrays, list(shapes)
+        self.ins, self.outs = len(arrays), len(self.shapes)
+
+
+def gather(arrays, routes, use_x, collective_id, name, work=Work()):
     depth = lax.axis_size("ctx") // 4
     pieces = (4 if use_x else 2) * depth
     count = len(arrays)
     dma = pltpu.SemaphoreType.DMA
     return pl.pallas_call(
-        functools.partial(gather_kernel, depth, use_x, routes),
-        out_shape=[jax.ShapeDtypeStruct((2 * pieces, *a.shape), a.dtype) for a in arrays],
-        in_specs=[pl.BlockSpec(memory_space=pltpu.VMEM)] * count,
-        out_specs=[pl.BlockSpec(memory_space=pl.ANY)] * count,
+        functools.partial(gather_kernel, depth, use_x, routes, work),
+        out_shape=[jax.ShapeDtypeStruct((2 * pieces, *a.shape), a.dtype) for a in arrays]
+        + work.shapes,
+        in_specs=[pl.BlockSpec(memory_space=pltpu.VMEM)] * (count + work.ins),
+        out_specs=[pl.BlockSpec(memory_space=pl.ANY)] * count
+        + [pl.BlockSpec(memory_space=pltpu.VMEM)] * work.outs,
         scratch_shapes=[
             dma((count, 2 * pieces)),
             dma((count, 2, depth)),
@@ -272,7 +290,7 @@
             collective_id=collective_id, has_side_effects=True, vmem_limit_bytes=VMEM_LIMIT
         ),
         name=name,
-    )(*arrays)
+    )(*arrays, *work.arrays)
 
 
 def add_up(dst, sources, rows):
@@ -289,13 +307,12 @@
     lax.fori_loop(0, rows // block, body, 0)
 
 
-def scatter_kernel(depth, use_x, routes, *refs):
+def scatter_kernel(depth, use_x, routes, work, *refs):
     count = len(routes)
-    ins, outs = refs[:count], refs[count : 2 * count]
-    own, part, land_q, land_p, land_z = (
-        refs[(2 + i) * count : (3 + i) * count] for i in range(5)
-    )
-    load_sem, c_send, c_recv, q_send, q_recv, p_send, p_recv, z_send, z_recv = refs[7 * count :]
+    ins, work_ins, refs = refs[:count], refs[count : count + work.ins], refs[count + work.ins :]
+    outs, work_outs, refs = refs[:count], refs[count : count + work.outs], refs[count + work.outs :]
+    own, part, land_q, land_p, land_z = (refs[i * count : (1 + i) * count] for i in range(5))
+    load_sem, c_send, c_recv, q_send, q_recv, p_send, p_recv, z_send, z_recv = refs[5 * count :]
     place = Place(depth, use_x)
     pieces = (4 if use_x else 2) * depth
     rows = [out.shape[0] for out in outs]
@@ -419,6 +436,12 @@
 
         both_sides(place, depth - 1 - s, leaf)
 
+        if work.count:
+
+            @pl.when(s < work.count)
+            def _():
+                work.body(s, place.ctx, *work_ins, *work_outs)
+
         @pl.when(s < depth + 1)
         def _():
             both_sides(place, depth - s, middle)
@@ -446,6 +469,8 @@
         return carry
 
     lax.fori_loop(0, depth + 2, step, 0)
+    for item in range(depth + 2, work.count):
+        work.body(item, place.ctx, *work_ins, *work_outs)
 
     def finish(z0, carry):
         for k in range(count):
@@ -474,7 +499,7 @@
     lax.fori_loop(0, pieces, finish_partner, 0)
 
 
-def scatter(arrays, routes, use_x, collective_id, name):
+def scatter(arrays, routes, use_x, collective_id, name, work=Work()):
     depth = lax.axis_size("ctx") // 4
     pieces = (4 if use_x else 2) * depth
     count = len(arrays)
@@ -483,10 +508,11 @@
     pairs = [a.reshape(pieces, 2, *s) for a, s in zip(arrays, shapes)]
     bf16 = jnp.bfloat16
     return pl.pallas_call(
-        functools.partial(scatter_kernel, depth, use_x, routes),
-        out_shape=[jax.ShapeDtypeStruct(s, jnp.float32) for s in shapes],
-        in_specs=[pl.BlockSpec(memory_space=pl.ANY)] * count,
-        out_specs=[pl.BlockSpec(memory_space=pltpu.VMEM)] * count,
+        functools.partial(scatter_kernel, depth, use_x, routes, work),
+        out_shape=[jax.ShapeDtypeStruct(s, jnp.float32) for s in shapes] + work.shapes,
+        in_specs=[pl.BlockSpec(memory_space=pl.ANY)] * count
+        + [pl.BlockSpec(memory_space=pltpu.VMEM)] * work.ins,
+        out_specs=[pl.BlockSpec(memory_space=pltpu.VMEM)] * (count + work.outs),
         scratch_shapes=[pltpu.VMEM((pieces, *s), bf16) for s in shapes]
         + [pltpu.VMEM((pieces, *s), bf16) for s in shapes]
         + [pltpu.VMEM((2, depth, *s), bf16) for s in shapes]
@@ -507,7 +533,7 @@
             collective_id=collective_id, has_side_effects=True, vmem_limit_bytes=VMEM_LIMIT
         ),
         name=name,
-    )(*pairs)
+    )(*pairs, *work.arrays)
 
 
 def padded(rows, multiple=16):
@@ -519,7 +545,7 @@
 
 
 XY, YX, ONLY_Y = ("x", "y"), ("y", "x"), (None, "y")
-WEIGHT_ROUTES = (YX, YX, XY, XY, YX)
+REST_ROUTES = (YX, XY, XY, YX)
 
 
 def halves(values, split_count):
@@ -551,19 +577,119 @@
     )
 
 
+def terms_kernel(grads, values, out):
+    for i in range(values.shape[0]):
+        out[i] = lax.dot_general(
+            grads[...], values[i], (((0,), (0,)), ((), ())), preferred_element_type=jnp.float32
+        ).astype(out.dtype)
+
+
 def weight_terms(grads, values, split_count):
-    part = values.shape[1] // split_count
-    return jnp.stack(
-        [
-            lax.dot_general(
-                grads,
-                values[:, i * part : (i + 1) * part],
-                (((0,), (0,)), ((), ())),
-                preferred_element_type=jnp.float32,
-            ).astype(jnp.bfloat16)
-            for i in range(split_count)
-        ]
-    )
+    rows, width = grads.shape
+    values = jnp.transpose(halves(values, split_count), (1, 0, 2))
+    block = next((b for b in (512, 256, 128) if width % b == 0), width)
+    part = values.shape[2]
+    return pl.pallas_call(
+        terms_kernel,
+        out_shape=jax.ShapeDtypeStruct((split_count, width, part), jnp.bfloat16),
+        grid=(width // block,),
+        in_specs=[
+            pl.BlockSpec((rows, block), lambda i: (0, i)),
+            pl.BlockSpec(values.shape, lambda i: (0, 0, 0)),
+        ],
+        out_specs=pl.BlockSpec((split_count, block, part), lambda i: (0, i, 0)),
+        compiler_params=pltpu.CompilerParams(vmem_limit_bytes=VMEM_LIMIT),
+        cost_estimate=pl.CostEstimate(
+            flops=2 * rows * width * part * split_count,
+            bytes_accessed=2 * width * part * split_count,
+            transcendentals=0,
+        ),
+        name="weight_terms",
+    )(grads, values)
+
+
+PIECES_PER_BLOCK = 4
+
+
+def block_scores(step, ctx, kv_ref, group, query):
+    _, _, block_len, width = kv_ref.shape
+    span = pl.ds(step * PIECES_PER_BLOCK, PIECES_PER_BLOCK)
+    kv = kv_ref[span, group].reshape(PIECES_PER_BLOCK * block_len, width)
+    scores = (
+        lax.dot_general(kv, query, (((1,), (1,)), ((), ())), preferred_element_type=jnp.float32)
+        * 0.125
+    )
+    key_pos = step * kv.shape[0] + lax.broadcasted_iota(jnp.int32, scores.shape, 0)
+    query_pos = ctx * block_len + lax.rem(
+        lax.broadcasted_iota(jnp.int32, scores.shape, 1), block_len
+    )
+    return kv, scores, key_pos <= query_pos
+
+
+def attend_body(group, ctx, kv_ref, query_ref, out_ref, logsum_ref):
+    query = query_ref[group]
+    rows, width = query.shape
+
+    def body(step, carry):
+        peak, total, acc = carry
+        kv, scores, allowed = block_scores(step, ctx, kv_ref, group, query)
+        scores = jnp.where(allowed, scores, -jnp.inf)
+        new_peak = jnp.maximum(peak, jnp.max(scores, axis=0, keepdims=True))
+        terms = jnp.exp(scores - new_peak)
+        shrink = jnp.exp(peak - new_peak)
+        total = total * shrink + jnp.sum(terms, axis=0, keepdims=True)
+        acc = acc * shrink + lax.dot_general(
+            kv,
+            terms.astype(jnp.bfloat16),
+            (((0,), (0,)), ((), ())),
+            preferred_element_type=jnp.float32,
+        )
+        return new_peak, total, acc
+
+    peak, total, acc = lax.fori_loop(
+        0,
+        ctx // PIECES_PER_BLOCK + 1,
+        body,
+        (
+            jnp.full((1, rows), -jnp.inf, jnp.float32),
+            jnp.zeros((1, rows), jnp.float32),
+            jnp.zeros((width, rows), jnp.float32),
+        ),
+    )
+    out_ref[group] = acc / total
+    logsum_ref[group] = peak + jnp.log(total)
+
+
+def retrace_body(group, ctx, kv_ref, query_ref, grad_ref, logsum_ref, delta_ref, dq_ref, dkv_ref):
+    query, grad = query_ref[group], grad_ref[group]
+    logsum, delta = logsum_ref[group], delta_ref[group]
+    blocks, _, block_len, width = kv_ref.shape
+    needed = ctx // PIECES_PER_BLOCK + 1
+
+    def body(step, dq):
+        kv, scores, allowed = block_scores(step, ctx, kv_ref, group, query)
+        probs = jnp.where(allowed, jnp.exp(scores - logsum), 0.0)
+        grad_probs = lax.dot_general(
+            kv, grad, (((1,), (1,)), ((), ())), preferred_element_type=jnp.float32
+        )
+        grad_scores = (probs * (grad_probs - delta) * 0.125).astype(jnp.bfloat16)
+        dkv = jnp.dot(
+            probs.astype(jnp.bfloat16), grad, preferred_element_type=jnp.float32
+        ) + jnp.dot(grad_scores, query, preferred_element_type=jnp.float32)
+        span = pl.ds(step * PIECES_PER_BLOCK, PIECES_PER_BLOCK)
+        dkv_ref[span, group] = dkv.astype(jnp.bfloat16).reshape(PIECES_PER_BLOCK, block_len, width)
+        return dq + lax.dot_general(
+            grad_scores, kv, (((0,), (0,)), ((), ())), preferred_element_type=jnp.float32
+        )
+
+    dq_ref[group] = lax.fori_loop(0, needed, body, jnp.zeros(query.shape, jnp.float32))
+
+    def clear(step, carry):
+        span = pl.ds(step * PIECES_PER_BLOCK, PIECES_PER_BLOCK)
+        dkv_ref[span, group] = jnp.zeros((PIECES_PER_BLOCK, block_len, width), jnp.bfloat16)
+        return carry
+
+    lax.fori_loop(needed, blocks // PIECES_PER_BLOCK, clear, 0)
 
 
 def local(
@@ -574,8 +700,6 @@
     split_count = lax.axis_size("fsdp")
     cycle_size = lax.axis_size("ctx")
     cycle_index = lax.axis_index("ctx")
-    length = block_len * cycle_size
-    key_block = min(512, length)
     groups = KV_HEADS
     head_size = HEAD
     repeat_count = HEADS // KV_HEADS
@@ -584,7 +708,6 @@
     cosine, sine_table = tables(positions, head_size)
     cosine = jnp.tile(cosine, (seq_count, 1))
     sine_table = jnp.tile(sine_table, (seq_count, 1))
-    needed = (cycle_index * block_len + block_len + key_block - 1) // key_block
     wide_q, wide_k, wide_v = w_query.shape[1], w_key.shape[1], w_value.shape[1]
     wide_o, wide_g, wide_u = w_out.shape[1], w_gate.shape[1], w_up.shape[1]
     wide_d = w_down.shape[1]
@@ -612,25 +735,15 @@
         ],
         axis=0,
     )
-    first, out_w, gate_w, up_w, down_w = gather(
-        [
-            first_piece,
-            pad_rows(w_out.T, pad_o),
-            pad_rows(w_gate.T, pad_g),
-            pad_rows(w_up.T, pad_u),
-            pad_rows(w_down.T, pad_d),
-        ],
-        WEIGHT_ROUTES,
-        True,
-        0,
-        "gather_weights",
-    )
+    half = padded(first_piece.shape[0] // 2)
+    first_a, first_b = gather(
+        [first_piece[:half], first_piece[half:]], (YX, XY), True, 0, "gather_first"
+    )
+    first = jnp.concatenate([first_a, first_b], axis=1)
     gain_rows = first[:cycle_size, pad_q + wide_k, : 2 * gain_size]
     gain_first = gain_rows[:, :gain_size].reshape(-1).astype(jnp.float32)
     gain_second = gain_rows[:, gain_size:].reshape(-1).astype(jnp.float32)
-    first, out_w, gate_w, up_w, down_w = (
-        w.reshape(split_count, -1, w.shape[-1]) for w in (first, out_w, gate_w, up_w, down_w)
-    )
+    first = first.reshape(split_count, -1, part_width)
 
     resid1 = inputs.reshape(row_count, model_width).astype(jnp.float32)
     normal1 = normed(resid1, gain_first).astype(jnp.bfloat16)
@@ -638,51 +751,54 @@
     query_raw = open_up(raw, wide_q, 0, pad_q).reshape(row_count, HEADS, head_size)
     query_rot = rotate(query_raw, cosine, sine_table).astype(jnp.bfloat16)
     key_raw = open_up(raw, wide_k, pad_q, pad_k).reshape(row_count, groups, head_size)
-    key_rows = (
-        rotate(key_raw, cosine, sine_table)
-        .astype(jnp.bfloat16)
-        .reshape(seq_count, block_len, kv_width)
-    )
-    value_rows = (
-        open_up(raw, wide_v, pad_q + pad_k, pad_v)
-        .astype(jnp.bfloat16)
-        .reshape(seq_count, block_len, kv_width)
-    )
-    query_grouped = query_rot.reshape(seq_count, block_len, groups, repeat_count, head_size)
+    key_rows = rotate(key_raw, cosine, sine_table).astype(jnp.bfloat16)
+    value_rows = open_up(raw, wide_v, pad_q + pad_k, pad_v).astype(jnp.bfloat16)
+    value_rows = value_rows.reshape(row_count, groups, head_size)
+    pair_rows = jnp.transpose(jnp.concatenate([key_rows, value_rows], axis=-1), (1, 0, 2))
     (pair_all,) = gather(
-        [jnp.concatenate([key_rows, value_rows], axis=-1).reshape(row_count, 2 * kv_width)],
+        [pair_rows.reshape(groups * row_count, 2 * head_size)],
         (ONLY_Y,),
         False,
         1,
         "gather_pairs",
     )
-    pair_all = pair_all.reshape(cycle_size, seq_count, block_len, 2 * kv_width)
-    pair_all = jnp.transpose(pair_all, (1, 0, 2, 3)).reshape(seq_count, length, 2 * kv_width)
-    keys_all = pair_all[..., :kv_width]
-    values_all = pair_all[..., kv_width:]
-    key_heads = keys_all.reshape(seq_count, length, groups, head_size)
-    value_heads = values_all.reshape(seq_count, length, groups, head_size)
-    scores = (
-        jnp.einsum(
-            "sqgrd,skgd->sgrqk", query_grouped, key_heads, preferred_element_type=jnp.float32
-        )
-        * 0.125
-    )
-    allowed = jnp.arange(length, dtype=jnp.int32)[None, :] <= positions[:, None]
-    scores = jnp.where(allowed, scores, -jnp.inf)
-    new_peak = jnp.max(scores, axis=-1)
-    exp_terms = jnp.exp(scores - new_peak[..., None])
-    denom_run = jnp.sum(exp_terms, axis=-1)
-    running = jnp.einsum(
-        "sgrqk,skgd->sgrqd",
-        exp_terms.astype(jnp.bfloat16),
-        value_heads,
-        preferred_element_type=jnp.float32,
-    )
-    attended_wide = running / denom_run[..., None]
-    attended = jnp.transpose(attended_wide, (0, 3, 1, 2, 4)).astype(jnp.bfloat16)
-    logsum = new_peak + jnp.log(denom_run)
-    attended_rows = attended.reshape(row_count, HEADS * head_size)
+    pair_all = pair_all.reshape(cycle_size, groups, row_count, 2 * head_size)
+
+    def by_group(values):
+        values = values.reshape(row_count, groups, repeat_count, head_size)
+        return jnp.transpose(values, (1, 2, 0, 3)).reshape(groups, repeat_count * row_count, head_size)
+
+    query_grouped = jnp.pad(by_group(query_rot), ((0, 0), (0, 0), (0, head_size)))
+    width = repeat_count * row_count
+    out_w, gate_w, up_w, down_w, attended_turned, logsum = gather(
+        [
+            pad_rows(w_out.T, pad_o),
+            pad_rows(w_gate.T, pad_g),
+            pad_rows(w_up.T, pad_u),
+            pad_rows(w_down.T, pad_d),
+        ],
+        REST_ROUTES,
+        True,
+        4,
+        "gather_rest_attend",
+        Work(
+            groups,
+            attend_body,
+            [pair_all, query_grouped],
+            [
+                jax.ShapeDtypeStruct((groups, 2 * head_size, width), jnp.float32),
+                jax.ShapeDtypeStruct((groups, 1, width), jnp.float32),
+            ],
+        ),
+    )
+    out_w, gate_w, up_w, down_w = (
+        w.reshape(split_count, -1, w.shape[-1]) for w in (out_w, gate_w, up_w, down_w)
+    )
+    attended_wide = jnp.transpose(
+        attended_turned[:, head_size:].reshape(groups, head_size, repeat_count, row_count),
+        (3, 0, 2, 1),
+    )
+    attended_rows = attended_wide.astype(jnp.bfloat16).reshape(row_count, HEADS * head_size)
     resid2 = resid1 + open_up(forward_dot(attended_rows, out_w), wide_o, 0, pad_o)
     normal2 = normed(resid2, gain_second).astype(jnp.bfloat16)
     gate_act = forward_dot(normal2, gate_w)
@@ -711,71 +827,56 @@
     terms_gate = weight_terms(grad_gate, normal2, split_count)
     terms_up = weight_terms(grad_up, normal2, split_count)
     grad_attended = backward_dot(grad_branch, out_w).astype(jnp.bfloat16)
-    grad_grouped = grad_attended.reshape(seq_count, block_len, groups, repeat_count, head_size)
     row_delta = jnp.sum(
-        jnp.transpose(grad_grouped, (0, 2, 3, 1, 4)).astype(jnp.float32) * attended_wide, axis=-1
-    )
-
-    def retrace(step_index, loop_state):
-        grad_query_acc, grad_pair_all = loop_state
-        key_start = step_index * key_block
-        pair = lax.dynamic_slice_in_dim(pair_all, key_start, key_block, 1)
-        key_heads = pair[..., :kv_width].reshape(seq_count, key_block, groups, head_size)
-        value_heads = pair[..., kv_width:].reshape(seq_count, key_block, groups, head_size)
-        scores = (
-            jnp.einsum(
-                "sqgrd,skgd->sgrqk", query_grouped, key_heads, preferred_element_type=jnp.float32
-            )
-            * 0.125
-        )
-        allowed = (key_start + jnp.arange(key_block, dtype=jnp.int32))[None, :] <= positions[
-            :, None
-        ]
-        prob_full = jnp.where(
-            allowed, jnp.exp(jnp.where(allowed, scores, -jnp.inf) - logsum[..., None]), 0.0
-        )
-        grad_probs = jnp.einsum(
-            "sqgrd,skgd->sgrqk", grad_grouped, value_heads, preferred_element_type=jnp.float32
-        )
-        grad_scores = (prob_full * (grad_probs - row_delta[..., None]) * 0.125).astype(jnp.bfloat16)
-        prob_low = prob_full.astype(jnp.bfloat16)
-        value_term = jnp.einsum(
-            "sgrqk,sqgrd->skgd", prob_low, grad_grouped, preferred_element_type=jnp.float32
-        ).reshape(seq_count, key_block, kv_width)
-        key_term = jnp.einsum(
-            "sgrqk,sqgrd->skgd", grad_scores, query_grouped, preferred_element_type=jnp.float32
-        ).reshape(seq_count, key_block, kv_width)
-        grad_query_acc = grad_query_acc + jnp.einsum(
-            "sgrqk,skgd->sgrqd", grad_scores, key_heads, preferred_element_type=jnp.float32
-        )
-        pair_term = jnp.concatenate([key_term, value_term], axis=-1).astype(jnp.bfloat16)
-        grad_pair_all = lax.dynamic_update_slice_in_dim(grad_pair_all, pair_term, key_start, 1)
-        return (grad_query_acc, grad_pair_all)
-
-    back_state = (
-        jnp.zeros((seq_count, groups, repeat_count, block_len, head_size), jnp.float32),
-        jnp.zeros((seq_count, length, 2 * kv_width), jnp.bfloat16),
-    )
-    grad_query_acc, grad_pair_all = lax.fori_loop(0, needed, retrace, back_state)
-    grad_pair_all = grad_pair_all.reshape(seq_count, cycle_size, block_len, 2 * kv_width)
-    grad_pair_all = jnp.transpose(grad_pair_all, (1, 0, 2, 3)).reshape(
-        cycle_size, row_count, 2 * kv_width
-    )
-    (grad_pair_own,) = scatter([grad_pair_all], (ONLY_Y,), False, 2, "scatter_pairs")
-    grad_query_rows = jnp.transpose(grad_query_acc, (0, 3, 1, 2, 4)).reshape(
-        row_count, HEADS, head_size
-    )
+        grad_attended.astype(jnp.float32).reshape(attended_wide.shape) * attended_wide, axis=-1
+    )
+    row_delta = jnp.transpose(row_delta, (1, 2, 0)).reshape(groups, 1, width)
+    grad_grouped = jnp.pad(by_group(grad_attended), ((0, 0), (0, 0), (head_size, 0)))
+
+    def pieces_of(terms):
+        return terms.reshape(split_count * cycle_size, -1, terms.shape[-1])
+
+    sum_out, sum_gate, sum_up, sum_down, grad_query_acc, grad_pair_all = scatter(
+        [pieces_of(t) for t in (terms_out, terms_gate, terms_up, terms_down)],
+        REST_ROUTES,
+        True,
+        3,
+        "scatter_rest_retrace",
+        Work(
+            groups,
+            retrace_body,
+            [pair_all, query_grouped, grad_grouped, logsum, row_delta],
+            [
+                jax.ShapeDtypeStruct(query_grouped.shape, jnp.float32),
+                jax.ShapeDtypeStruct(pair_all.shape, jnp.bfloat16),
+            ],
+        ),
+    )
+    (grad_pair_own,) = scatter(
+        [grad_pair_all.reshape(cycle_size, groups * row_count, 2 * head_size)],
+        (ONLY_Y,),
+        False,
+        2,
+        "scatter_pairs",
+    )
+    grad_pair_own = jnp.transpose(
+        grad_pair_own.reshape(groups, row_count, 2 * head_size), (1, 0, 2)
+    )
+    grad_query_rows = jnp.transpose(
+        grad_query_acc[..., :head_size].reshape(groups, repeat_count, row_count, head_size),
+        (2, 0, 1, 3),
+    ).reshape(row_count, HEADS, head_size)
     grad_query = (
         unrotate(grad_query_rows, cosine, sine_table)
         .reshape(row_count, HEADS * head_size)
         .astype(jnp.bfloat16)
     )
     grad_keys = (
-        unrotate(grad_pair_own[..., :kv_width].reshape(row_count, groups, head_size), cosine, sine_table)
+        unrotate(grad_pair_own[..., :head_size], cosine, sine_table)
         .reshape(row_count, kv_width)
         .astype(jnp.bfloat16)
     )
-    grad_values = grad_pair_own[..., kv_width:].astype(jnp.bfloat16)
+    grad_values = grad_pair_own[..., head_size:].astype(jnp.bfloat16).reshape(row_count, kv_width)
 
     def shaped(values, wide, pad):
         pieces = values.reshape(row_count, cycle_size, wide)
@@ -802,15 +903,9 @@
     terms_first = terms_first.reshape(split_count, cycle_size, -1, part_width)
     terms_first = terms_first.at[:, :, pad_q + wide_k, : 2 * gain_size].set(gain_terms[None])
 
-    def pieces_of(terms):
-        return terms.reshape(split_count * cycle_size, -1, terms.shape[-1])
-
-    sum_first, sum_out, sum_gate, sum_up, sum_down = scatter(
-        [pieces_of(t) for t in (terms_first, terms_out, terms_gate, terms_up, terms_down)],
-        WEIGHT_ROUTES,
-        True,
-        3,
-        "scatter_weights",
+    terms_first = terms_first.reshape(split_count * cycle_size, -1, part_width)
+    sum_first = jnp.concatenate(
+        scatter([terms_first[:, :half], terms_first[:, half:]], (YX, XY), True, 5, "scatter_first")
     )
     start_k, start_v = pad_q, pad_q + pad_k
     gain_sums = sum_first[pad_q + wide_k]

time: 485 us -> 430 us (0.89); the launches traced: 479 us -> 428 us
  matrix products: 67.1 us -> 33.6 us
  Pallas kernels: 289 us -> 312 us
  local copies, waits for them, and re-layouts: 83.2 us -> 62.1 us
  other arithmetic: 36.8 us -> 19 us
    dot_general x17 -> x0, matrix products: 34.9 us -> none  [the longest x10 9.54 us: weight_terms(): lax.dot_general(grads, values[:, i * part:(i + 1) * part], (((0,), (0,)),...]
    pallas_call x4 -> x11, Pallas kernels: 289 us -> 312 us  [the longest x3 149 us: scatter(): pl.pallas_call(functools.partial(scatter_kernel, depth, use_x, routes, wo...]
    another operation x6 -> x5, local copies, waits for them, and re-layouts: 25.4 us -> 3.22 us  [the longest x2 2.88 us: halves(): values.reshape(values.shape[0], split_count, values.shape[1] // split_count)]
    another operation x9 -> x4, other arithmetic: 12.5 us -> 0.96 us  [the longest x5 12.3 us: weight_terms(): jnp.stack([lax.dot_general(grads, values[:, i * part:(i + 1) * part], (((...]
    reduce_sum x2 -> x1, other arithmetic: 10.3 us -> 0.08 us  [local(): jnp.sum(grad_attended.astype(jnp.float32).reshape(attended_wide.shape) *...]
    concatenate x4, local copies, waits for them, and re-layouts: 1.02 us -> 6.25 us  [backward_dot(): jnp.concatenate([jnp.dot(grads, weights[i], preferred_element_type=jnp.fl...]
where the time goes in v2:
time: 430 us; the launch traced here: 428 us
  Pallas kernels  312 us (73%)
  local copies, waits for them, and re-layouts  62.1 us (14%)
  matrix products  33.6 us (8%)
  other arithmetic  19 us (4%)
    pallas_call x3, Pallas kernels, scatter(): pl.pallas_call(functools.partial(scatter_kernel, depth, use_x, routes, wo...  149 us
    pallas_call x3, Pallas kernels, gather(): pl.pallas_call(functools.partial(gather_kernel, depth, use_x, routes, wor...  139 us
    pallas_call x5, Pallas kernels, weight_terms(): pl.pallas_call(terms_kernel, out_shape=jax.ShapeDtypeStruct((split_count,...  23.3 us
    dot_general x10, matrix products, backward_dot(): jnp.dot(grads, weights[i], preferred_element_type=jnp.float32)  21.2 us
    dot_general x10, matrix products, forward_dot(): lax.dot_general(values[:, i * part:(i + 1) * part], weights[i], (((1,), (...  12.4 us
    slice x4, local copies, waits for them, and re-layouts, forward_dot(): weights[i]  10.9 us

profile of v2, /device:TPU:0, one launch (start us, length us, event | category | flops | bytes accessed | tf_op | source)
XLA Modules:
  0.0 428.5 jit_solution(7920898548993110748)
XLA Ops:
  2.2 1.4 fusion.46.refs_1_
  3.5 1.5 pad.54.refs_0_
  5.0 28.9 %gather_first.1 = (bf16[32,64,480]{2,1,0:T(8,128)(2,1)}, bf16[32,64,480]{2,1,0:T(8,128)(2,1)}) custom-call(bf16[64,480]{1,0:T(8,128)(2,1)} %pad.54.refs_0_, bf16[64,480]{1,0:T(8,128)(2,1)} %fusion.46.refs_1_), custom_call_target="tpu_custom_call" | custom-call | tf_op jit(solution)/shard_map/gather_first/pallas_call | solution.py:274
  34.0 0.9 slice.205
  35.1 1.1 fusion.23
  36.2 1.1 fusion.21
  37.3 1.7 constant_dynamic-update-slice_fusion.1
  39.7 1.6 copy-done.8
  42.1 0.8 convolution_add_fusion.2
  45.2 24.3 %gather_pairs.1 = bf16[16,640,128]{2,1,0:T(8,128)(2,1)} custom-call(bf16[640,128]{1,0:T(8,128)(2,1)} %bitcast.259), custom_call_target="tpu_custom_call" | custom-call | tf_op jit(solution)/shard_map/gather_pairs/pallas_call | solution.py:274
  69.5 1.1 slice.262
  72.3 0.9 pad.58.refs_5_
  74.5 86.0 %gather_rest_attend.1 = (bf16[32,64,480]{2,1,0:T(8,128)(2,1)}, bf16[32,160,480]{2,1,0:T(8,128)(2,1)}, bf16[32,160,480]{2,1,0:T(8,128)(2,1)}, bf16[32,64,1280]{2,...) custom-call(bf16[64,480]{1,0:T(8,128)(2,1)} %pad.52.refs_0_, bf16[160,480]{1,0:T(8,128)(2,1)} %bitcast.264, ...), custom_call_target="tpu_custom_call" | custom-call | tf_op jit(solution)/shard_map/gather_rest_attend/pallas_call | solution.py:274
  160.6 1.8 fusion.73
  163.9 0.9 multiply_reduce_fusion.2
  165.2 5.7 %fusion.69 = (bf16[16,160,480]{2,1,0:T(8,128)(2,1)}, bf16[16,160,480]{2,1,0:T(8,128)(2,1)S(1)}, bf16[16,160,480]{2,1,0:T(8,128)(2,1)S(1)}, bf16[16,160,480]{2,1,0:T(8,128)(2,1)S(1)}) fusion(bf16[32,160,480]{2,1,0:T(8,128)(2,1)} %get-tuple-element.43, bf16[32,160,480]{2,1,0:T(8,128)(2,1)} %get-tuple-element.44), kind=kLoop, calls=%fused_computation.149 | loop fusion | bytes 19660800 | tf_op jit(solution)/shard_map/slice | solution.py:562
  171.0 2.6 fusion.44
  173.5 1.0 fusion.42
  174.6 2.1 convolution_add_fusion
  176.7 1.7 reshape_reshape.32
  178.4 2.5 convolution_bitcast_fusion.1
  180.9 2.4 convolution_bitcast_fusion
  183.4 2.3 multiply_convert_fusion
  185.7 0.8 copy-done.14
  186.6 1.8 fusion.80
  188.4 1.7 concatenate.138
  190.0 2.9 fusion.81
  193.0 1.8 concatenate.139
  194.8 3.8 fusion.78
  198.5 1.7 concatenate.135
  200.2 2.9 fusion.79
  203.1 1.1 concatenate.136
  204.2 2.2 multiply_reduce_fusion
  207.1 1.7 fusion.7
  210.8 1.0 pad.61.refs_6_
  213.9 5.5 %weight_terms.7 = bf16[2,2560,480]{2,1,0:T(8,128)(2,1)} custom-call(bf16[128,2560]{1,0:T(8,128)(2,1)} %copy-done.14, bf16[2,128,480]{2,1,0:T(8,128)(2,1)} %fusion.31.values), custom_call_target="tpu_custom_call" | custom-call | flops 629145600 | bytes 4915200 | tf_op jit(solution)/shard_map/weight_terms/pallas_call | solution.py:592
  219.4 5.5 %weight_terms.6 = bf16[2,2560,480]{2,1,0:T(8,128)(2,1)} custom-call(bf16[128,2560]{1,0:T(8,128)(2,1)} %get-tuple-element.72.grads, bf16[2,128,480]{2,1,0:T(8,128)(2,1)} %fusion.31.values), custom_call_target="tpu_custom_call" | custom-call | flops 629145600 | bytes 4915200 | tf_op jit(solution)/shard_map/weight_terms/pallas_call | solution.py:592
  224.9 1.4 copy.73
  226.4 1.1 copy.74
  227.5 0.9 copy.75.grads
  228.4 4.5 %weight_terms.8 = bf16[2,1024,1280]{2,1,0:T(8,128)(2,1)} custom-call(bf16[128,1024]{1,0:T(8,128)(2,1)} %copy.75.grads, bf16[2,128,1280]{2,1,0:T(8,128)(2,1)} %bitcast.231), custom_call_target="tpu_custom_call" | custom-call | flops 671088640 | bytes 5242880 | tf_op jit(solution)/shard_map/weight_terms/pallas_call | solution.py:592
  232.8 1.0 pad.60
  233.8 0.9 copy.71.grads
  234.7 1.8 copy.70
  236.5 2.9 weight_terms.5
  239.4 95.6 %scatter_rest_retrace.1 = (f32[64,480]{1,0:T(8,128)}, f32[160,480]{1,0:T(8,128)}, f32[160,480]{1,0:T(8,128)}, f32[64,1280]{1,0:T(8,128)}, f32[5,384,128]{2,1,0:T(8,128)}, /*index=5*/bf16[16,5,128,128]{3,2,1,0:T(8,128)(2,1)}) custom-call(bf16[16,2,64,480]{3,2,1,0:T(8,128)(2,1)} %bitcast.219, bf16[16,2,160,480]{3,2,1,0:T(8,128)(2,1)} %bitcast.211, ...), custom_call_target="tpu_custom_call" | custom-call | tf_op jit(solution)/shard_map/scatter_rest_retrace/pallas_call | solution.py:510
  335.0 1.5 copy.77
  336.7 1.0 copy.78
  337.8 26.4 %scatter_pairs.1 = f32[640,128]{1,0:T(8,128)} custom-call(bf16[8,2,640,128]{3,2,1,0:T(8,128)(2,1)} %bitcast.232), custom_call_target="tpu_custom_call" | custom-call | tf_op jit(solution)/shard_map/scatter_pairs/pallas_call | solution.py:510
  364.2 1.2 copy.79
  366.8 2.9 fusion.64
  369.7 0.9 fusion.62
  371.7 1.4 copy_bitcast_fusion.grads
  374.2 4.9 %weight_terms.9 = bf16[2,2048,480]{2,1,0:T(8,128)(2,1)} custom-call(bf16[128,2048]{1,0:T(8,128)(2,1)} %copy_bitcast_fusion.grads, bf16[2,128,480]{2,1,0:T(8,128)(2,1)} %fusion.32.values), custom_call_target="tpu_custom_call" | custom-call | flops 503316480 | bytes 3932160 | tf_op jit(solution)/shard_map/weight_terms/pallas_call | solution.py:592
  379.1 1.9 scatter.4
  381.0 4.8 %fusion.71 = (bf16[32,64,480]{2,1,0:T(8,128)(2,1)}, bf16[32,64,480]{2,1,0:T(8,128)(2,1)}) fusion(bf16[32,128,480]{2,1,0:T(8,128)(2,1)} %bitcast.214), kind=kLoop, calls=%fused_computation.151 | loop fusion | bytes 7864320 | tf_op jit(solution)/shard_map/slice | solution.py:908
  385.8 27.4 %scatter_first.1 = (f32[64,480]{1,0:T(8,128)}, f32[64,480]{1,0:T(8,128)}) custom-call(bf16[16,2,64,480]{3,2,1,0:T(8,128)(2,1)} %bitcast.221, bf16[16,2,64,480]{3,2,1,0:T(8,128)(2,1)} %bitcast.220), custom_call_target="tpu_custom_call" | custom-call | tf_op jit(solution)/shard_map/scatter_first/pallas_call | solution.py:510
  413.2 1.6 slice_bitcast_fusion.3
  414.8 1.5 slice_bitcast_fusion.4
  416.2 1.3 slice_bitcast_fusion.6
  417.6 2.9 fusion.68
  420.5 1.0 fusion.29
  421.6 1.0 convolution_add_fusion.4
  423.7 1.9 fusion.12
  (195 shorter events, 22.3 us)
Async XLA Ops:
  34.0 5.1 %copy-start.25 = (bf16[32,64,480]{2,1,0:T(8,128)(2,1)S(1)}, bf16[32,64,480]{2,1,0:T(8,128)(2,1)}, u32[]{:S(2)}) copy-start(bf16[32,64,480]{2,1,0:T(8,128)(2,1)} %get-tuple-element.39) | copy-start | bytes 5898244
  35.0 4.2 copy-start.45
  35.1 4.2 copy-start.47
  36.2 3.1 copy-start.59
  36.2 3.1 copy-start.56
  39.3 2.0 copy-start.8
  43.3 1.0 copy-start.18
  43.5 1.7 copy-start.43
  70.5 2.7 copy-start.42
  70.6 3.3 copy-start.49
  160.6 1.9 copy-start.32
  162.5 0.7 copy-start.24
  162.5 1.4 copy-start.3
  164.8 47.0 %copy-start.10 = (f32[128,16,60]{0,2,1:T(8,128)}, f32[128,16,60]{0,2,1:T(8,128)S(1)}, u32[]{:S(2)}) copy-start(f32[128,16,60]{0,2,1:T(8,128)S(1)} %get-tuple-element.80) | copy-start | bytes 1474564
  164.9 41.6 %copy-start.53 = (f32[128]{0:T(128)}, f32[128]{0:T(128)S(1)}, u32[]{:S(2)}) copy-start(f32[128]{0:T(128)S(1)} %fusion.55) | copy-start | bytes 1540
  165.0 6.0 %copy-start.50 = (f32[960]{0:T(1024)}, f32[960]{0:T(1024)S(1)}, u32[]{:S(2)}) copy-start(f32[960]{0:T(1024)S(1)} %reshape.638) | copy-start | bytes 11524
  165.2 9.3 %copy-start.27 = (bf16[128,960]{0,1:T(8,128)(2,1)}, bf16[128,960]{0,1:T(8,128)(2,1)S(1)}, u32[]{:S(2)}) copy-start(bf16[128,960]{0,1:T(8,128)(2,1)S(1)} %fusion.26) | copy-start | bytes 737284
  171.0 3.6 copy-start
  171.0 3.6 copy-start.1
  178.4 2.5 copy-start.12
  178.4 5.0 %copy-start.29 = (f32[128,2560]{1,0:T(8,128)S(1)}, f32[128,2560]{1,0:T(8,128)}, u32[]{:S(2)}) copy-start(f32[128,2560]{1,0:T(8,128)} %fusion.44) | copy-start | bytes 3932164
  178.4 5.0 %copy-start.30 = (f32[128,2560]{1,0:T(8,128)S(1)}, f32[128,2560]{1,0:T(8,128)}, u32[]{:S(2)}) copy-start(f32[128,2560]{1,0:T(8,128)} %convolution_add_fusion) | copy-start | bytes 3932164
  180.9 2.6 copy-start.6
  180.9 2.6 copy-start.28
  183.4 3.1 copy-start.2
  185.7 0.8 copy-start.14
  192.9 7.3 %copy-start.7 = (bf16[16,160,480]{2,1,0:T(8,128)(2,1)S(1)}, bf16[16,160,480]{2,1,0:T(8,128)(2,1)}, u32[]{:S(2)}) copy-start(bf16[16,160,480]{2,1,0:T(8,128)(2,1)} %get-tuple-element.63) | copy-start | bytes 7372804
  203.1 5.7 %copy-start.26 = (bf16[32,64,480]{2,1,0:T(8,128)(2,1)S(1)}, bf16[32,64,480]{2,1,0:T(8,128)(2,1)}, u32[]{:S(2)}) copy-start(bf16[32,64,480]{2,1,0:T(8,128)(2,1)} %get-tuple-element.42) | copy-start | bytes 5898244
  206.5 0.6 copy-start.58
  207.1 2.8 copy-start.33
  208.8 2.1 copy-start.31
  210.8 2.2 copy-start.54
  211.9 0.8 copy-start.16
  224.9 2.6 copy-start.13
  364.2 1.9 copy-start.15
  366.1 3.6 copy-start.9
  366.7 3.9 copy-start.4
  366.8 3.9 copy-start.48
  366.8 3.9 copy-start.57
  369.6 1.8 copy-start.35
  369.6 1.9 copy-start.52
  369.7 3.4 copy-start.46
  369.7 3.5 copy-start.17
  370.6 0.9 copy-start.37
  417.6 2.9 copy-start.19
  421.5 2.0 copy-start.11
  421.5 2.1 copy-start.5
  421.5 2.1 copy-start.20
  421.5 2.1 copy-start.21
  421.6 2.1 copy-start.22
  421.6 2.1 copy-start.23
  421.6 2.1 copy-start.34
  421.6 2.1 copy-start.36
  421.6 2.1 copy-start.38
  421.6 2.1 copy-start.51
  421.6 2.1 copy-start.55
  423.7 1.9 copy-start.41
  423.7 2.7 copy-start.44
  423.7 3.3 copy-start.40
  423.7 4.0 copy-start.39

commit v3 on v2

--- a/solution.py
+++ b/solution.py
@@ -38,11 +38,6 @@
 
 def unrotate(values, cosine, sine_table):
     return rotate(values, cosine, -sine_table)
-
-
-def normed(row_values, gain_vec):
-    scale_rows = lax.rsqrt(jnp.mean(row_values * row_values, axis=-1, keepdims=True) + EPSILON)
-    return row_values * scale_rows * gain_vec
 
 
 class Place:
@@ -108,19 +103,38 @@
         body(low, False)
 
 
-def gather_kernel(depth, use_x, routes, work, *refs):
-    count = len(routes)
-    ins, work_ins, refs = refs[:count], refs[count : count + work.ins], refs[count + work.ins :]
-    outs, work_outs, refs = refs[:count], refs[count : count + work.outs], refs[count + work.outs :]
+class Chunk:
+    def __init__(self, array, start, rows, route):
+        self.array, self.start, self.rows, self.route = array, start, rows, route
+        self.span = pl.ds(start, rows)
+
+
+def cut(array, rows, parts, routes):
+    size = padded(-(-rows // parts))
+    starts = range(0, rows, size)
+    return [
+        Chunk(array, start, min(size, rows - start), routes[i % len(routes)])
+        for i, start in enumerate(starts)
+    ]
+
+
+def gather_kernel(depth, use_x, chunks, work, *refs):
+    total, count = chunks[-1].array + 1, len(chunks)
+    routes = [chunk.route for chunk in chunks]
+    ins, work_ins, refs = refs[:total], refs[total : total + work.ins], refs[total + work.ins :]
+    outs, work_outs, refs = refs[:total], refs[total : total + work.outs], refs[total + work.outs :]
     recv, send_z, send_p, send_q, send_c, local_sem = refs
     place = Place(depth, use_x)
     place.barrier()
 
+    def landing(k, slot):
+        return outs[chunks[k].array].at[slot, chunks[k].span]
+
     def copy(k, pid, send_sem, way, src=None):
         slot = pid * 2 + place.c
         return pltpu.make_async_remote_copy(
-            src_ref=outs[k].at[slot] if src is None else src,
-            dst_ref=outs[k].at[slot],
+            src_ref=landing(k, slot) if src is None else src,
+            dst_ref=landing(k, slot),
             send_sem=send_sem,
             recv_sem=recv.at[k, slot],
             device_id=place.device(way),
@@ -147,7 +161,7 @@
     own = []
     for k in range(count):
         pid = place.piece(routes[k], 0, 0, place.z)
-        src = ins[k]
+        src = ins[chunks[k].array].at[chunks[k].span]
 
         @pl.when(place.has_up)
         def _():
@@ -161,7 +175,7 @@
             forward_p(k, place.z, src).start()
         forward_q(k, 0, place.z, src).start()
         forward_c(k, pid, src).start()
-        mine = pltpu.make_async_copy(src, outs[k].at[pid * 2 + place.c], local_sem.at[k])
+        mine = pltpu.make_async_copy(src, landing(k, pid * 2 + place.c), local_sem.at[k])
         mine.start()
         own.append(mine)
 
@@ -246,8 +260,8 @@
             forward_c(k, pid).wait_send()
             slot = pid * 2 + 1 - place.c
             pltpu.make_async_remote_copy(
-                src_ref=outs[k].at[slot],
-                dst_ref=outs[k].at[slot],
+                src_ref=landing(k, slot),
+                dst_ref=landing(k, slot),
                 send_sem=send_c.at[k, pid],
                 recv_sem=recv.at[k, slot],
                 device_id=place.device("c"),
@@ -266,17 +280,17 @@
         self.ins, self.outs = len(arrays), len(self.shapes)
 
 
-def gather(arrays, routes, use_x, collective_id, name, work=Work()):
+def gather(arrays, chunks, use_x, collective_id, name, work=Work()):
     depth = lax.axis_size("ctx") // 4
     pieces = (4 if use_x else 2) * depth
-    count = len(arrays)
+    total, count = len(arrays), len(chunks)
     dma = pltpu.SemaphoreType.DMA
     return pl.pallas_call(
-        functools.partial(gather_kernel, depth, use_x, routes, work),
+        functools.partial(gather_kernel, depth, use_x, chunks, work),
         out_shape=[jax.ShapeDtypeStruct((2 * pieces, *a.shape), a.dtype) for a in arrays]
         + work.shapes,
-        in_specs=[pl.BlockSpec(memory_space=pltpu.VMEM)] * (count + work.ins),
-        out_specs=[pl.BlockSpec(memory_space=pl.ANY)] * count
+        in_specs=[pl.BlockSpec(memory_space=pltpu.VMEM)] * (total + work.ins),
+        out_specs=[pl.BlockSpec(memory_space=pl.ANY)] * total
         + [pl.BlockSpec(memory_space=pltpu.VMEM)] * work.outs,
         scratch_shapes=[
             dma((count, 2 * pieces)),
@@ -307,20 +321,38 @@
     lax.fori_loop(0, rows // block, body, 0)
 
 
-def scatter_kernel(depth, use_x, routes, work, *refs):
-    count = len(routes)
-    ins, work_ins, refs = refs[:count], refs[count : count + work.ins], refs[count + work.ins :]
-    outs, work_outs, refs = refs[:count], refs[count : count + work.outs], refs[count + work.outs :]
-    own, part, land_q, land_p, land_z = (refs[i * count : (1 + i) * count] for i in range(5))
-    load_sem, c_send, c_recv, q_send, q_recv, p_send, p_recv, z_send, z_recv = refs[5 * count :]
+def scatter_kernel(depth, use_x, chunks, work, *refs):
+    total, count = chunks[-1].array + 1, len(chunks)
+    routes = [chunk.route for chunk in chunks]
+    ins, work_ins, refs = refs[:total], refs[total : total + work.ins], refs[total + work.ins :]
+    outs, work_outs, refs = refs[:total], refs[total : total + work.outs], refs[total + work.outs :]
+    whole = [refs[i * total : (1 + i) * total] for i in range(5)]
+    load_sem, c_send, c_recv, q_send, q_recv, p_send, p_recv, z_send, z_recv = refs[5 * total :]
+
+    class View:
+        def __init__(self, ref, span):
+            self.ref, self.span = ref, span
+
+        @property
+        def at(self):
+            return self
+
+        def __getitem__(self, index):
+            index = index if isinstance(index, tuple) else (index,)
+            return self.ref.at[(*index, self.span)]
+
+    own, part, land_q, land_p, land_z = (
+        [View(group[chunk.array], chunk.span) for chunk in chunks] for group in whole
+    )
+    sums = [outs[chunk.array].at[chunk.span] for chunk in chunks]
     place = Place(depth, use_x)
     pieces = (4 if use_x else 2) * depth
-    rows = [out.shape[0] for out in outs]
+    rows = [chunk.rows for chunk in chunks]
 
     def load(k):
-        return pltpu.make_async_copy(ins[k].at[:, place.c], own[k], load_sem.at[k])
-
-    for k in range(count):
+        return pltpu.make_async_copy(ins[k].at[:, place.c], whole[0][k], load_sem.at[k])
+
+    for k in range(total):
         load(k).start()
     place.barrier()
 
@@ -336,7 +368,7 @@
 
     def send_c(k, pid):
         return remote(
-            ins[k].at[pid, 1 - place.c], part[k].at[pid], c_send.at[k, pid], c_recv.at[k, pid], "c"
+            ins[chunks[k].array].at[pid, 1 - place.c, chunks[k].span], part[k].at[pid], c_send.at[k, pid], c_recv.at[k, pid], "c"
         )
 
     def send_q(k, rel_p, z0):
@@ -383,7 +415,7 @@
         return carry
 
     lax.fori_loop(0, depth, first, 0)
-    for k in range(count):
+    for k in range(total):
         load(k).wait()
 
     def step(s, carry):
@@ -454,17 +486,17 @@
         def _():
             for k in range(count):
                 _, sources = sources_of(k, place.z)
-                add_up(outs[k], sources, rows[k])
+                add_up(sums[k], sources, rows[k])
 
                 @pl.when(place.has_down)
                 def _():
                     wait_z(k, place.z)
-                    add_up(outs[k], [outs[k], land_z[k].at[place.z]], rows[k])
+                    add_up(sums[k], [sums[k], land_z[k].at[place.z]], rows[k])
 
                 @pl.when(place.has_up)
                 def _():
                     wait_z(k, depth)
-                    add_up(outs[k], [outs[k], land_z[k].at[depth]], rows[k])
+                    add_up(sums[k], [sums[k], land_z[k].at[depth]], rows[k])
 
         return carry
 
@@ -499,27 +531,27 @@
     lax.fori_loop(0, pieces, finish_partner, 0)
 
 
-def scatter(arrays, routes, use_x, collective_id, name, work=Work()):
+def scatter(arrays, chunks, use_x, collective_id, name, work=Work()):
     depth = lax.axis_size("ctx") // 4
     pieces = (4 if use_x else 2) * depth
-    count = len(arrays)
+    total, count = len(arrays), len(chunks)
     dma = pltpu.SemaphoreType.DMA
     shapes = [a.shape[1:] for a in arrays]
     pairs = [a.reshape(pieces, 2, *s) for a, s in zip(arrays, shapes)]
     bf16 = jnp.bfloat16
     return pl.pallas_call(
-        functools.partial(scatter_kernel, depth, use_x, routes, work),
+        functools.partial(scatter_kernel, depth, use_x, chunks, work),
         out_shape=[jax.ShapeDtypeStruct(s, jnp.float32) for s in shapes] + work.shapes,
-        in_specs=[pl.BlockSpec(memory_space=pl.ANY)] * count
+        in_specs=[pl.BlockSpec(memory_space=pl.ANY)] * total
         + [pl.BlockSpec(memory_space=pltpu.VMEM)] * work.ins,
-        out_specs=[pl.BlockSpec(memory_space=pltpu.VMEM)] * (count + work.outs),
+        out_specs=[pl.BlockSpec(memory_space=pltpu.VMEM)] * (total + work.outs),
         scratch_shapes=[pltpu.VMEM((pieces, *s), bf16) for s in shapes]
         + [pltpu.VMEM((pieces, *s), bf16) for s in shapes]
         + [pltpu.VMEM((2, depth, *s), bf16) for s in shapes]
         + [pltpu.VMEM((depth, *s), bf16) for s in shapes]
         + [pltpu.VMEM((depth + 1, *s), bf16) for s in shapes]
         + [
-            dma((count,)),
+            dma((total,)),
             dma((count, pieces)),
             dma((count, pieces)),
             dma((count, 2, depth)),
@@ -545,9 +577,6 @@
 
 
 XY, YX, ONLY_Y = ("x", "y"), ("y", "x"), (None, "y")
-REST_ROUTES = (YX, XY, XY, YX)
-
-
 def halves(values, split_count):
     return values.reshape(values.shape[0], split_count, values.shape[1] // split_count)
 
@@ -692,6 +721,193 @@
     lax.fori_loop(needed, blocks // PIECES_PER_BLOCK, clear, 0)
 
 
+def wait_all(copies):
+    for copy in copies:
+        copy.wait()
+
+
+def turned(left, right):
+    return lax.dot_general(left, right, (((1,), (1,)), ((), ())), preferred_element_type=jnp.float32)
+
+
+def plain(left, right):
+    return jnp.dot(left, right, preferred_element_type=jnp.float32)
+
+
+def mlp_kernel(
+    real_width,
+    attended_ref, resid_ref, grad_ref, gain_ref, out_hbm, gate_hbm, up_hbm, down_hbm,
+    output_ref, grad_resid_ref, grad_attended_ref, term_gain_ref,
+    terms_out_hbm, terms_gate_hbm, terms_up_hbm, terms_down_hbm,
+    out_w, gate_w, up_w, down_w, terms_out, terms_gate, terms_up, terms_down,
+    resid2_ref, normal_ref, gate_ref, up_ref, hidden_ref, grad_gate_ref, grad_up_ref, branch_ref,
+    load_sem, store_sem,
+):
+    splits, _, part = gate_w.shape
+    span = down_w.shape[2]
+    width = out_w.shape[1]
+    loads = [
+        pltpu.make_async_copy(src, dst, load_sem.at[i])
+        for i, (src, dst) in enumerate(
+            ((out_hbm, out_w), (gate_hbm, gate_w), (up_hbm, up_w), (down_hbm, down_w))
+        )
+    ]
+    for load in loads:
+        load.start()
+
+    def slice_of(i, size=part):
+        return slice(i * size, (i + 1) * size)
+
+    loads[0].wait()
+    resid2 = resid_ref[...]
+    for i in range(splits):
+        resid2 = resid2 + turned(attended_ref[:, slice_of(i)], out_w[i])
+    scale = lax.rsqrt(jnp.sum(resid2 * resid2, axis=-1, keepdims=True) / real_width + EPSILON)
+    resid2_ref[...] = resid2
+    normal_ref[...] = (resid2 * scale * gain_ref[...]).astype(jnp.bfloat16)
+    loads[1].wait()
+    loads[2].wait()
+    block = 256 if span % 256 == 0 else 128
+    steps = span // block
+
+    def lanes(i, step):
+        return pl.ds(pl.multiple_of(i * span + step * block, block), block)
+
+    def forward(index, carry):
+        cols = pl.ds(pl.multiple_of(index * block, block), block)
+        gate = up = None
+        for i in range(splits):
+            normal = normal_ref[:, slice_of(i)]
+            gate_term = turned(normal, gate_w[i, cols, :])
+            up_term = turned(normal, up_w[i, cols, :])
+            gate = gate_term if gate is None else gate + gate_term
+            up = up_term if up is None else up + up_term
+        gate_ref[:, cols] = gate
+        up_ref[:, cols] = up
+        hidden_ref[:, cols] = (gate * jax.nn.sigmoid(gate) * up).astype(jnp.bfloat16)
+        return carry
+
+    lax.fori_loop(0, splits * steps, forward, 0)
+    loads[3].wait()
+    total = resid2_ref[...]
+    for i in range(splits):
+        total = total + turned(hidden_ref[:, slice_of(i, span)], down_w[i])
+    output_ref[...] = total.astype(jnp.bfloat16)
+
+    for i in range(splits):
+
+        def backward(step, carry):
+            inner = pl.ds(pl.multiple_of(step * block, block), block)
+            cols = lanes(i, step)
+            grad_hidden = plain(grad_ref[...], down_w[i, :, inner])
+            gate, up = gate_ref[:, cols], up_ref[:, cols]
+            sigma = jax.nn.sigmoid(gate)
+            grad_up_ref[:, cols] = (grad_hidden * gate * sigma).astype(jnp.bfloat16)
+            grad_gate_ref[:, cols] = (
+                grad_hidden * up * sigma * (1.0 + gate * (1.0 - sigma))
+            ).astype(jnp.bfloat16)
+            return carry
+
+        lax.fori_loop(0, steps, backward, 0)
+
+    def terms(rows, left_ref, right_ref, size, target):
+        rows_block = 256 if rows % 256 == 0 else 128
+
+        def body(step, carry):
+            cols = pl.ds(pl.multiple_of(step * rows_block, rows_block), rows_block)
+            left = left_ref[:, cols]
+            for i in range(splits):
+                target[i, cols, :] = lax.dot_general(
+                    left,
+                    right_ref[:, slice_of(i, size)],
+                    (((0,), (0,)), ((), ())),
+                    preferred_element_type=jnp.float32,
+                ).astype(jnp.bfloat16)
+            return carry
+
+        lax.fori_loop(0, rows // rows_block, body, 0)
+
+    stores = [
+        pltpu.make_async_copy(src, dst, store_sem.at[i])
+        for i, (src, dst) in enumerate(
+            (
+                (terms_down, terms_down_hbm),
+                (terms_gate, terms_gate_hbm),
+                (terms_up, terms_up_hbm),
+                (terms_out, terms_out_hbm),
+            )
+        )
+    ]
+    terms(width, grad_ref, hidden_ref, span, terms_down)
+    stores[0].start()
+    terms(splits * span, grad_gate_ref, normal_ref, part, terms_gate)
+    stores[1].start()
+    terms(splits * span, grad_up_ref, normal_ref, part, terms_up)
+    stores[2].start()
+
+    resid2 = resid2_ref[...]
+    scale = lax.rsqrt(jnp.sum(resid2 * resid2, axis=-1, keepdims=True) / real_width + EPSILON)
+    pulls, inner_sum = [], 0.0
+    for i in range(splits):
+        pull = plain(grad_gate_ref[...], gate_w[i]) + plain(grad_up_ref[...], up_w[i])
+        resid_part = resid2_ref[:, slice_of(i)]
+        term_gain_ref[:, slice_of(i)] = jnp.sum(pull * resid_part * scale, axis=0, keepdims=True)
+        pull = pull * gain_ref[:, slice_of(i)]
+        inner_sum = inner_sum + jnp.sum(pull * resid_part, axis=-1, keepdims=True)
+        pulls.append(pull)
+    shift = scale * scale * scale * inner_sum / real_width
+    for i in range(splits):
+        grad_resid = (
+            grad_ref[:, slice_of(i)].astype(jnp.float32)
+            + pulls[i] * scale
+            - resid2_ref[:, slice_of(i)] * shift
+        )
+        grad_resid_ref[:, slice_of(i)] = grad_resid
+        branch_ref[:, slice_of(i)] = grad_resid.astype(jnp.bfloat16)
+    for i in range(splits):
+        grad_attended_ref[:, slice_of(i)] = plain(branch_ref[...], out_w[i]).astype(jnp.bfloat16)
+    terms(width, branch_ref, attended_ref, part, terms_out)
+    stores[3].start()
+    wait_all(stores)
+
+
+def mlp(attended, resid1, grad_rows, gain, out_w, gate_w, up_w, down_w, real_width):
+    rows, width = resid1.shape
+    hidden_width = gate_w.shape[1]
+    f32, bf16 = jnp.float32, jnp.bfloat16
+    weights = [out_w, gate_w, up_w, down_w]
+    vmem, anywhere = pl.BlockSpec(memory_space=pltpu.VMEM), pl.BlockSpec(memory_space=pl.ANY)
+    kept = [pltpu.VMEM(w.shape, bf16) for w in weights]
+    return pl.pallas_call(
+        functools.partial(mlp_kernel, real_width),
+        out_shape=[
+            jax.ShapeDtypeStruct((rows, width), bf16),
+            jax.ShapeDtypeStruct((rows, width), f32),
+            jax.ShapeDtypeStruct(attended.shape, bf16),
+            jax.ShapeDtypeStruct((1, width), f32),
+        ]
+        + [jax.ShapeDtypeStruct(w.shape, bf16) for w in weights],
+        in_specs=[vmem] * 4 + [anywhere] * 4,
+        out_specs=[vmem] * 4 + [anywhere] * 4,
+        scratch_shapes=kept
+        + kept
+        + [
+            pltpu.VMEM((rows, width), f32),
+            pltpu.VMEM((rows, width), bf16),
+            pltpu.VMEM((rows, hidden_width), f32),
+            pltpu.VMEM((rows, hidden_width), f32),
+            pltpu.VMEM((rows, hidden_width), bf16),
+            pltpu.VMEM((rows, hidden_width), bf16),
+            pltpu.VMEM((rows, hidden_width), bf16),
+            pltpu.VMEM((rows, width), bf16),
+            pltpu.SemaphoreType.DMA((4,)),
+            pltpu.SemaphoreType.DMA((4,)),
+        ],
+        compiler_params=pltpu.CompilerParams(vmem_limit_bytes=VMEM_LIMIT),
+        name="mlp",
+    )(attended, resid1, grad_rows, gain, *weights)
+
+
 def local(
     inputs, grad_output, w_query, w_key, w_value, w_out, w_gate, w_up, w_down, gain_attn, gain_mlp
 ):
@@ -709,55 +925,67 @@
     cosine = jnp.tile(cosine, (seq_count, 1))
     sine_table = jnp.tile(sine_table, (seq_count, 1))
     wide_q, wide_k, wide_v = w_query.shape[1], w_key.shape[1], w_value.shape[1]
-    wide_o, wide_g, wide_u = w_out.shape[1], w_gate.shape[1], w_up.shape[1]
-    wide_d = w_down.shape[1]
+    wide_o, wide_g = w_out.shape[1], w_gate.shape[1]
     pad_q, pad_k, pad_v = padded(wide_q), padded(wide_k + 1), padded(wide_v)
-    pad_o, pad_g, pad_u, pad_d = padded(wide_o), padded(wide_g), padded(wide_u), padded(wide_d)
+    pad_o, pad_g = padded(wide_o), padded(wide_g)
     part_width = w_query.shape[0]
+    wide_part = part_width // wide_o * pad_o
     gain_size = gain_attn.shape[0]
 
-    def open_up(values, wide, start, pad):
+    def spread(weight, wide, pad):
+        pieces = weight.reshape(-1, wide, weight.shape[1])
+        pieces = jnp.pad(pieces, ((0, 0), (0, pad - wide), (0, 0)))
+        return pieces.reshape(-1, weight.shape[1]).T
+
+    def gathered_spread(total, wide, pad):
+        pieces = total.T.reshape(-1, pad, total.shape[0])
+        return pieces[:, :wide].reshape(-1, total.shape[0])
+
+    def open_up(values, wide, start):
         pieces = values.reshape(values.shape[0], cycle_size, -1)
         return pieces[:, :, start : start + wide].reshape(values.shape[0], cycle_size * wide)
 
-    def close_up(values, wide, pad):
-        pieces = values.reshape(values.shape[0], cycle_size, wide)
-        return jnp.pad(pieces, ((0, 0), (0, 0), (0, pad - wide))).reshape(values.shape[0], -1)
+    def close_up(values):
+        pieces = values.reshape(row_count, cycle_size, wide_o)
+        return jnp.pad(pieces, ((0, 0), (0, 0), (0, pad_o - wide_o))).reshape(row_count, -1)
+
+    def model(weight):
+        return spread(weight, wide_o, pad_o)
 
     gain_row = jnp.pad(
-        jnp.concatenate([gain_attn, gain_mlp]), (0, part_width - 2 * gain_size)
+        jnp.concatenate([jnp.pad(g, (0, pad_o - gain_size)) for g in (gain_attn, gain_mlp)]),
+        (0, wide_part - 2 * pad_o),
     )[None, :]
     first_piece = jnp.concatenate(
         [
-            pad_rows(w_query.T, pad_q),
-            pad_rows(jnp.concatenate([w_key.T, gain_row], axis=0), pad_k),
-            pad_rows(w_value.T, pad_v),
+            pad_rows(model(w_query), pad_q),
+            pad_rows(jnp.concatenate([model(w_key), gain_row], axis=0), pad_k),
+            pad_rows(model(w_value), pad_v),
         ],
         axis=0,
     )
-    half = padded(first_piece.shape[0] // 2)
-    first_a, first_b = gather(
-        [first_piece[:half], first_piece[half:]], (YX, XY), True, 0, "gather_first"
-    )
-    first = jnp.concatenate([first_a, first_b], axis=1)
-    gain_rows = first[:cycle_size, pad_q + wide_k, : 2 * gain_size]
-    gain_first = gain_rows[:, :gain_size].reshape(-1).astype(jnp.float32)
-    gain_second = gain_rows[:, gain_size:].reshape(-1).astype(jnp.float32)
-    first = first.reshape(split_count, -1, part_width)
-
-    resid1 = inputs.reshape(row_count, model_width).astype(jnp.float32)
-    normal1 = normed(resid1, gain_first).astype(jnp.bfloat16)
+    first_chunks = cut(0, first_piece.shape[0], 4, (YX, XY))
+    (first,) = gather([first_piece], first_chunks, True, 0, "gather_first")
+    gain_rows = first[:cycle_size, pad_q + wide_k, : 2 * pad_o]
+    gain_first = gain_rows[:, :pad_o].reshape(1, -1).astype(jnp.float32)
+    gain_second = gain_rows[:, pad_o:].reshape(1, -1).astype(jnp.float32)
+    first = first.reshape(split_count, -1, wide_part)
+
+    resid1 = close_up(inputs.reshape(row_count, model_width)).astype(jnp.float32)
+    scale1 = lax.rsqrt(jnp.sum(resid1 * resid1, axis=-1, keepdims=True) / model_width + EPSILON)
+    normal1 = (resid1 * scale1 * gain_first).astype(jnp.bfloat16)
     raw = forward_dot(normal1, first)
-    query_raw = open_up(raw, wide_q, 0, pad_q).reshape(row_count, HEADS, head_size)
+    query_raw = open_up(raw, wide_q, 0).reshape(row_count, HEADS, head_size)
     query_rot = rotate(query_raw, cosine, sine_table).astype(jnp.bfloat16)
-    key_raw = open_up(raw, wide_k, pad_q, pad_k).reshape(row_count, groups, head_size)
+    key_raw = open_up(raw, wide_k, pad_q).reshape(row_count, groups, head_size)
     key_rows = rotate(key_raw, cosine, sine_table).astype(jnp.bfloat16)
-    value_rows = open_up(raw, wide_v, pad_q + pad_k, pad_v).astype(jnp.bfloat16)
+    value_rows = open_up(raw, wide_v, pad_q + pad_k).astype(jnp.bfloat16)
     value_rows = value_rows.reshape(row_count, groups, head_size)
     pair_rows = jnp.transpose(jnp.concatenate([key_rows, value_rows], axis=-1), (1, 0, 2))
+    pair_chunks = cut(0, groups * row_count, 2, (ONLY_Y,))
     (pair_all,) = gather(
         [pair_rows.reshape(groups * row_count, 2 * head_size)],
-        (ONLY_Y,),
+        pair_chunks,
         False,
         1,
         "gather_pairs",
@@ -770,14 +998,21 @@
 
     query_grouped = jnp.pad(by_group(query_rot), ((0, 0), (0, 0), (0, head_size)))
     width = repeat_count * row_count
+    out_piece = jnp.pad(w_out.T, ((0, pad_o - wide_o), (0, wide_part - part_width)))
+    rest_chunks = (
+        cut(0, pad_o, 2, (XY, YX))
+        + cut(1, pad_g, 1, (XY,))
+        + cut(2, pad_g, 1, (YX,))
+        + cut(3, pad_o, 2, (XY, YX))
+    )
     out_w, gate_w, up_w, down_w, attended_turned, logsum = gather(
         [
-            pad_rows(w_out.T, pad_o),
-            pad_rows(w_gate.T, pad_g),
-            pad_rows(w_up.T, pad_u),
-            pad_rows(w_down.T, pad_d),
+            out_piece,
+            pad_rows(model(w_gate), pad_g),
+            pad_rows(model(w_up), pad_g),
+            pad_rows(spread(w_down, wide_g, pad_g), pad_o),
         ],
-        REST_ROUTES,
+        rest_chunks,
         True,
         4,
         "gather_rest_attend",
@@ -798,35 +1033,16 @@
         attended_turned[:, head_size:].reshape(groups, head_size, repeat_count, row_count),
         (3, 0, 2, 1),
     )
-    attended_rows = attended_wide.astype(jnp.bfloat16).reshape(row_count, HEADS * head_size)
-    resid2 = resid1 + open_up(forward_dot(attended_rows, out_w), wide_o, 0, pad_o)
-    normal2 = normed(resid2, gain_second).astype(jnp.bfloat16)
-    gate_act = forward_dot(normal2, gate_w)
-    up_act = forward_dot(normal2, up_w)
-    gate_sigma = jax.nn.sigmoid(gate_act)
-    hidden = (gate_act * gate_sigma * up_act).astype(jnp.bfloat16)
-    hidden_flat = open_up(hidden, wide_g, 0, pad_g)
-    output = (
-        resid2 + open_up(forward_dot(hidden_flat, down_w), wide_d, 0, pad_d)
-    ).astype(jnp.bfloat16)
-
-    grad_rows = grad_output.reshape(row_count, model_width)
-    grad_rows_padded = close_up(grad_rows, wide_d, pad_d)
-    terms_down = weight_terms(grad_rows_padded, hidden_flat, split_count)
-    grad_hidden = close_up(backward_dot(grad_rows_padded, down_w), wide_g, pad_g)
-    grad_up = (grad_hidden * gate_act * gate_sigma).astype(jnp.bfloat16)
-    grad_gate = (grad_hidden * up_act * gate_sigma * (1.0 + gate_act * (1.0 - gate_sigma))).astype(
-        jnp.bfloat16
-    )
-    grad_norm2 = backward_dot(grad_gate, gate_w) + backward_dot(grad_up, up_w)
-    normed_out, pull_second = jax.vjp(normed, resid2, gain_second)
-    grad_part2, term_gain2 = pull_second(grad_norm2)
-    grad_resid2 = grad_rows.astype(jnp.float32) + grad_part2
-    grad_branch = close_up(grad_resid2.astype(jnp.bfloat16), wide_o, pad_o)
-    terms_out = weight_terms(grad_branch, attended_rows, split_count)
-    terms_gate = weight_terms(grad_gate, normal2, split_count)
-    terms_up = weight_terms(grad_up, normal2, split_count)
-    grad_attended = backward_dot(grad_branch, out_w).astype(jnp.bfloat16)
+    attended = jnp.pad(
+        attended_wide.astype(jnp.bfloat16).reshape(row_count, split_count, part_width),
+        ((0, 0), (0, 0), (0, wide_part - part_width)),
+    ).reshape(row_count, -1)
+    grad_rows = close_up(grad_output.reshape(row_count, model_width))
+    output, grad_resid2, grad_attended, term_gain2, terms_out, terms_gate, terms_up, terms_down = mlp(
+        attended, resid1, grad_rows, gain_second, out_w, gate_w, up_w, down_w, model_width
+    )
+    grad_attended = grad_attended.reshape(row_count, split_count, wide_part)[..., :part_width]
+    grad_attended = grad_attended.reshape(row_count, -1)
     row_delta = jnp.sum(
         grad_attended.astype(jnp.float32).reshape(attended_wide.shape) * attended_wide, axis=-1
     )
@@ -838,7 +1054,7 @@
 
     sum_out, sum_gate, sum_up, sum_down, grad_query_acc, grad_pair_all = scatter(
         [pieces_of(t) for t in (terms_out, terms_gate, terms_up, terms_down)],
-        REST_ROUTES,
+        rest_chunks,
         True,
         3,
         "scatter_rest_retrace",
@@ -854,7 +1070,7 @@
     )
     (grad_pair_own,) = scatter(
         [grad_pair_all.reshape(cycle_size, groups * row_count, 2 * head_size)],
-        (ONLY_Y,),
+        pair_chunks,
         False,
         2,
         "scatter_pairs",
@@ -891,36 +1107,39 @@
         axis=-1,
     ).reshape(row_count, -1)
     grad_norm1 = backward_dot(grad_raw, first)
-    normed_first, pull_first = jax.vjp(normed, resid1, gain_first)
-    grad_part1, term_gain1 = pull_first(grad_norm1)
-    grad_input = (
-        (grad_resid2 + grad_part1).astype(jnp.bfloat16).reshape(seq_count, block_len, model_width)
-    )
+    term_gain1 = jnp.sum(grad_norm1 * resid1 * scale1, axis=0)
+    pull = grad_norm1 * gain_first
+    shift = scale1**3 * jnp.sum(pull * resid1, axis=-1, keepdims=True) / model_width
+    grad_input = (grad_resid2 + pull * scale1 - resid1 * shift).astype(jnp.bfloat16)
     gain_terms = jnp.concatenate(
-        [term_gain1.reshape(cycle_size, -1), term_gain2.reshape(cycle_size, -1)], axis=-1
+        [term_gain1.reshape(cycle_size, pad_o), term_gain2.reshape(cycle_size, pad_o)], axis=-1
     ).astype(jnp.bfloat16)
     terms_first = weight_terms(grad_raw, normal1, split_count)
-    terms_first = terms_first.reshape(split_count, cycle_size, -1, part_width)
-    terms_first = terms_first.at[:, :, pad_q + wide_k, : 2 * gain_size].set(gain_terms[None])
-
-    terms_first = terms_first.reshape(split_count * cycle_size, -1, part_width)
-    sum_first = jnp.concatenate(
-        scatter([terms_first[:, :half], terms_first[:, half:]], (YX, XY), True, 5, "scatter_first")
-    )
+    terms_first = terms_first.reshape(split_count, cycle_size, -1, wide_part)
+    terms_first = terms_first.at[:, :, pad_q + wide_k, : 2 * pad_o].set(gain_terms[None])
+    terms_first = terms_first.reshape(split_count * cycle_size, -1, wide_part)
+    (sum_first,) = scatter([terms_first], first_chunks, True, 5, "scatter_first")
     start_k, start_v = pad_q, pad_q + pad_k
     gain_sums = sum_first[pad_q + wide_k]
+
+    def model_sum(total):
+        return gathered_spread(total, wide_o, pad_o)
+
+    def rows_of(values):
+        return open_up(values, wide_o, 0).reshape(seq_count, block_len, model_width)
+
     return (
-        output.reshape(seq_count, block_len, model_width),
-        grad_input,
-        sum_first[:wide_q].T,
-        sum_first[start_k : start_k + wide_k].T,
-        sum_first[start_v : start_v + wide_v].T,
-        sum_out[:wide_o].T,
-        sum_gate[:wide_g].T,
-        sum_up[:wide_u].T,
-        sum_down[:wide_d].T,
+        rows_of(output),
+        rows_of(grad_input),
+        model_sum(sum_first[:wide_q]),
+        model_sum(sum_first[start_k : start_k + wide_k]),
+        model_sum(sum_first[start_v : start_v + wide_v]),
+        sum_out[:wide_o, :part_width].T,
+        model_sum(sum_gate[:wide_g]),
+        model_sum(sum_up[:wide_g]),
+        gathered_spread(sum_down[:wide_o], wide_g, pad_g),
         gain_sums[:gain_size],
-        gain_sums[gain_size : 2 * gain_size],
+        gain_sums[pad_o : pad_o + gain_size],
     )
 
 

time: 430 us -> 377 us (0.88)
  matrix products: 33.6 us -> 4.13 us
  local copies, waits for them, and re-layouts: 62.1 us -> 45.2 us
  other arithmetic: 19 us -> 11.8 us
    pallas_call x6 -> x7, Pallas kernels: 289 us -> 308 us  [the longest x3 144 us: scatter(): pl.pallas_call(functools.partial(scatter_kernel, depth, use_x, chunks, wo...]
    dot_general x10 -> x2, matrix products: 21.2 us -> 2.52 us  [backward_dot(): jnp.dot(grads, weights[i], preferred_element_type=jnp.float32)]
    pallas_call x5 -> x1, Pallas kernels: 23.3 us -> 4.83 us  [weight_terms(): pl.pallas_call(terms_kernel, out_shape=jax.ShapeDtypeStruct((split_count,...]
    reshape x6 -> x23, local copies, waits for them, and re-layouts: 1.84 us -> 12.9 us  [the longest x5 4.09 us: gathered_spread(): return pieces[:, :wide].reshape(-1, total.shape[0])]
    dot_general x10 -> x2, matrix products: 12.4 us -> 1.61 us  [forward_dot(): lax.dot_general(values[:, i * part:(i + 1) * part], weights[i], (((1,), (...]
    slice x4 -> x1, local copies, waits for them, and re-layouts: 10.9 us -> 2.49 us  [forward_dot(): weights[i]]
    unnamed x124 -> x37, local copies, waits for them, and re-layouts: 8.23 us -> 0.43 us
    concatenate x6 -> x1, local copies, waits for them, and re-layouts: 6.49 us -> 0.67 us  [local(): jnp.concatenate([term_gain1.reshape(cycle_size, pad_o), term_gain2.reshap...]
where the time goes in v3:
time: 377 us; the launch traced here: 376 us
  Pallas kernels  313 us (83%)
  local copies, waits for them, and re-layouts  45.2 us (12%)
  other arithmetic  11.8 us (3%)
  matrix products  4.13 us (1%)
    pallas_call x3, Pallas kernels, scatter(): pl.pallas_call(functools.partial(scatter_kernel, depth, use_x, chunks, wo...  144 us
    pallas_call x3, Pallas kernels, gather(): pl.pallas_call(functools.partial(gather_kernel, depth, use_x, chunks, wor...  135 us
    pallas_call x1, Pallas kernels, mlp(): pl.pallas_call(functools.partial(mlp_kernel, real_width), out_shape=[jax....  29.4 us

profile of v3, /device:TPU:0, one launch (start us, length us, event | category | flops | bytes accessed | tf_op | source)
XLA Modules:
  0.0 375.5 jit_solution(12562406590768234912)
XLA Ops:
  0.7 0.8 fusion.26
  1.5 0.8 reshape.406
  2.5 0.8 reshape.408
  3.5 0.8 fusion.24
  4.2 1.5 pad.82.refs_0_
  5.7 1.0 reshape.404
  6.9 0.7 fusion.16.refs_0_
  7.6 1.6 pad.85.refs_3_
  9.2 1.0 reshape_reshape.42
  10.3 0.5 add_rsqrt_fusion
  11.0 0.9 copy.66.grad_ref
  12.2 0.9 reshape.401
  13.5 0.9 reshape.403
  14.5 1.0 copy.56.resid_ref
  15.5 1.0 copy.80
  16.5 29.5 %gather_first.1 = bf16[32,128,512]{2,1,0:T(8,128)(2,1)} custom-call(bf16[128,512]{1,0:T(8,128)(2,1)} %fusion.16.refs_0_), custom_call_target="tpu_custom_call" | custom-call | tf_op jit(solution)/shard_map/gather_first/pallas_call | solution.py:288
  46.0 0.8 slice.157
  46.9 0.7 reshape.444.gain_ref
  47.7 1.9 fusion.13.values
  49.6 1.2 multiply_convert_fusion.1
  50.7 2.5 fusion.30
  53.2 0.8 fusion.19
  54.0 0.8 convolution_add_fusion
  54.9 0.3 copy.83
  55.7 0.8 copy.59
  57.4 0.9 pad.96.refs_5_
  58.3 22.2 %gather_pairs.1 = bf16[16,640,128]{2,1,0:T(8,128)(2,1)} custom-call(bf16[640,128]{1,0:T(8,128)(2,1)} %bitcast.215), custom_call_target="tpu_custom_call" | custom-call | tf_op jit(solution)/shard_map/gather_pairs/pallas_call | solution.py:288
  80.5 82.9 %gather_rest_attend.1 = (bf16[32,64,512]{2,1,0:T(8,128)(2,1)}, bf16[32,160,512]{2,1,0:T(8,128)(2,1)}, bf16[32,160,512]{2,1,0:T(8,128)(2,1)}, bf16[32,64,1280]{2,...) custom-call(bf16[64,512]{1,0:T(8,128)(2,1)} %pad.82.refs_0_, bf16[160,512]{1,0:T(8,128)(2,1)} %bitcast.213, ...), custom_call_target="tpu_custom_call" | custom-call | tf_op jit(solution)/shard_map/gather_rest_attend/pallas_call | solution.py:288
  163.4 1.1 fusion.11
  164.5 0.9 copy.81.attended_ref
  165.3 29.4 %mlp.1 = (bf16[128,1024]{1,0:T(8,128)(2,1)}, f32[128,1024]{1,0:T(8,128)}, bf16[128,1024]{1,0:T(8,128)(2,1)}, f32[1,1024]{1,0:T(1,128)}, bf16[2,1024,512]{2,1,0:T...) custom-call(bf16[128,1024]{1,0:T(8,128)(2,1)} %copy.81.attended_ref, ...), custom_call_target="tpu_custom_call" | custom-call | tf_op jit(solution)/shard_map/mlp/pallas_call | solution.py:881
  194.7 1.1 copy.67
  195.8 0.7 reshape_reshape.46
  196.6 0.7 convert_reduce_fusion
  197.3 0.7 concatenate.73
  198.0 1.1 copy.82
  199.1 1.1 fusion.12
  200.2 0.6 reshape.425.refs_8_
  201.1 1.0 pad.99.refs_6_
  202.1 92.6 %scatter_rest_retrace.1 = (f32[64,512]{1,0:T(8,128)}, f32[160,512]{1,0:T(8,128)}, f32[160,512]{1,0:T(8,128)}, f32[64,1280]{1,0:T(8,128)}, f32[5,384,128]{2,1,0:T(8,128)}, /*index=5*/bf16[16,5,128,128]{3,2,1,0:T(8,128)(2,1)}) custom-call(bf16[16,2,64,512]{3,2,1,0:T(8,128)(2,1)} %bitcast.195, bf16[16,2,160,512]{3,2,1,0:T(8,128)(2,1)} %bitcast.182, ...), custom_call_target="tpu_custom_call" | custom-call | tf_op jit(solution)/shard_map/scatter_rest_retrace/pallas_call | solution.py:542
  294.8 1.5 copy.70
  296.4 0.7 pad_maximum_fusion.2
  297.1 23.2 %scatter_pairs.1 = f32[640,128]{1,0:T(8,128)} custom-call(bf16[8,2,640,128]{3,2,1,0:T(8,128)(2,1)} %bitcast.190), custom_call_target="tpu_custom_call" | custom-call | tf_op jit(solution)/shard_map/scatter_pairs/pallas_call | solution.py:542
  320.3 1.2 copy.72
  321.5 1.0 convert_element_type.131
  322.6 1.6 slice_bitcast_fusion.2
  324.5 0.7 slice_bitcast_fusion.1
  325.9 0.6 fusion.5
  326.5 1.4 copy_bitcast_fusion.grads
  327.9 2.1 convolution_bitcast_fusion
  330.1 0.4 convolution_bitcast_fusion.1
  331.0 0.4 multiply_reduce_fusion
  331.8 0.7 reshape_reshape.54
  332.7 0.9 reshape.439
  333.8 0.9 reshape.441
  334.8 4.8 %weight_terms.1 = bf16[2,2048,512]{2,1,0:T(8,128)(2,1)} custom-call(bf16[128,2048]{1,0:T(8,128)(2,1)} %copy_bitcast_fusion.grads, bf16[2,128,512]{2,1,0:T(8,128)(2,1)} %fusion.13.values), custom_call_target="tpu_custom_call" | custom-call | flops 536870912 | bytes 4194304 | tf_op jit(solution)/shard_map/weight_terms/pallas_call | solution.py:621
  339.6 1.9 scatter.4
  341.5 28.5 %scatter_first.1 = f32[128,512]{1,0:T(8,128)} custom-call(bf16[16,2,128,512]{3,2,1,0:T(8,128)(2,1)} %bitcast.176), custom_call_target="tpu_custom_call" | custom-call | tf_op jit(solution)/shard_map/scatter_first/pallas_call | solution.py:542
  370.0 1.3 slice_bitcast_fusion.6
  371.3 0.8 slice_bitcast_fusion.4
  372.1 0.9 slice_bitcast_fusion.3
  373.1 0.7 reshape.437
  373.9 0.7 reshape.435
  374.7 0.8 reshape.433
  (95 shorter events, 5.8 us)
Async XLA Ops:
  0.6 11.2 %copy-start.9 = (bf16[480,160]{0,1:T(8,128)(2,1)S(1)}, bf16[480,160]{0,1:T(8,128)(2,1)}, u32[]{:S(2)}) copy-start(bf16[480,160]{0,1:T(8,128)(2,1)} %param.19) | copy-start | bytes 460804
  0.7 10.2 %copy-start.8 = (bf16[1,128,960]{1,2,0:T(8,128)(2,1)S(1)}, bf16[1,128,960]{1,2,0:T(8,128)(2,1)}, u32[]{:S(2)}) copy-start(bf16[1,128,960]{1,2,0:T(8,128)(2,1)} %param.14) | copy-start | bytes 737284
  5.7 7.4 %copy-start.10 = (bf16[480,160]{0,1:T(8,128)(2,1)S(1)}, bf16[480,160]{0,1:T(8,128)(2,1)}, u32[]{:S(2)}) copy-start(bf16[480,160]{0,1:T(8,128)(2,1)} %param.20) | copy-start | bytes 460804
  10.2 4.3 %copy-start.2 = (bf16[128,16,60]{0,2,1:T(8,128)(2,1)}, bf16[128,16,60]{0,2,1:T(8,128)(2,1)S(1)}, u32[]{:S(2)}) copy-start(bf16[128,16,60]{0,2,1:T(8,128)(2,1)S(1)} %reshape_reshape.42) | copy-start | bytes 737284
  10.3 0.5 copy-start.16
  47.6 5.6 %copy-start.12 = (f32[1024]{0:T(1024)}, f32[1024]{0:T(1024)S(1)}, u32[]{:S(2)}) copy-start(f32[1024]{0:T(1024)S(1)} %reshape.443) | copy-start | bytes 12292
  54.9 0.7 copy-start.11
  320.3 4.2 %copy-start.5 = (f32[64,1280]{1,0:T(8,128)S(1)}, f32[64,1280]{1,0:T(8,128)}, u32[]{:S(2)}) copy-start(f32[64,1280]{1,0:T(8,128)} %get-tuple-element.62) | copy-start | bytes 983044
  326.5 3.5 copy-start
  330.0 1.0 copy-start.3
  330.0 0.9 copy-start.15
  330.0 1.3 copy-start.14
  330.0 1.4 copy-start.17
  330.0 1.4 copy-start.1
  330.1 1.4 copy-start.4
  330.1 1.4 copy-start.13
  330.5 2.0 copy-start.7
  331.3 2.3 copy-start.6

commit v4 on v3

--- a/solution.py
+++ b/solution.py
@@ -105,7 +105,8 @@
 
 class Chunk:
     def __init__(self, array, start, rows, route):
-        self.array, self.start, self.rows, self.route = array, start, rows, route
+        self.array, self.start, self.rows, self.route = array, start, rows, route[:2]
+        self.late = len(route) > 2
         self.span = pl.ds(start, rows)
 
 
@@ -119,11 +120,13 @@
 
 
 def gather_kernel(depth, use_x, chunks, work, *refs):
-    total, count = chunks[-1].array + 1, len(chunks)
+    total, count = 1 + max(chunk.array for chunk in chunks), len(chunks)
     routes = [chunk.route for chunk in chunks]
+    early = [k for k in range(count) if not chunks[k].late]
+    late = [k for k in range(count) if chunks[k].late]
     ins, work_ins, refs = refs[:total], refs[total : total + work.ins], refs[total + work.ins :]
     outs, work_outs, refs = refs[:total], refs[total : total + work.outs], refs[total + work.outs :]
-    recv, send_z, send_p, send_q, send_c, local_sem = refs
+    recv, send_z, send_p, send_q, send_c, local_sem, send_l = refs
     place = Place(depth, use_x)
     place.barrier()
 
@@ -141,7 +144,23 @@
             device_id_type=MESH,
         )
 
+    def forward_late(k, rel_p, rel_q, z0, up, src=None):
+        pid = place.piece(routes[k], rel_p, rel_q, z0)
+        sem = send_l.at[late.index(k), 2 * rel_p + rel_q, 0 if up else 1, z0]
+        return copy(k, pid, sem, "up" if up else "down", src)
+
+    def both_late(k, rel_p, rel_q):
+        @pl.when(place.has_up)
+        def _():
+            forward_late(k, rel_p, rel_q, place.z, True).start()
+
+        @pl.when(place.has_down)
+        def _():
+            forward_late(k, rel_p, rel_q, place.z, False).start()
+
     def forward_z(k, z0, up, src=None):
+        if chunks[k].late:
+            return forward_late(k, 0, 0, z0, up, src)
         pid = place.piece(routes[k], 0, 0, z0)
         return copy(k, pid, send_z.at[k, 0 if up else 1, z0], "up" if up else "down", src)
 
@@ -179,9 +198,32 @@
         mine.start()
         own.append(mine)
 
+    for k in late:
+        pid = place.piece(routes[k], 1, 0, place.z)
+        arrived(k, pid)
+        forward_q(k, 1, place.z).start()
+        both_late(k, 1, 0)
+        forward_c(k, pid).start()
+    for k in late:
+        for rel_p in (0, 1):
+            pid = place.piece(routes[k], rel_p, 1, place.z)
+            arrived(k, pid)
+            both_late(k, rel_p, 1)
+            forward_c(k, pid).start()
+
     def step(d, carry):
         def from_z(z0, above):
-            for k in range(count):
+            for k in late:
+                for rel_p, rel_q in ((0, 0), (1, 0), (0, 1), (1, 1)):
+                    pid = place.piece(routes[k], rel_p, rel_q, z0)
+                    arrived(k, pid)
+
+                    @pl.when(place.has_down if above else place.has_up)
+                    def _():
+                        forward_late(k, rel_p, rel_q, z0, not above).start()
+
+                    forward_c(k, pid).start()
+            for k in early:
                 pid = place.piece(routes[k], 0, 0, z0)
                 arrived(k, pid)
                 if above:
@@ -202,7 +244,7 @@
                 forward_c(k, pid).start()
 
         def from_p(z0, above):
-            for k in range(count):
+            for k in early:
                 if routes[k][0] is not None:
                     pid = place.piece(routes[k], 1, 0, z0)
                     arrived(k, pid)
@@ -210,7 +252,7 @@
                     forward_c(k, pid).start()
 
         def from_q(rel_p, z0, above):
-            for k in range(count):
+            for k in early:
                 if routes[k][0] is not None or not rel_p:
                     pid = place.piece(routes[k], rel_p, 1, z0)
                     arrived(k, pid)
@@ -237,7 +279,24 @@
         work.body(item, place.ctx, *work_ins, *work_outs)
 
     def finish(z0, carry):
-        for k in range(count):
+        for k in late:
+            for rel_p, rel_q in ((0, 0), (1, 0), (0, 1), (1, 1)):
+
+                @pl.when(place.has_up & (z0 <= place.z))
+                def _():
+                    forward_late(k, rel_p, rel_q, z0, True).wait_send()
+
+                @pl.when(place.has_down & (z0 >= place.z))
+                def _():
+                    forward_late(k, rel_p, rel_q, z0, False).wait_send()
+
+            @pl.when(z0 == place.z)
+            def _():
+                forward_p(k, z0).wait_send()
+                forward_q(k, 0, z0).wait_send()
+                forward_q(k, 1, z0).wait_send()
+
+        for k in early:
 
             @pl.when(place.has_up & (z0 <= place.z))
             def _():
@@ -299,6 +358,7 @@
             dma((count, 2, depth)),
             dma((count, pieces)),
             dma((count,)),
+            dma((max(1, sum(chunk.late for chunk in chunks)), 4, 2, depth)),
         ],
         compiler_params=pltpu.CompilerParams(
             collective_id=collective_id, has_side_effects=True, vmem_limit_bytes=VMEM_LIMIT
@@ -322,12 +382,15 @@
 
 
 def scatter_kernel(depth, use_x, chunks, work, *refs):
-    total, count = chunks[-1].array + 1, len(chunks)
+    total, count = 1 + max(chunk.array for chunk in chunks), len(chunks)
     routes = [chunk.route for chunk in chunks]
+    early = [k for k in range(count) if not chunks[k].late]
+    late = [k for k in range(count) if chunks[k].late]
     ins, work_ins, refs = refs[:total], refs[total : total + work.ins], refs[total + work.ins :]
     outs, work_outs, refs = refs[:total], refs[total : total + work.outs], refs[total + work.outs :]
     whole = [refs[i * total : (1 + i) * total] for i in range(5)]
-    load_sem, c_send, c_recv, q_send, q_recv, p_send, p_recv, z_send, z_recv = refs[5 * total :]
+    land_l, refs = refs[5 * total : 5 * total + len(late)], refs[5 * total + len(late) :]
+    load_sem, c_send, c_recv, q_send, q_recv, p_send, p_recv, z_send, z_recv, l_send, l_recv = refs
 
     class View:
         def __init__(self, ref, span):
@@ -401,6 +464,57 @@
             "up" if up else "down",
         )
 
+    def send_late(k, rel_p, rel_q, z0, up):
+        target = z0 if up else jnp.where(z0 == place.z - 1, depth, z0)
+        i, rel = late.index(k), 2 * rel_p + rel_q
+        return remote(
+            own[k].at[place.piece(routes[k], rel_p, rel_q, z0)],
+            land_l[i].at[rel, target],
+            l_send.at[i, rel, z0],
+            l_recv.at[i, rel, target],
+            "up" if up else "down",
+        )
+
+    def late_child(k, rel_p, rel_q, index):
+        i, rel = late.index(k), 2 * rel_p + rel_q
+        child = land_l[i].at[rel, index]
+        pltpu.make_async_copy(child, child, l_recv.at[i, rel, index]).wait()
+        return child
+
+    def add_children(k, rel_p, rel_q, total_ref):
+        @pl.when(place.has_down)
+        def _():
+            add_up(total_ref, [total_ref, late_child(k, rel_p, rel_q, place.z)], rows[k])
+
+        @pl.when(place.has_up)
+        def _():
+            add_up(total_ref, [total_ref, late_child(k, rel_p, rel_q, depth)], rows[k])
+
+    def late_along(z0, above):
+        for k in late:
+            for rel_p, rel_q in ((1, 1), (0, 1), (1, 0), (0, 0)):
+                pid = place.piece(routes[k], rel_p, rel_q, z0)
+                send_c(k, pid).wait_recv()
+                sources = [own[k].at[pid], part[k].at[pid]]
+                child = place.has_down if above else place.has_up
+
+                @pl.when(child)
+                def _():
+                    add_up(own[k].at[pid], sources + [late_child(k, rel_p, rel_q, z0)], rows[k])
+
+                @pl.when(jnp.logical_not(child))
+                def _():
+                    add_up(own[k].at[pid], sources, rows[k])
+
+                send_late(k, rel_p, rel_q, z0, above).start()
+
+    def late_here(k, rel_p, rel_q, target, extra):
+        pid = place.piece(routes[k], rel_p, rel_q, place.z)
+        send_c(k, pid).wait_recv()
+        target = own[k].at[pid] if target is None else target
+        add_up(target, [own[k].at[pid], part[k].at[pid]] + extra, rows[k])
+        add_children(k, rel_p, rel_q, target)
+
     def wait_z(k, index):
         pltpu.make_async_copy(land_z[k].at[index], land_z[k].at[index], z_recv.at[k, index]).wait()
 
@@ -420,7 +534,7 @@
 
     def step(s, carry):
         def leaf(z0, above):
-            for k in range(count):
+            for k in early:
                 for rel_p in (1, 0) if routes[k][0] is not None else (0,):
                     pid = place.piece(routes[k], rel_p, 1, z0)
                     send_c(k, pid).wait_recv()
@@ -428,7 +542,7 @@
                     send_q(k, rel_p, z0).start()
 
         def middle(z0, above):
-            for k in range(count):
+            for k in early:
                 if routes[k][0] is not None:
                     pid = place.piece(routes[k], 1, 0, z0)
                     send_c(k, pid).wait_recv()
@@ -451,7 +565,7 @@
             return pid, sources
 
         def along(z0, above):
-            for k in range(count):
+            for k in early:
                 pid, sources = sources_of(k, z0)
                 child = place.has_down if above else place.has_up
 
@@ -466,6 +580,26 @@
 
                 send_z(k, z0, above).start()
 
+        if late:
+
+            @pl.when(s < depth - 1)
+            def _():
+                both_sides(place, depth - 1 - s, late_along)
+
+            @pl.when(s == depth - 1)
+            def _():
+                for k in late:
+                    for rel_p in (1, 0):
+                        late_here(k, rel_p, 1, None, [])
+                        send_q(k, rel_p, place.z).start()
+
+            @pl.when(s == depth)
+            def _():
+                for k in late:
+                    send_q(k, 1, place.z).wait_recv()
+                    late_here(k, 1, 0, None, [land_q[k].at[1, place.z]])
+                    send_p(k, place.z).start()
+
         both_sides(place, depth - 1 - s, leaf)
 
         if work.count:
@@ -484,7 +618,12 @@
 
         @pl.when(s == depth + 1)
         def _():
-            for k in range(count):
+            for k in late:
+                send_q(k, 0, place.z).wait_recv()
+                send_p(k, place.z).wait_recv()
+                extra = [land_q[k].at[0, place.z], land_p[k].at[place.z]]
+                late_here(k, 0, 0, sums[k], extra)
+            for k in early:
                 _, sources = sources_of(k, place.z)
                 add_up(sums[k], sources, rows[k])
 
@@ -505,7 +644,24 @@
         work.body(item, place.ctx, *work_ins, *work_outs)
 
     def finish(z0, carry):
-        for k in range(count):
+        for k in late:
+            for rel_p, rel_q in ((1, 1), (0, 1), (1, 0), (0, 0)):
+
+                @pl.when(z0 > place.z)
+                def _():
+                    send_late(k, rel_p, rel_q, z0, True).wait_send()
+
+                @pl.when(z0 < place.z)
+                def _():
+                    send_late(k, rel_p, rel_q, z0, False).wait_send()
+
+            @pl.when(z0 == place.z)
+            def _():
+                send_p(k, z0).wait_send()
+                send_q(k, 0, z0).wait_send()
+                send_q(k, 1, z0).wait_send()
+
+        for k in early:
             send_q(k, 0, z0).wait_send()
             if routes[k][0] is not None:
                 send_q(k, 1, z0).wait_send()
@@ -539,6 +695,7 @@
     shapes = [a.shape[1:] for a in arrays]
     pairs = [a.reshape(pieces, 2, *s) for a, s in zip(arrays, shapes)]
     bf16 = jnp.bfloat16
+    late = [chunk for chunk in chunks if chunk.late]
     return pl.pallas_call(
         functools.partial(scatter_kernel, depth, use_x, chunks, work),
         out_shape=[jax.ShapeDtypeStruct(s, jnp.float32) for s in shapes] + work.shapes,
@@ -550,6 +707,7 @@
         + [pltpu.VMEM((2, depth, *s), bf16) for s in shapes]
         + [pltpu.VMEM((depth, *s), bf16) for s in shapes]
         + [pltpu.VMEM((depth + 1, *s), bf16) for s in shapes]
+        + [pltpu.VMEM((4, depth + 1, c.rows, *shapes[c.array][1:]), bf16) for c in late]
         + [
             dma((total,)),
             dma((count, pieces)),
@@ -560,6 +718,8 @@
             dma((count, depth)),
             dma((count, depth)),
             dma((count, depth + 1)),
+            dma((max(1, len(late)), 4, depth)),
+            dma((max(1, len(late)), 4, depth + 1)),
         ],
         compiler_params=pltpu.CompilerParams(
             collective_id=collective_id, has_side_effects=True, vmem_limit_bytes=VMEM_LIMIT
@@ -577,6 +737,7 @@
 
 
 XY, YX, ONLY_Y = ("x", "y"), ("y", "x"), (None, "y")
+XYZ, YXZ = ("x", "y", "z"), ("y", "x", "z")
 def halves(values, split_count):
     return values.reshape(values.shape[0], split_count, values.shape[1] // split_count)
 
@@ -719,6 +880,39 @@
         return carry
 
     lax.fori_loop(needed, blocks // PIECES_PER_BLOCK, clear, 0)
+
+
+def one_hot(rows, columns, wide, pad):
+    row = lax.broadcasted_iota(jnp.int32, (rows, columns), 0)
+    column = lax.broadcasted_iota(jnp.int32, (rows, columns), 1)
+    place = column // pad * wide + column % pad
+    chosen = (row == place) & (column % pad < wide)
+    return jnp.where(chosen, 1.0, 0.0).astype(jnp.bfloat16)
+
+
+def pieces_kernel(plans, *refs):
+    ins, outs = refs[: len(plans)], refs[len(plans) :]
+    for (target, start, wide, pad), weight in zip(plans, ins):
+        rows, columns = weight.shape
+        end = padded(columns)
+        lanes = outs[target].shape[1]
+        turn = one_hot(end, columns, columns, columns)
+        piece = turned(turn, weight[...]).astype(jnp.bfloat16)
+        if wide != pad or lanes != rows:
+            piece = plain(piece, one_hot(rows, lanes, wide, pad)).astype(jnp.bfloat16)
+        outs[target][start : start + end, :] = piece
+
+
+def make_pieces(weights, plans, shapes):
+    vmem = pl.BlockSpec(memory_space=pltpu.VMEM)
+    return pl.pallas_call(
+        functools.partial(pieces_kernel, plans),
+        out_shape=[jax.ShapeDtypeStruct(shape, jnp.bfloat16) for shape in shapes],
+        in_specs=[vmem] * len(weights),
+        out_specs=[vmem] * len(shapes),
+        compiler_params=pltpu.CompilerParams(vmem_limit_bytes=VMEM_LIMIT),
+        name="make_pieces",
+    )(*weights)
 
 
 def wait_all(copies):
@@ -926,17 +1120,12 @@
     sine_table = jnp.tile(sine_table, (seq_count, 1))
     wide_q, wide_k, wide_v = w_query.shape[1], w_key.shape[1], w_value.shape[1]
     wide_o, wide_g = w_out.shape[1], w_gate.shape[1]
-    pad_q, pad_k, pad_v = padded(wide_q), padded(wide_k + 1), padded(wide_v)
+    pad_q, pad_k, pad_v = padded(wide_q), padded(wide_k), padded(wide_v)
     pad_o, pad_g = padded(wide_o), padded(wide_g)
     part_width = w_query.shape[0]
     wide_part = part_width // wide_o * pad_o
     gain_size = gain_attn.shape[0]
 
-    def spread(weight, wide, pad):
-        pieces = weight.reshape(-1, wide, weight.shape[1])
-        pieces = jnp.pad(pieces, ((0, 0), (0, pad - wide), (0, 0)))
-        return pieces.reshape(-1, weight.shape[1]).T
-
     def gathered_spread(total, wide, pad):
         pieces = total.T.reshape(-1, pad, total.shape[0])
         return pieces[:, :wide].reshape(-1, total.shape[0])
@@ -949,24 +1138,32 @@
         pieces = values.reshape(row_count, cycle_size, wide_o)
         return jnp.pad(pieces, ((0, 0), (0, 0), (0, pad_o - wide_o))).reshape(row_count, -1)
 
-    def model(weight):
-        return spread(weight, wide_o, pad_o)
-
-    gain_row = jnp.pad(
-        jnp.concatenate([jnp.pad(g, (0, pad_o - gain_size)) for g in (gain_attn, gain_mlp)]),
-        (0, wide_part - 2 * pad_o),
-    )[None, :]
-    first_piece = jnp.concatenate(
+    gain_row = jnp.concatenate([jnp.pad(g, (0, pad_o - gain_size)) for g in (gain_attn, gain_mlp)])
+    gain_piece = jnp.pad(gain_row[None, :], ((0, padded(1) - 1), (0, 0)))
+    hidden_part = w_down.shape[0] // wide_g * pad_g
+    first_rows = pad_q + pad_k + pad_v
+    first_piece, out_piece, gate_piece, up_piece, down_piece = make_pieces(
+        [w_query, w_key, w_value, w_out, w_gate, w_up, w_down],
+        (
+            (0, 0, wide_o, pad_o),
+            (0, pad_q, wide_o, pad_o),
+            (0, pad_q + pad_k, wide_o, pad_o),
+            (1, 0, part_width, wide_part),
+            (2, 0, wide_o, pad_o),
+            (3, 0, wide_o, pad_o),
+            (4, 0, wide_g, pad_g),
+        ),
         [
-            pad_rows(model(w_query), pad_q),
-            pad_rows(jnp.concatenate([model(w_key), gain_row], axis=0), pad_k),
-            pad_rows(model(w_value), pad_v),
+            (first_rows, wide_part),
+            (pad_o, wide_part),
+            (pad_g, wide_part),
+            (pad_g, wide_part),
+            (pad_o, hidden_part),
         ],
-        axis=0,
-    )
-    first_chunks = cut(0, first_piece.shape[0], 4, (YX, XY))
-    (first,) = gather([first_piece], first_chunks, True, 0, "gather_first")
-    gain_rows = first[:cycle_size, pad_q + wide_k, : 2 * pad_o]
+    )
+    first_chunks = cut(0, first_rows, 4, (YX, XY)) + cut(1, padded(1), 1, (XY,))
+    first, gains = gather([first_piece, gain_piece], first_chunks, True, 0, "gather_first")
+    gain_rows = gains[:cycle_size, 0]
     gain_first = gain_rows[:, :pad_o].reshape(1, -1).astype(jnp.float32)
     gain_second = gain_rows[:, pad_o:].reshape(1, -1).astype(jnp.float32)
     first = first.reshape(split_count, -1, wide_part)
@@ -998,20 +1195,16 @@
 
     query_grouped = jnp.pad(by_group(query_rot), ((0, 0), (0, 0), (0, head_size)))
     width = repeat_count * row_count
-    out_piece = jnp.pad(w_out.T, ((0, pad_o - wide_o), (0, wide_part - part_width)))
+    late_rows = padded(pad_g // 8)
+    main_rows = pad_g - late_rows
     rest_chunks = (
-        cut(0, pad_o, 2, (XY, YX))
-        + cut(1, pad_g, 1, (XY,))
-        + cut(2, pad_g, 1, (YX,))
+        cut(0, pad_o, 2, (XYZ, YXZ))
+        + [Chunk(1, main_rows, late_rows, XYZ), Chunk(2, main_rows, late_rows, YXZ)]
+        + [Chunk(1, 0, main_rows, XY), Chunk(2, 0, main_rows, YX)]
         + cut(3, pad_o, 2, (XY, YX))
     )
     out_w, gate_w, up_w, down_w, attended_turned, logsum = gather(
-        [
-            out_piece,
-            pad_rows(model(w_gate), pad_g),
-            pad_rows(model(w_up), pad_g),
-            pad_rows(spread(w_down, wide_g, pad_g), pad_o),
-        ],
+        [out_piece, gate_piece, up_piece, down_piece],
         rest_chunks,
         True,
         4,
@@ -1115,12 +1308,13 @@
         [term_gain1.reshape(cycle_size, pad_o), term_gain2.reshape(cycle_size, pad_o)], axis=-1
     ).astype(jnp.bfloat16)
     terms_first = weight_terms(grad_raw, normal1, split_count)
-    terms_first = terms_first.reshape(split_count, cycle_size, -1, wide_part)
-    terms_first = terms_first.at[:, :, pad_q + wide_k, : 2 * pad_o].set(gain_terms[None])
-    terms_first = terms_first.reshape(split_count * cycle_size, -1, wide_part)
-    (sum_first,) = scatter([terms_first], first_chunks, True, 5, "scatter_first")
+    gain_terms = jnp.pad(gain_terms[:, None, :], ((0, 0), (0, padded(1) - 1), (0, 0)))
+    gain_terms = jnp.tile(gain_terms, (split_count, 1, 1))
+    sum_first, gain_sums = scatter(
+        [pieces_of(terms_first), gain_terms], first_chunks, True, 5, "scatter_first"
+    )
+    gain_sums = gain_sums[0]
     start_k, start_v = pad_q, pad_q + pad_k
-    gain_sums = sum_first[pad_q + wide_k]
 
     def model_sum(total):
         return gathered_spread(total, wide_o, pad_o)

time: 377 us -> 392 us (1.040)
  Pallas kernels: 313 us -> 327 us
    unnamed x37 -> x47, local copies, waits for them, and re-layouts: 0.43 us -> 12.4 us
    pallas_call x3, Pallas kernels: 135 us -> 142 us  [gather(): pl.pallas_call(functools.partial(gather_kernel, depth, use_x, chunks, wor...]
    reshape x10 -> x0, local copies, waits for them, and re-layouts: 5.46 us -> none  [the longest x5 3.34 us: spread(): pieces = weight.reshape(-1, wide, weight.shape[1])]
where the time goes in v4:
time: 392 us; the launch traced here: 391 us
  Pallas kernels  327 us (83%)
  local copies, waits for them, and re-layouts  47 us (12%)
  other arithmetic  11 us (3%)
  matrix products  4.11 us (1%)
    pallas_call x3, Pallas kernels, scatter(): pl.pallas_call(functools.partial(scatter_kernel, depth, use_x, chunks, wo...  147 us
    pallas_call x3, Pallas kernels, gather(): pl.pallas_call(functools.partial(gather_kernel, depth, use_x, chunks, wor...  142 us
    pallas_call x1, Pallas kernels, mlp(): pl.pallas_call(functools.partial(mlp_kernel, real_width), out_shape=[jax....  29.4 us
    unnamed x47, local copies, waits for them, and re-layouts  12.4 us

profile of v4, /device:TPU:0, one launch (start us, length us, event | category | flops | bytes accessed | tf_op | source)
XLA Modules:
  0.0 390.7 jit_solution(13370189361104975725)
XLA Ops:
  0.7 0.8 fusion.20
  1.5 0.6 pad.47.refs_1_
  2.1 0.7 fusion.17
  2.9 1.6 copy.72.refs_0_
  4.5 1.5 copy.73.refs_1_
  6.0 1.5 copy.74.refs_2_
  7.6 1.6 copy.75.refs_3_
  9.2 1.7 copy.76.refs_4_
  10.9 1.7 copy.77.refs_5_
  12.7 1.0 reshape_reshape.42
  13.7 0.7 copy-done.1
  14.5 0.5 copy-done.17
  15.0 0.5 add_rsqrt_fusion
  15.6 0.9 copy.89.grad_ref
  16.5 0.9 copy.78.refs_6_
  17.4 3.7 make_pieces.1
  21.1 1.0 pad_convert_fusion
  22.1 1.0 copy.79.resid_ref
  23.1 1.0 copy.103
  24.1 30.6 %gather_first.1 = (bf16[32,128,512]{2,1,0:T(8,128)(2,1)}, bf16[32,16,128]{2,1,0:T(8,128)(2,1)}) custom-call(bf16[128,512]{1,0:T(8,128)(2,1)} %get-tuple-element.44.refs_0_, bf16[16,128]{1,0:T(8,128)(2,1)} %pad.47.refs_1_), custom_call_target="tpu_custom_call" | custom-call | tf_op jit(solution)/shard_map/gather_first/pallas_call | solution.py:347
  54.8 0.8 slice.126
  55.6 0.7 reshape.378.gain_ref
  56.4 1.9 fusion.13.values
  58.3 1.2 multiply_convert_fusion.1
  59.5 2.5 fusion.24
  62.0 0.8 fusion.15
  62.8 0.8 convolution_add_fusion
  64.5 0.8 copy.82
  66.1 0.9 pad.48.refs_5_
  67.0 22.5 %gather_pairs.1 = bf16[16,640,128]{2,1,0:T(8,128)(2,1)} custom-call(bf16[640,128]{1,0:T(8,128)(2,1)} %bitcast.190), custom_call_target="tpu_custom_call" | custom-call | tf_op jit(solution)/shard_map/gather_pairs/pallas_call | solution.py:347
  89.5 88.9 %gather_rest_attend.1 = (bf16[32,64,512]{2,1,0:T(8,128)(2,1)}, bf16[32,160,512]{2,1,0:T(8,128)(2,1)}, bf16[32,160,512]{2,1,0:T(8,128)(2,1)}, bf16[32,64,1280]{2,...) custom-call(bf16[64,512]{1,0:T(8,128)(2,1)} %get-tuple-element.40.refs_0_, ...), custom_call_target="tpu_custom_call" | custom-call | tf_op jit(solution)/shard_map/gather_rest_attend/pallas_call | solution.py:347
  178.4 1.1 fusion.11
  179.6 0.9 copy.105.attended_ref
  180.4 29.4 %mlp.1 = (bf16[128,1024]{1,0:T(8,128)(2,1)}, f32[128,1024]{1,0:T(8,128)}, bf16[128,1024]{1,0:T(8,128)(2,1)}, f32[1,1024]{1,0:T(1,128)}, bf16[2,1024,512]{2,1,0:T...) custom-call(bf16[128,1024]{1,0:T(8,128)(2,1)} %copy.105.attended_ref, ...), custom_call_target="tpu_custom_call" | custom-call | tf_op jit(solution)/shard_map/mlp/pallas_call | solution.py:1075
  209.8 1.2 copy.90
  211.0 0.7 reshape_reshape.46
  211.8 0.7 convert_reduce_fusion
  212.5 0.7 concatenate.68
  213.2 1.1 copy.106
  214.4 0.6 reshape.360.refs_8_
  215.3 1.0 pad.51.refs_6_
  216.3 93.5 %scatter_rest_retrace.1 = (f32[64,512]{1,0:T(8,128)}, f32[160,512]{1,0:T(8,128)}, f32[160,512]{1,0:T(8,128)}, f32[64,1280]{1,0:T(8,128)}, f32[5,384,128]{2,1,0:T(8,128)}, /*index=5*/bf16[16,5,128,128]{3,2,1,0:T(8,128)(2,1)}) custom-call(bf16[16,2,64,512]{3,2,1,0:T(8,128)(2,1)} %bitcast.172, bf16[16,2,160,512]{3,2,1,0:T(8,128)(2,1)} %bitcast.159, ...), custom_call_target="tpu_custom_call" | custom-call | tf_op jit(solution)/shard_map/scatter_rest_retrace/pallas_call | solution.py:699
  309.8 1.5 copy.93
  311.4 0.7 pad_maximum_fusion.2
  312.1 24.0 %scatter_pairs.1 = f32[640,128]{1,0:T(8,128)} custom-call(bf16[8,2,640,128]{3,2,1,0:T(8,128)(2,1)} %bitcast.167), custom_call_target="tpu_custom_call" | custom-call | tf_op jit(solution)/shard_map/scatter_pairs/pallas_call | solution.py:699
  336.2 1.2 copy.95
  337.4 1.0 convert_element_type.118
  338.5 0.7 slice_bitcast_fusion.2
  339.5 0.7 slice_bitcast_fusion.1
  340.9 0.6 fusion.5
  341.5 1.4 copy_bitcast_fusion.grads
  342.9 2.1 convolution_bitcast_fusion
  346.8 0.7 reshape_reshape.54
  347.6 0.7 tile.8
  348.4 0.9 reshape.373
  349.5 0.9 reshape.375
  350.4 4.8 %weight_terms.1 = bf16[2,2048,512]{2,1,0:T(8,128)(2,1)} custom-call(bf16[128,2048]{1,0:T(8,128)(2,1)} %copy_bitcast_fusion.grads, bf16[2,128,512]{2,1,0:T(8,128)(2,1)} %fusion.13.values), custom_call_target="tpu_custom_call" | custom-call | flops 536870912 | bytes 4194304 | tf_op jit(solution)/shard_map/weight_terms/pallas_call | solution.py:782
  355.2 29.9 %scatter_first.1 = (f32[128,512]{1,0:T(8,128)}, f32[16,128]{1,0:T(8,128)}) custom-call(bf16[16,2,128,512]{3,2,1,0:T(8,128)(2,1)} %bitcast.153, bf16[16,2,16,128]{3,2,1,0:T(8,128)(2,1)} %bitcast.191), custom_call_target="tpu_custom_call" | custom-call | tf_op jit(solution)/shard_map/scatter_first/pallas_call | solution.py:699
  385.1 1.3 slice_bitcast_fusion.6
  386.5 0.8 slice_bitcast_fusion.4
  387.3 0.9 slice_bitcast_fusion.3
  388.3 0.7 reshape.371
  389.1 0.7 reshape.369
  389.9 0.8 reshape.367
  (86 shorter events, 5.9 us)
Async XLA Ops:
  0.6 15.9 %copy-start.10 = (bf16[1280,60]{0,1:T(8,128)(2,1)S(1)}, bf16[1280,60]{0,1:T(8,128)(2,1)}, u32[]{:S(2)}) copy-start(bf16[1280,60]{0,1:T(8,128)(2,1)} %param.19) | copy-start | bytes 460804
  0.7 14.9 %copy-start.9 = (bf16[1,128,960]{1,2,0:T(8,128)(2,1)S(1)}, bf16[1,128,960]{1,2,0:T(8,128)(2,1)}, u32[]{:S(2)}) copy-start(bf16[1,128,960]{1,2,0:T(8,128)(2,1)} %param.12) | copy-start | bytes 737284
  13.7 0.7 copy-start.1
  14.5 0.5 copy-start.17
  56.4 5.6 %copy-start.13 = (f32[1024]{0:T(1024)}, f32[1024]{0:T(1024)S(1)}, u32[]{:S(2)}) copy-start(f32[1024]{0:T(1024)S(1)} %reshape.377) | copy-start | bytes 12292
  63.6 0.7 copy-start.11
  209.8 4.5 %copy-start.4 = (f32[5,128,384]{2,1,0:T(8,128)S(1)}, f32[5,128,384]{2,1,0:T(8,128)}, u32[]{:S(2)}) copy-start(f32[5,128,384]{2,1,0:T(8,128)} %get-tuple-element.47) | copy-start | bytes 2949124
  336.2 2.3 copy-start.12
  336.2 3.3 copy-start.6
  341.5 3.5 copy-start.3
  345.0 1.0 copy-start.2
  345.0 0.9 copy-start.16
  345.0 1.3 copy-start.15
  345.0 1.4 copy-start.18
  345.0 1.4 copy-start
  345.0 1.4 copy-start.5
  345.0 1.4 copy-start.14
  345.8 2.5 copy-start.8
  346.6 2.7 copy-start.7

commit v5 on v3

--- a/solution.py
+++ b/solution.py
@@ -308,7 +308,7 @@
 
 
 def add_up(dst, sources, rows):
-    block = 32 if rows % 32 == 0 else 16
+    block = max(b for b in range(16, 81, 16) if rows % b == 0)
 
     def body(i, carry):
         span = pl.ds(pl.multiple_of(i * block, block), block)
@@ -721,6 +721,45 @@
     lax.fori_loop(needed, blocks // PIECES_PER_BLOCK, clear, 0)
 
 
+def one_hot(rows, columns, wide, pad):
+    row = lax.broadcasted_iota(jnp.int32, (rows, columns), 0)
+    column = lax.broadcasted_iota(jnp.int32, (rows, columns), 1)
+    place = column // pad * wide + column % pad
+    chosen = (row == place) & (column % pad < wide)
+    return jnp.where(chosen, 1.0, 0.0).astype(jnp.bfloat16)
+
+
+def eye(rows, columns):
+    row = lax.broadcasted_iota(jnp.int32, (rows, columns), 0)
+    column = lax.broadcasted_iota(jnp.int32, (rows, columns), 1)
+    return jnp.where(row == column, 1.0, 0.0).astype(jnp.bfloat16)
+
+
+def pieces_kernel(plans, *refs):
+    ins, outs = refs[: len(plans)], refs[len(plans) :]
+    for (target, start, end, wide, pad), weight in zip(plans, ins):
+        columns, rows = weight.shape
+        lanes = outs[target].shape[1]
+        piece = weight[...]
+        if end != columns:
+            piece = plain(eye(end, columns), piece).astype(jnp.bfloat16)
+        if wide != pad or lanes != rows:
+            piece = plain(piece, one_hot(rows, lanes, wide, pad)).astype(jnp.bfloat16)
+        outs[target][start : start + end, :] = piece
+
+
+def make_pieces(weights, plans, shapes):
+    vmem = pl.BlockSpec(memory_space=pltpu.VMEM)
+    return pl.pallas_call(
+        functools.partial(pieces_kernel, plans),
+        out_shape=[jax.ShapeDtypeStruct(shape, jnp.bfloat16) for shape in shapes],
+        in_specs=[vmem] * len(weights),
+        out_specs=[vmem] * len(shapes),
+        compiler_params=pltpu.CompilerParams(vmem_limit_bytes=VMEM_LIMIT),
+        name="make_pieces",
+    )(*weights)
+
+
 def wait_all(copies):
     for copy in copies:
         copy.wait()
@@ -932,11 +971,6 @@
     wide_part = part_width // wide_o * pad_o
     gain_size = gain_attn.shape[0]
 
-    def spread(weight, wide, pad):
-        pieces = weight.reshape(-1, wide, weight.shape[1])
-        pieces = jnp.pad(pieces, ((0, 0), (0, pad - wide), (0, 0)))
-        return pieces.reshape(-1, weight.shape[1]).T
-
     def gathered_spread(total, wide, pad):
         pieces = total.T.reshape(-1, pad, total.shape[0])
         return pieces[:, :wide].reshape(-1, total.shape[0])
@@ -949,22 +983,38 @@
         pieces = values.reshape(row_count, cycle_size, wide_o)
         return jnp.pad(pieces, ((0, 0), (0, 0), (0, pad_o - wide_o))).reshape(row_count, -1)
 
-    def model(weight):
-        return spread(weight, wide_o, pad_o)
-
-    gain_row = jnp.pad(
-        jnp.concatenate([jnp.pad(g, (0, pad_o - gain_size)) for g in (gain_attn, gain_mlp)]),
-        (0, wide_part - 2 * pad_o),
-    )[None, :]
-    first_piece = jnp.concatenate(
+    gain_row = jnp.concatenate([gain_attn, gain_mlp])
+    gain_row = jnp.pad(gain_row, (0, part_width - 2 * gain_size))[None, :]
+    hidden_part = w_down.shape[0] // wide_g * pad_g
+    first_rows = pad_q + pad_k + pad_v
+    first_piece, out_piece, gate_piece, up_piece, down_piece = make_pieces(
         [
-            pad_rows(model(w_query), pad_q),
-            pad_rows(jnp.concatenate([model(w_key), gain_row], axis=0), pad_k),
-            pad_rows(model(w_value), pad_v),
+            w_query.T,
+            jnp.concatenate([w_key.T, gain_row], axis=0),
+            w_value.T,
+            w_out.T,
+            w_gate.T,
+            w_up.T,
+            w_down.T,
         ],
-        axis=0,
-    )
-    first_chunks = cut(0, first_piece.shape[0], 4, (YX, XY))
+        (
+            (0, 0, pad_q, wide_o, pad_o),
+            (0, pad_q, pad_k, wide_o, pad_o),
+            (0, pad_q + pad_k, pad_v, wide_o, pad_o),
+            (1, 0, pad_o, part_width, wide_part),
+            (2, 0, pad_g, wide_o, pad_o),
+            (3, 0, pad_g, wide_o, pad_o),
+            (4, 0, pad_o, wide_g, pad_g),
+        ),
+        [
+            (first_rows, wide_part),
+            (pad_o, wide_part),
+            (pad_g, wide_part),
+            (pad_g, wide_part),
+            (pad_o, hidden_part),
+        ],
+    )
+    first_chunks = cut(0, first_rows, 4, (YX, XY))
     (first,) = gather([first_piece], first_chunks, True, 0, "gather_first")
     gain_rows = first[:cycle_size, pad_q + wide_k, : 2 * pad_o]
     gain_first = gain_rows[:, :pad_o].reshape(1, -1).astype(jnp.float32)
@@ -998,7 +1048,6 @@
 
     query_grouped = jnp.pad(by_group(query_rot), ((0, 0), (0, 0), (0, head_size)))
     width = repeat_count * row_count
-    out_piece = jnp.pad(w_out.T, ((0, pad_o - wide_o), (0, wide_part - part_width)))
     rest_chunks = (
         cut(0, pad_o, 2, (XY, YX))
         + cut(1, pad_g, 1, (XY,))
@@ -1006,12 +1055,7 @@
         + cut(3, pad_o, 2, (XY, YX))
     )
     out_w, gate_w, up_w, down_w, attended_turned, logsum = gather(
-        [
-            out_piece,
-            pad_rows(model(w_gate), pad_g),
-            pad_rows(model(w_up), pad_g),
-            pad_rows(spread(w_down, wide_g, pad_g), pad_o),
-        ],
+        [out_piece, gate_piece, up_piece, down_piece],
         rest_chunks,
         True,
         4,

time: 377 us -> 372 us (0.987)
  local copies, waits for them, and re-layouts: 45.2 us -> 37.4 us
    reshape x10 -> x0, local copies, waits for them, and re-layouts: 5.46 us -> none  [the longest x5 3.34 us: spread(): pieces = weight.reshape(-1, wide, weight.shape[1])]
where the time goes in v5:
time: 372 us; the launch traced here: 371 us
  Pallas kernels  316 us (85%)
  local copies, waits for them, and re-layouts  37.4 us (10%)
  other arithmetic  12.4 us (3%)
  matrix products  4.12 us (1%)
    pallas_call x3, Pallas kernels, scatter(): pl.pallas_call(functools.partial(scatter_kernel, depth, use_x, chunks, wo...  144 us
    pallas_call x3, Pallas kernels, gather(): pl.pallas_call(functools.partial(gather_kernel, depth, use_x, chunks, wor...  134 us
    pallas_call x1, Pallas kernels, mlp(): pl.pallas_call(functools.partial(mlp_kernel, real_width), out_shape=[jax....  29.4 us

profile of v5, /device:TPU:0, one launch (start us, length us, event | category | flops | bytes accessed | tf_op | source)
XLA Modules:
  0.0 371.0 jit_solution(11761154160726159932)
XLA Ops:
  0.7 0.8 fusion.20
  1.4 1.4 pad_maximum_fusion.4.refs_1_
  2.8 0.7 fusion.17
  3.5 1.0 reshape_reshape.42
  4.7 0.5 add_rsqrt_fusion
  5.2 1.0 reshape_reshape.45
  6.2 0.9 copy.66.grad_ref
  7.1 1.0 copy.56.resid_ref
  8.2 1.0 copy.80
  9.2 2.9 make_pieces.1
  12.1 29.5 %gather_first.1 = bf16[32,128,512]{2,1,0:T(8,128)(2,1)} custom-call(bf16[128,512]{1,0:T(8,128)(2,1)} %get-tuple-element.52.refs_0_), custom_call_target="tpu_custom_call" | custom-call | tf_op jit(solution)/shard_map/gather_first/pallas_call | solution.py:288
  41.6 0.8 slice.157
  42.5 0.7 reshape.402.gain_ref
  43.3 1.9 fusion.13.values
  45.2 1.2 multiply_convert_fusion.1
  46.3 2.5 fusion.25
  48.8 0.8 fusion.15
  49.7 0.8 convolution_add_fusion
  50.5 0.3 copy.83
  51.3 0.8 copy.59
  52.4 0.3 copy.61
  53.0 0.9 pad.39.refs_5_
  53.9 22.2 %gather_pairs.1 = bf16[16,640,128]{2,1,0:T(8,128)(2,1)} custom-call(bf16[640,128]{1,0:T(8,128)(2,1)} %bitcast.193), custom_call_target="tpu_custom_call" | custom-call | tf_op jit(solution)/shard_map/gather_pairs/pallas_call | solution.py:288
  76.1 82.8 %gather_rest_attend.1 = (bf16[32,64,512]{2,1,0:T(8,128)(2,1)}, bf16[32,160,512]{2,1,0:T(8,128)(2,1)}, bf16[32,160,512]{2,1,0:T(8,128)(2,1)}, bf16[32,64,1280]{2,...) custom-call(bf16[64,512]{1,0:T(8,128)(2,1)} %get-tuple-element.48.refs_0_, ...), custom_call_target="tpu_custom_call" | custom-call | tf_op jit(solution)/shard_map/gather_rest_attend/pallas_call | solution.py:288
  158.9 1.1 fusion.11
  160.0 0.9 copy.81.attended_ref
  160.9 29.4 %mlp.1 = (bf16[128,1024]{1,0:T(8,128)(2,1)}, f32[128,1024]{1,0:T(8,128)}, bf16[128,1024]{1,0:T(8,128)(2,1)}, f32[1,1024]{1,0:T(1,128)}, bf16[2,1024,512]{2,1,0:T...) custom-call(bf16[128,1024]{1,0:T(8,128)(2,1)} %copy.81.attended_ref, ...), custom_call_target="tpu_custom_call" | custom-call | tf_op jit(solution)/shard_map/mlp/pallas_call | solution.py:920
  190.3 1.1 copy.67
  191.4 0.7 reshape_reshape.46
  192.1 0.7 convert_reduce_fusion
  192.8 0.7 concatenate.69
  193.5 1.1 copy.82
  194.7 1.1 fusion.12
  195.8 0.6 reshape.383.refs_8_
  196.4 0.3 copy.69
  196.7 1.0 pad.42.refs_6_
  197.6 92.6 %scatter_rest_retrace.1 = (f32[64,512]{1,0:T(8,128)}, f32[160,512]{1,0:T(8,128)}, f32[160,512]{1,0:T(8,128)}, f32[64,1280]{1,0:T(8,128)}, f32[5,384,128]{2,1,0:T(8,128)}, /*index=5*/bf16[16,5,128,128]{3,2,1,0:T(8,128)(2,1)}) custom-call(bf16[16,2,64,512]{3,2,1,0:T(8,128)(2,1)} %bitcast.175, bf16[16,2,160,512]{3,2,1,0:T(8,128)(2,1)} %bitcast.162, ...), custom_call_target="tpu_custom_call" | custom-call | tf_op jit(solution)/shard_map/scatter_rest_retrace/pallas_call | solution.py:542
  290.3 1.5 copy.70
  291.9 0.7 pad_maximum_fusion.2
  292.6 23.1 %scatter_pairs.1 = f32[640,128]{1,0:T(8,128)} custom-call(bf16[8,2,640,128]{3,2,1,0:T(8,128)(2,1)} %bitcast.170), custom_call_target="tpu_custom_call" | custom-call | tf_op jit(solution)/shard_map/scatter_pairs/pallas_call | solution.py:542
  315.8 1.2 copy.72
  316.9 1.0 convert_element_type.110
  318.1 1.6 slice_bitcast_fusion.2
  319.6 0.3 copy.71
  320.0 0.7 slice_bitcast_fusion.1
  320.7 0.3 copy.74
  321.0 0.3 copy.73
  321.3 0.6 fusion.5
  321.9 1.4 copy_bitcast_fusion.grads
  323.4 2.1 convolution_bitcast_fusion
  325.5 0.4 convolution_bitcast_fusion.1
  326.4 0.4 multiply_reduce_fusion
  327.2 0.7 reshape_reshape.54
  328.2 0.9 reshape.397
  329.3 0.9 reshape.399
  330.2 4.8 %weight_terms.1 = bf16[2,2048,512]{2,1,0:T(8,128)(2,1)} custom-call(bf16[128,2048]{1,0:T(8,128)(2,1)} %copy_bitcast_fusion.grads, bf16[2,128,512]{2,1,0:T(8,128)(2,1)} %fusion.13.values), custom_call_target="tpu_custom_call" | custom-call | flops 536870912 | bytes 4194304 | tf_op jit(solution)/shard_map/weight_terms/pallas_call | solution.py:621
  335.0 1.9 scatter.4
  336.9 28.5 %scatter_first.1 = f32[128,512]{1,0:T(8,128)} custom-call(bf16[16,2,128,512]{3,2,1,0:T(8,128)(2,1)} %bitcast.156), custom_call_target="tpu_custom_call" | custom-call | tf_op jit(solution)/shard_map/scatter_first/pallas_call | solution.py:542
  365.4 1.3 slice_bitcast_fusion.6
  366.8 0.8 slice_bitcast_fusion.4
  367.6 0.9 slice_bitcast_fusion.3
  368.6 0.7 reshape.395
  369.4 0.7 reshape.393
  370.2 0.8 reshape.391
  (71 shorter events, 3.1 us)
Async XLA Ops:
  4.5 2.6 copy-start.2
  4.7 0.5 copy-start.13
  43.2 5.6 %copy-start.9 = (f32[1024]{0:T(1024)}, f32[1024]{0:T(1024)S(1)}, u32[]{:S(2)}) copy-start(f32[1024]{0:T(1024)S(1)} %reshape.401) | copy-start | bytes 12292
  50.5 0.7 copy-start.8
  315.7 4.2 %copy-start.5 = (f32[64,1280]{1,0:T(8,128)S(1)}, f32[64,1280]{1,0:T(8,128)}, u32[]{:S(2)}) copy-start(f32[64,1280]{1,0:T(8,128)} %get-tuple-element.72) | copy-start | bytes 983044
  321.9 3.5 copy-start
  325.4 1.0 copy-start.3
  325.4 0.9 copy-start.12
  325.5 1.3 copy-start.11
  325.5 1.4 copy-start.14
  325.5 1.4 copy-start.1
  325.5 1.4 copy-start.4
  325.5 1.4 copy-start.10
  326.0 2.0 copy-start.7
  326.8 2.3 copy-start.6
